TPU v7x, 32 devices: a whole 2x2x4 slice. The times are simulated.
32 devices in a mesh: groups: 2 (over x), seq: 16 (over z, y, core).
Axes of the slice: x: 2, y: 2, z: 4, core: 2. Of those that a mesh axis runs over, the one named last changes fastest.
Arguments:
- self_query: bfloat16 [4096, 5120], P(('groups', 'seq')), parts along dimension 0, may hold values from -384 to 384
- self_key: bfloat16 [4096, 5120], P(('groups', 'seq')), parts along dimension 0, may hold values from -20 to 20
- self_value: bfloat16 [4096, 5120], P(('groups', 'seq')), parts along dimension 0, may hold values from -6 to 6
- cross_query: bfloat16 [4096, 5120], P(('groups', 'seq')), parts along dimension 0, may hold values from -384 to 384
- context: bfloat16 [512, 4096], P('groups'), parts along dimension 0, may hold values from -6 to 6
- key_weight: bfloat16 [4096, 5120], P(None, 'seq'), may hold values from -0.09375 to 0.09375
- value_weight: bfloat16 [4096, 5120], P(None, 'seq'), may hold values from -0.09375 to 0.09375
- band_width: int32 [40], replicated, may hold values from 0 to 15
Outputs:
- self_out: bfloat16 [4096, 5120], P(('groups', 'seq')), parts along dimension 0
- cross_out: bfloat16 [4096, 5120], P(('groups', 'seq')), parts along dimension 0
There are 2 independent parts, one for each index of `groups`. A program takes and returns all parts, laid end to end along the dimension named above; an argument that names none is the same for every part. Nothing has to cross between parts.
All inputs are finite; a program needn't handle non-finite values.
Results may differ from a plain program's by a relative error of at most 0.006.
The roundings to bfloat16 on the way count: a program that leaves them out, or rounds other values in their place, can miss the bound.
Values may be sent and summed in bfloat16 or wider, within the bound.
No kernel may reach another device: no remote copies, remote signals or barrier semaphores. Data moves between devices by JAX's collectives and lax.ppermute only.
A program may use at most 128 MiB of HBM per device.

v0:
```python
import functools
import math

import jax
import jax.numpy as jnp
from jax import lax
from jax.experimental import pallas as pl
from jax.experimental.pallas import tpu as pltpu
from jax.sharding import PartitionSpec as P


SB = 16
SEATS = 4
REACH = 3
LOG2_E = 1.4426950408889634


def pack_kernel(*refs, head_dim):
    query_ref, key_ref, value_ref = sources = refs[-5:-2] if len(refs) == 7 else refs[-4:-1]
    orders, outs = (refs[:2], refs[-2:]) if len(refs) == 7 else (refs[:1], refs[-1:])
    del query_ref, key_ref, value_ref
    for order_ref, out_ref in zip(orders, outs):
        per_run = out_ref.shape[2]

        def fill(slot, carry, order_ref=order_ref, out_ref=out_ref, per_run=per_run):
            head = jnp.maximum(order_ref[slot], 0)
            columns = pl.ds(pl.multiple_of(head * head_dim, head_dim), head_dim)
            for index, source in enumerate(sources):
                out_ref[slot // per_run, index, slot % per_run] = source[:, columns]
            return carry

        lax.fori_loop(0, out_ref.shape[0] * per_run, fill, 0)


def unpack_kernel(*refs, head_dim):
    count = len(refs) // 2
    out_ref = refs[-1]
    for order_ref, returned_ref in zip(refs[:count], refs[count:-1]):
        per_run = returned_ref.shape[1]

        def fill(slot, carry, order_ref=order_ref, returned_ref=returned_ref, per_run=per_run):
            head = order_ref[slot]

            @pl.when(head >= 0)
            def _():
                columns = pl.ds(pl.multiple_of(head * head_dim, head_dim), head_dim)
                out_ref[:, columns] = returned_ref[slot // per_run, slot % per_run]

            return carry

        lax.fori_loop(0, returned_ref.shape[0] * per_run, fill, 0)


def attend_tile(tile, width, band, data_ref, out_ref, score_ref, scale):
    stripe_len, _, _, rows, head_dim = data_ref.shape
    start = jnp.clip(2 * tile - band, 0, stripe_len - width)
    query = data_ref[pl.ds(2 * tile, 2), 0, 0].reshape(2 * rows, head_dim)
    peak = None
    for chunk in range(0, width, 2):
        keys = data_ref[pl.ds(start + chunk, 2), 1, 0].reshape(2 * rows, head_dim)
        scores = lax.dot_general(
            query, keys, (((1,), (1,)), ((), ())), preferred_element_type=jnp.float32
        )
        for part in range(2):
            key_block = start + chunk + part
            halves = []
            for half in range(2):
                outside = jnp.abs(2 * tile + half - key_block) > band
                bias = jnp.where(outside, -jnp.inf, 0.0).astype(jnp.float32)
                halves.append(
                    scores[half * rows : (half + 1) * rows, part * rows : (part + 1) * rows] + bias
                )
            masked = jnp.concatenate(halves, axis=0)
            score_ref[:, (chunk + part) * rows : (chunk + part + 1) * rows] = masked
            peak = masked if peak is None else jnp.maximum(peak, masked)
    peak = jnp.max(peak, axis=1, keepdims=True)
    total = None
    running = None
    for chunk in range(0, width, 2):
        weights = jnp.exp2(
            (score_ref[:, chunk * rows : (chunk + 2) * rows] - peak) * (scale * LOG2_E)
        )
        values = data_ref[pl.ds(start + chunk, 2), 2, 0].reshape(2 * rows, head_dim)
        partial = weights[:, :rows] + weights[:, rows:]
        product = jnp.dot(
            weights.astype(jnp.bfloat16), values, preferred_element_type=jnp.float32
        )
        total = partial if total is None else total + partial
        running = product if running is None else running + product
    total = jnp.sum(total, axis=1, keepdims=True)
    out_ref[pl.ds(2 * tile, 2), 0] = (
        (running / total).astype(jnp.bfloat16).reshape(2, rows, head_dim)
    )


def attend_kernel(band_ref, data_ref, out_ref, score_ref, *, scale):
    stripe_len = data_ref.shape[0]
    band = band_ref[pl.program_id(0)]

    def step(tile, carry):
        low = jnp.maximum(2 * tile - band, 0)
        high = jnp.minimum(2 * tile + 1 + band, stripe_len - 1)
        quarter = stripe_len // 4
        level = (high - low) // quarter
        for index in range(4):

            @pl.when(level == index)
            def _():
                attend_tile(
                    tile, (index + 1) * quarter, band, data_ref, out_ref, score_ref, scale
                )

        return carry

    @pl.when(band >= 0)
    def _():
        lax.fori_loop(0, stripe_len // 2, step, 0)


def cross_kernel(query_ref, key_ref, value_ref, out_ref, *, head_dim, scale, group):
    def step(index, carry):
        for offset in range(group):
            head = index * group + offset
            columns = pl.ds(pl.multiple_of(head * head_dim, head_dim), head_dim)
            scores = lax.dot_general(
                query_ref[:, columns],
                key_ref[:, columns],
                (((1,), (1,)), ((), ())),
                preferred_element_type=jnp.float32,
            )
            peak = jnp.max(scores, axis=1, keepdims=True)
            weights = jnp.exp2((scores - peak) * (scale * LOG2_E))
            total = jnp.sum(weights, axis=1, keepdims=True)
            running = jnp.dot(
                weights.astype(jnp.bfloat16),
                value_ref[:, columns],
                preferred_element_type=jnp.float32,
            )
            out_ref[:, columns] = (running / total).astype(jnp.bfloat16)
        return carry

    lax.fori_loop(0, query_ref.shape[1] // head_dim // group, step, 0)


def narrow_kernel(band_ref, place_ref, own_ref, low_ref, high_ref, out_ref, *, scale, reach):
    seats, _, per_run, _, _ = own_ref.shape
    first = place_ref[0]

    def block_of(part, place, run):
        if place < reach:
            return low_ref[place, part, run]
        if place < reach + seats:
            return own_ref[place - reach, part + 1, run]
        return high_ref[place - reach - seats, part, run]

    def step(run, carry):
        band = band_ref[run]
        for seat in range(seats):
            query = own_ref[seat, 0, run]
            tiles = []
            for place in range(seat, seat + 2 * reach + 1):
                scores = lax.dot_general(
                    query,
                    block_of(0, place, run),
                    (((1,), (1,)), ((), ())),
                    preferred_element_type=jnp.float32,
                )
                if place != seat + reach:
                    block = first + place - reach
                    outside = (abs(place - seat - reach) > band) | (block < 0) | (block >= SB)
                    scores = scores + jnp.where(outside, -jnp.inf, 0.0).astype(jnp.float32)
                tiles.append(scores)
            peak = jnp.max(functools.reduce(jnp.maximum, tiles), axis=1, keepdims=True)
            total, running = 0.0, 0.0
            for place, scores in enumerate(tiles, seat):
                weights = jnp.exp2((scores - peak) * (scale * LOG2_E))
                total = total + weights
                running = running + jnp.dot(
                    weights.astype(jnp.bfloat16),
                    block_of(1, place, run),
                    preferred_element_type=jnp.float32,
                )
            total = jnp.sum(total, axis=1, keepdims=True)
            out_ref[seat, run] = (running / total).astype(jnp.bfloat16)
        return carry

    lax.fori_loop(0, per_run, step, 0)


def project_kernel(context_ref, key_ref, value_ref, out_ref, total_ref):
    weights = jnp.concatenate([key_ref[...], value_ref[...]], axis=0)
    product = lax.dot_general(
        context_ref[...], weights, (((1,), (1,)), ((), ())), preferred_element_type=jnp.float32
    )

    @pl.when(pl.program_id(0) == 0)
    def _():
        total_ref[...] = product

    @pl.when(pl.program_id(0) > 0)
    def _():
        total_ref[...] += product

    @pl.when(pl.program_id(0) == pl.num_programs(0) - 1)
    def _():
        out_ref[0] = total_ref[...].astype(jnp.bfloat16)


def project(context, key_weight, value_weight, steps=4):
    text_len, depth = context.shape
    columns = key_weight.shape[1]
    part = depth // steps
    weight_spec = pl.BlockSpec((columns, part), lambda step: (0, step))
    return pl.pallas_call(
        project_kernel,
        out_shape=jax.ShapeDtypeStruct((1, text_len, 2 * columns), jnp.bfloat16),
        grid=(steps,),
        in_specs=[
            pl.BlockSpec((text_len, part), lambda step: (0, step)),
            weight_spec,
            weight_spec,
        ],
        out_specs=pl.BlockSpec((1, text_len, 2 * columns), lambda step: (0, 0, 0)),
        scratch_shapes=[pltpu.VMEM((text_len, 2 * columns), jnp.float32)],
        name="project",
    )(context, key_weight.T, value_weight.T)


def cross_pairs_kernel(
    place_ref, query_ref, mine_ref, other_ref, out_ref, key_ref, value_ref, *, head_dim, scale
):
    entries, _, pair_width = mine_ref.shape
    columns = pair_width // 2
    bits = entries.bit_length() - 1

    def attend(even_ref, odd_ref):
        def step(entry, carry):
            pair = place_ref[0]
            for bit in range(bits):
                pair = pair ^ (((entry >> bit) & 1) << (bits - 1 - bit))
            key_ref[:, :columns] = even_ref[entry, :, :columns]
            key_ref[:, columns:] = odd_ref[entry, :, :columns]
            value_ref[:, :columns] = even_ref[entry, :, columns:]
            value_ref[:, columns:] = odd_ref[entry, :, columns:]
            for offset in range(pair_width // head_dim):
                source = pl.ds(offset * head_dim, head_dim)
                target = pl.ds(
                    pl.multiple_of(pair * pair_width + offset * head_dim, head_dim), head_dim
                )
                scores = lax.dot_general(
                    query_ref[:, target],
                    key_ref[:, source],
                    (((1,), (1,)), ((), ())),
                    preferred_element_type=jnp.float32,
                )
                peak = jnp.max(scores, axis=1, keepdims=True)
                weights = jnp.exp2((scores - peak) * (scale * LOG2_E))
                total = jnp.sum(weights, axis=1, keepdims=True)
                running = jnp.dot(
                    weights.astype(jnp.bfloat16),
                    value_ref[:, source],
                    preferred_element_type=jnp.float32,
                )
                out_ref[:, target] = (running / total).astype(jnp.bfloat16)
            return carry

        lax.fori_loop(0, entries, step, 0)

    @pl.when(place_ref[1] == 0)
    def _():
        attend(mine_ref, other_ref)

    @pl.when(place_ref[1] == 1)
    def _():
        attend(other_ref, mine_ref)


def swap(values, distance):
    devices = lax.axis_size("seq")
    return lax.ppermute(values, "seq", [(source, source ^ distance) for source in range(devices)])


def doubles(key_weight, head_dim):
    devices = lax.axis_size("seq")
    return (2 * key_weight.shape[1]) % head_dim == 0 and devices & (devices - 1) == 0


def cross_attention(cross_query, context, key_weight, value_weight, head_dim, scale, text):
    devices = lax.axis_size("seq")
    device = lax.axis_index("seq")
    tok_rows, width = cross_query.shape
    out_shape = jax.ShapeDtypeStruct((tok_rows, width), jnp.bfloat16)
    vmem = pl.BlockSpec(memory_space=pltpu.VMEM)
    smem = pl.BlockSpec(memory_space=pltpu.SMEM)
    if text is None:
        text_key = jnp.dot(context, key_weight, preferred_element_type=jnp.float32)
        text_value = jnp.dot(context, value_weight, preferred_element_type=jnp.float32)
        return pl.pallas_call(
            functools.partial(cross_kernel, head_dim=head_dim, scale=scale, group=4),
            out_shape=out_shape,
            in_specs=[vmem, vmem, vmem],
            out_specs=vmem,
            name="cross",
        )(
            cross_query,
            lax.all_gather(text_key.astype(jnp.bfloat16), "seq", axis=1, tiled=True),
            lax.all_gather(text_value.astype(jnp.bfloat16), "seq", axis=1, tiled=True),
        )
    distance = devices // 4
    while distance > 1:
        came = swap(text, distance)
        text = jnp.concatenate([text, came], axis=0)
        distance //= 2
    other = swap(text, 1)
    place = jnp.stack([device // 2, device % 2]).astype(jnp.int32)
    pair = pltpu.VMEM(text.shape[1:], jnp.bfloat16)
    return pl.pallas_call(
        functools.partial(cross_pairs_kernel, head_dim=head_dim, scale=scale),
        out_shape=out_shape,
        in_specs=[smem, vmem, vmem, vmem],
        out_specs=vmem,
        scratch_shapes=[pair, pair],
        name="cross",
    )(place, cross_query, text, other)


def deal(rank, band_width, first, seats, per_run):
    slot_ids = jnp.arange(seats * per_run, dtype=jnp.int32)
    run, seat = slot_ids % per_run, slot_ids // per_run
    wanted = first + run * seats + jnp.where(run % 2 == 0, seat, seats - 1 - seat)
    hits = wanted[:, None] == rank[None, :]
    head_ids = jnp.arange(rank.shape[0], dtype=jnp.int32)
    order = jnp.sum(jnp.where(hits, head_ids[None, :] + 1, 0), axis=1) - 1
    bands = jnp.sum(jnp.where(hits, band_width[None, :] + 1, 0), axis=1) - 1
    return order, bands


def index_groups(devices, size):
    return [list(range(first, first + size)) for first in range(0, devices, size)]


def attention(rank, per_run, narrow_run, arrays):
    (self_query, self_key, self_value, cross_query, context, key_weight, value_weight, band_width) = (
        arrays
    )
    devices = lax.axis_size("seq")
    device = lax.axis_index("seq")
    tok_rows, width = self_query.shape
    head_count = band_width.shape[0]
    head_dim = width // head_count
    scale = 1.0 / math.sqrt(head_dim)
    vmem = pl.BlockSpec(memory_space=pltpu.VMEM)
    smem = pl.BlockSpec(memory_space=pltpu.SMEM)

    text = None
    if doubles(key_weight, head_dim):
        text = project(context, key_weight, value_weight)
        came = swap(text, devices // 2)
    deals = [deal(rank, band_width, 0, SB, per_run)]
    shapes = [(SB, 3, per_run, tok_rows, head_dim)]
    if narrow_run:
        deals.append(deal(rank, band_width, SB * per_run, SEATS, narrow_run))
        shapes.append((SEATS, 3, narrow_run, tok_rows, head_dim))
    packed = pl.pallas_call(
        functools.partial(pack_kernel, head_dim=head_dim),
        out_shape=[jax.ShapeDtypeStruct(shape, jnp.bfloat16) for shape in shapes],
        in_specs=[smem] * len(deals) + [vmem] * 3,
        out_specs=[vmem] * len(deals),
        name="pack",
    )(*[order for order, _ in deals], self_query, self_key, self_value)

    def exchange(values, size):
        return lax.all_to_all(
            values,
            "seq",
            split_axis=0,
            concat_axis=0,
            tiled=True,
            axis_index_groups=index_groups(devices, size),
        )

    outgoing = packed[0]
    if narrow_run:
        own = exchange(packed[1], SEATS)
        upward = [
            (source, source + SEATS)
            for source in range(devices - SEATS)
            if source // SB == (source + SEATS) // SB
        ]
        low = lax.ppermute(own[SEATS - REACH :, 1:], "seq", upward)
        high = lax.ppermute(own[:REACH, 1:], "seq", [(high, low) for low, high in upward])
        if text is not None:
            outgoing, came, own = lax.optimization_barrier((outgoing, came, own))
        else:
            outgoing, own = lax.optimization_barrier((outgoing, own))
    elif text is not None:
        outgoing, came = lax.optimization_barrier((outgoing, came))
    arrived = exchange(outgoing, SB)
    if text is not None:
        text = jnp.concatenate([text, came], axis=0)
    cross_out = cross_attention(
        cross_query, context, key_weight, value_weight, head_dim, scale, text
    )
    own_bands = lax.dynamic_slice_in_dim(deals[0][1], (device % SB) * per_run, per_run)
    results = pl.pallas_call(
        functools.partial(attend_kernel, scale=scale),
        out_shape=jax.ShapeDtypeStruct((SB, per_run, tok_rows, head_dim), jnp.bfloat16),
        grid_spec=pltpu.PrefetchScalarGridSpec(
            num_scalar_prefetch=1,
            grid=(per_run,),
            in_specs=[
                pl.BlockSpec(
                    (SB, 3, 1, tok_rows, head_dim), lambda run, bands: (0, 0, run, 0, 0)
                )
            ],
            out_specs=pl.BlockSpec(
                (SB, 1, tok_rows, head_dim), lambda run, bands: (0, run, 0, 0)
            ),
            scratch_shapes=[pltpu.VMEM((2 * tok_rows, SB * tok_rows), jnp.float32)],
        ),
        name="attend",
    )(own_bands, arrived)
    returned = [exchange(results, SB)]
    if narrow_run:
        narrow_bands = lax.dynamic_slice_in_dim(
            deals[1][1], (device % SEATS) * narrow_run, narrow_run
        )
        first = jnp.reshape(device % SB // SEATS * SEATS, (1,)).astype(jnp.int32)
        narrow = pl.pallas_call(
            functools.partial(narrow_kernel, scale=scale, reach=REACH),
            out_shape=jax.ShapeDtypeStruct((SEATS, narrow_run, tok_rows, head_dim), jnp.bfloat16),
            in_specs=[smem, smem, vmem, vmem, vmem],
            out_specs=vmem,
            name="narrow",
        )(narrow_bands, first, own, low, high)
        returned.append(exchange(narrow, SEATS))
    self_out = pl.pallas_call(
        functools.partial(unpack_kernel, head_dim=head_dim),
        out_shape=jax.ShapeDtypeStruct((tok_rows, width), jnp.bfloat16),
        in_specs=[smem] * len(deals) + [vmem] * len(deals),
        out_specs=vmem,
        name="unpack",
    )(*[order for order, _ in deals], *returned)
    return (self_out, cross_out)


def layer(*arrays):
    band_width = arrays[-1]
    head_count = band_width.shape[0]
    head_ids = jnp.arange(head_count, dtype=jnp.int32)
    ahead = (band_width[None, :] > band_width[:, None]) | (
        (band_width[None, :] == band_width[:, None]) & (head_ids[None, :] < head_ids[:, None])
    )
    rank = jnp.sum(ahead.astype(jnp.int32), axis=1)
    whole_run = head_count // SB
    narrow_count = head_count - whole_run * SB
    narrow_run = (narrow_count + SEATS - 1) // SEATS
    if not narrow_count or not whole_run:
        return attention(rank, (head_count + SB - 1) // SB, 0, arrays)
    close = jnp.sum((band_width <= REACH).astype(jnp.int32)) >= narrow_count
    return lax.cond(
        close,
        functools.partial(attention, rank, whole_run, narrow_run),
        functools.partial(attention, rank, whole_run + 1, 0),
        arrays,
    )


def solution(mesh):
    in_specs = (
        P(("groups", "seq"), None),
        P(("groups", "seq"), None),
        P(("groups", "seq"), None),
        P(("groups", "seq"), None),
        P("groups", None),
        P(None, "seq"),
        P(None, "seq"),
        P(),
    )
    out_specs = (P(("groups", "seq"), None), P(("groups", "seq"), None))
    return jax.shard_map(layer, mesh=mesh, in_specs=in_specs, out_specs=out_specs, check_vma=False)
```

profile of v0, /device:TPU:13, one launch (start us, length us, event | category | flops | bytes accessed | tf_op | source)
XLA Modules:
  0.0 229.4 jit_solution(5078978011757134292)
XLA Ops:
  0.6 1.3 fusion.15
  3.4 226.0 %conditional.1 = (bf16[128,5120]{1,0:T(8,128)(2,1)}, bf16[128,5120]{1,0:T(8,128)(2,1)}) conditional(s32[]{:T(128)} %convert_element_type.10, (s32[40,40]{1,0:T(8,128)S(1)}, s32[40]{0:T(128)}, bf16[128,5120]{1,0:T(8,128)(2,1)}, bf16[128,5120]{1,0:T(8,128)(2,1)}, bf16[128,5120]{1,0:T(8,128)(2,1)}, /*index=5*/bf16[4096,320]{0,1:T(8,128)(2,1)}, ...), branch_computations={%region_2.5_spmd, %region_5.10_spmd} | conditional | flops 5583179 | bytes 92023120 | solution.py:461
  5.7 5.5 %pack.3 = (bf16[16,3,2,128,128]{4,3,2,1,0:T(8,128)(2,1)}, bf16[4,3,2,128,128]{4,3,2,1,0:T(8,128)(2,1)}) custom-call(s32[32]{0:T(128)} %broadcast_add_fusion.7.refs_0_, s32[8]{0:T(128)} %broadcast_add_fusion.4.refs_1_, bf16[128,5120]{1,0:T(8,128)(2,1)} %get-tuple-element.84.refs_2_, bf16[128,5120]{1,0:T(8,128)(2,1)} %get-tuple-element.86.refs_3_, ...), custom_call_target="tpu_custom_call" | custom-call | tf_op jit(solution)/shard_map/cond/branch_1_fun/pack/pallas_call | solution.py:364
  11.2 4.3 %all-to-all-start.2 = ((bf16[4,3,2,128,128]{4,3,2,1,0:T(8,128)(2,1)}), bf16[4,3,2,128,128]{4,3,2,1,0:T(8,128)(2,1)S(1)}, u32[]{:S(2)}, u32[]{:S(2)}) async-start(bf16[4,3,2,128,128]{4,3,2,1,0:T(8,128)(2,1)} %get-tuple-element.56), calls=%async_computation.2 | async-start | bytes 1572864 | tf_op jit(solution)/shard_map/cond/branch_1_fun/all_to_all | solution.py:373
  15.5 5.4 %project.3 = bf16[1,256,640]{2,1,0:T(8,128)(2,1)} custom-call(bf16[256,4096]{1,0:T(8,128)(2,1)} %get-tuple-element.94.context_ref, bf16[320,4096]{1,0:T(8,128)(2,1)S(1)} %bitcast.10, bf16[320,4096]{1,0:T(8,128)(2,1)} %bitcast.12), custom_call_target="tpu_custom_call" | custom-call | tf_op jit(solution)/shard_map/cond/branch_1_fun/project/pallas_call | solution.py:214
  20.9 2.3 %collective-permute-start.4 = (bf16[1,256,640]{2,1,0:T(8,128)(2,1)}, bf16[1,256,640]{2,1,0:T(8,128)(2,1)}, u32[]{:S(2)}, u32[]{:S(2)}) collective-permute-start(bf16[1,256,640]{2,1,0:T(8,128)(2,1)} %project.3), channel_id=1, source_target_pairs={{0,8},{1,9},{2,10},{3,11},{4,12},{5,13},{6,14},{7,15},{8,0},{9,1},... | collective-permute-start | bytes 983048 | tf_op jit(solution)/shard_map/cond/branch_1_fun/ppermute | solution.py:280
  23.2 14.7 %collective-permute-done.4 = bf16[1,256,640]{2,1,0:T(8,128)(2,1)} collective-permute-done((bf16[1,256,640]{2,1,0:T(8,128)(2,1)}, bf16[1,256,640]{2,1,0:T(8,128)(2,1)}, u32[]{:S(2)}, u32[]{:S(2)}) %collective-permute-start.4) | collective-permute-done | bytes 327712 | tf_op jit(solution)/shard_map/cond/branch_1_fun/ppermute | solution.py:280
  38.8 7.1 %all-to-all-start.3 = ((bf16[16,3,2,128,128]{4,3,2,1,0:T(8,128)(2,1)}), bf16[16,3,2,128,128]{4,3,2,1,0:T(8,128)(2,1)S(1)}, u32[]{:S(2)}, u32[]{:S(2)}) async-start(bf16[16,3,2,128,128]{4,3,2,1,0:T(8,128)(2,1)} %get-tuple-element.57), calls=%async_computation.3 | async-start | bytes 6291456 | tf_op jit(solution)/shard_map/cond/branch_1_fun/all_to_all | solution.py:373
  47.3 65.4 %collective-permute-done.7 = bf16[2,256,640]{2,1,0:T(8,128)(2,1)S(1)} collective-permute-done((bf16[2,256,640]{2,1,0:T(8,128)(2,1)S(1)}, bf16[2,256,640]{2,1,0:T(8,128)(2,1)S(1)}, u32[]{:S(2)}, u32[]{:S(2)}) %collective-permute-start.7) | collective-permute-done | bytes 655392 | tf_op jit(solution)/shard_map/cond/branch_1_fun/ppermute | solution.py:280
  112.7 1.1 pad_maximum_fusion.4
  113.9 29.4 %collective-permute-done.8 = bf16[4,256,640]{2,1,0:T(8,128)(2,1)S(1)} collective-permute-done((bf16[4,256,640]{2,1,0:T(8,128)(2,1)S(1)}, bf16[4,256,640]{2,1,0:T(8,128)(2,1)S(1)}, u32[]{:S(2)}, u32[]{:S(2)}) %collective-permute-start.8) | collective-permute-done | bytes 1310752 | tf_op jit(solution)/shard_map/cond/branch_1_fun/ppermute | solution.py:280
  143.3 2.6 %pad_maximum_fusion.3.mine_ref = bf16[8,256,640]{2,1,0:T(8,128)(2,1)} fusion(bf16[4,256,640]{2,1,0:T(8,128)(2,1)S(1)} %collective-permute-done.8, bf16[2,256,640]{2,1,0:T(8,128)(2,1)S(1)} %collective-permute-done.7, bf16[1,256,640]{2,1,0:T(8,128)(2,1)} %collective-permute-done.4, bf16[1,256,640]{2,1,0:T(8,128)(2,1)S(1)} %copy-done.9), kind=kLoop, calls=%fused_computation.23 | loop fusion | flops 3932160 | bytes 5242880 | tf_op jit(solution)/shard_map/cond/branch_1_fun/concatenate | solution.py:312
  145.9 1.8 collective-permute-start.9
  148.8 2.1 collective-permute-start.6
  150.9 3.2 %collective-permute-start.5 = (bf16[3,2,2,128,128]{4,3,2,1,0:T(8,128)(2,1)}, bf16[3,2,2,128,128]{4,3,2,1,0:T(8,128)(2,1)}, u32[]{:S(2)}, u32[]{:S(2)}) collective-permute-start(bf16[3,2,2,128,128]{4,3,2,1,0:T(8,128)(2,1)} %get-tuple-element.104), channel_id=1, source_target_pairs={{0,4},{1,5},{2,6},{3,7},{4,8},{5,9},{6,10},{7,11},{8,12},{9,13},{1... | collective-permute-start | bytes 1179656 | tf_op jit(solution)/shard_map/cond/branch_1_fun/ppermute | solution.py:390
  154.8 6.9 %collective-permute-done.6.high_ref = bf16[3,2,2,128,128]{4,3,2,1,0:T(8,128)(2,1)S(1)} collective-permute-done((bf16[3,2,2,128,128]{4,3,2,1,0:T(8,128)(2,1)}, bf16[3,2,2,128,128]{4,3,2,1,0:T(8,128)(2,1)S(1)}, u32[]{:S(2)}, u32[]{:S(2)}) %collective-permute-start.6) | collective-permute-done | bytes 393248 | tf_op jit(solution)/shard_map/cond/branch_1_fun/ppermute | solution.py:391
  161.6 1.8 collective-permute-done.5.low_ref
  163.5 5.9 %narrow.1 = bf16[4,2,128,128]{3,2,1,0:T(8,128)(2,1)} custom-call(s32[2]{0:T(128)} %dynamic_slice.8.band_ref, s32[1]{0:T(128)} %bitcast.6.place_ref, bf16[4,3,2,128,128]{4,3,2,1,0:T(8,128)(2,1)} %copy-done.3, bf16[3,2,2,128,128]{4,3,2,1,0:T(8,128)(2,1)} %collective-permute-done.5.low_ref, bf16[3,2,2,128,128]{4,3,2,1,0:T(8,128)(2,1)} %copy-done.13), custom_call_target="tpu_custom_call" | custom-call | tf_op jit(solution)/shard_map/cond/branch_1_fun/narrow/pallas_call | solution.py:429
  169.3 4.6 %all-to-all-start.5 = ((bf16[4,2,128,128]{3,2,1,0:T(8,128)(2,1)}), bf16[4,2,128,128]{3,2,1,0:T(8,128)(2,1)S(1)}, u32[]{:S(2)}, u32[]{:S(2)}) async-start(bf16[4,2,128,128]{3,2,1,0:T(8,128)(2,1)} %narrow.1), calls=%async_computation.5 | async-start | bytes 524288 | tf_op jit(solution)/shard_map/cond/branch_1_fun/all_to_all | solution.py:373
  174.5 18.8 %attend.3 = bf16[16,2,128,128]{3,2,1,0:T(8,128)(2,1)} custom-call(s32[2]{0:T(128)} %dynamic_slice.7.band_ref, bf16[16,3,2,128,128]{4,3,2,1,0:T(8,128)(2,1)} %copy-done), custom_call_target="tpu_custom_call" | custom-call | tf_op jit(solution)/shard_map/cond/branch_1_fun/attend/pallas_call | solution.py:405
  193.3 6.9 %all-to-all-start.4 = ((bf16[16,2,128,128]{3,2,1,0:T(8,128)(2,1)}), bf16[16,2,128,128]{3,2,1,0:T(8,128)(2,1)S(1)}, u32[]{:S(2)}, u32[]{:S(2)}) async-start(bf16[16,2,128,128]{3,2,1,0:T(8,128)(2,1)} %attend.3), calls=%async_computation.4 | async-start | bytes 2097152 | tf_op jit(solution)/shard_map/cond/branch_1_fun/all_to_all | solution.py:373
  200.8 10.0 %cross.3 = bf16[128,5120]{1,0:T(8,128)(2,1)} custom-call(s32[2]{0:T(128)} %pad_add_fusion.1.place_ref, bf16[128,5120]{1,0:T(8,128)(2,1)S(1)} %copy-done.7, bf16[8,256,640]{2,1,0:T(8,128)(2,1)} %pad_maximum_fusion.3.mine_ref, bf16[8,256,640]{2,1,0:T(8,128)(2,1)} %collective-permute-done.9.other_ref), custom_call_target="tpu_custom_call" | custom-call | tf_op jit(solution)/shard_map/cond/branch_1_fun/cross/pallas_call | solution.py:317
  210.8 14.2 %all-to-all-done.4.refs_2_ = bf16[16,2,128,128]{3,2,1,0:T(8,128)(2,1)S(1)} async-done(((bf16[16,2,128,128]{3,2,1,0:T(8,128)(2,1)}), bf16[16,2,128,128]{3,2,1,0:T(8,128)(2,1)S(1)}, u32[]{:S(2)}, u32[]{:S(2)}) %all-to-all-start.4) | async-done | bytes 1048608 | tf_op jit(solution)/shard_map/cond/branch_1_fun/all_to_all | solution.py:373
  226.1 3.3 %unpack.3 = bf16[128,5120]{1,0:T(8,128)(2,1)} custom-call(s32[32]{0:T(128)} %broadcast_add_fusion.7.refs_0_, s32[8]{0:T(128)} %broadcast_add_fusion.4.refs_1_, bf16[16,2,128,128]{3,2,1,0:T(8,128)(2,1)} %copy-done.10, bf16[4,2,128,128]{3,2,1,0:T(8,128)(2,1)} %copy-done.12), custom_call_target="tpu_custom_call" | custom-call | tf_op jit(solution)/shard_map/cond/branch_1_fun/unpack/pallas_call | solution.py:437
  (41 shorter events, 9.3 us)
Async XLA Ops:
  5.7 9.8 %copy-start.2 = (bf16[4096,320]{0,1:T(8,128)(2,1)S(1)}, bf16[4096,320]{0,1:T(8,128)(2,1)}, u32[]{:S(2)}) copy-start(bf16[4096,320]{0,1:T(8,128)(2,1)} %get-tuple-element.90) | copy-start | bytes 7864324 | tf_op jit(solution)/shard_map/cond
  11.2 26.7 %all-to-all-start.2 = ((bf16[4,3,2,128,128]{4,3,2,1,0:T(8,128)(2,1)}), bf16[4,3,2,128,128]{4,3,2,1,0:T(8,128)(2,1)S(1)}, u32[]{:S(2)}, u32[]{:S(2)}) async-start(bf16[4,3,2,128,128]{4,3,2,1,0:T(8,128)(2,1)} %get-tuple-element.56), calls=%async_computation.2 | async-start | bytes 1572864 | tf_op jit(solution)/shard_map/cond/branch_1_fun/all_to_all | solution.py:373
  20.9 17.0 %collective-permute-start.4 = (bf16[1,256,640]{2,1,0:T(8,128)(2,1)}, bf16[1,256,640]{2,1,0:T(8,128)(2,1)}, u32[]{:S(2)}, u32[]{:S(2)}) collective-permute-start(bf16[1,256,640]{2,1,0:T(8,128)(2,1)} %project.3), channel_id=1, source_target_pairs={{0,8},{1,9},{2,10},{3,11},{4,12},{5,13},{6,14},{7,15},{8,0},{9,1},... | collective-permute-start | bytes 983048 | tf_op jit(solution)/shard_map/cond/branch_1_fun/ppermute | solution.py:280
  37.9 0.9 copy-start.3
  37.9 8.0 %copy-start.9 = (bf16[1,256,640]{2,1,0:T(8,128)(2,1)S(1)}, bf16[1,256,640]{2,1,0:T(8,128)(2,1)}, u32[]{:S(2)}) copy-start(bf16[1,256,640]{2,1,0:T(8,128)(2,1)} %project.3) | copy-start | bytes 983044 | tf_op jit(solution)/shard_map/cond
  38.8 130.6 %all-to-all-start.3 = ((bf16[16,3,2,128,128]{4,3,2,1,0:T(8,128)(2,1)}), bf16[16,3,2,128,128]{4,3,2,1,0:T(8,128)(2,1)S(1)}, u32[]{:S(2)}, u32[]{:S(2)}) async-start(bf16[16,3,2,128,128]{4,3,2,1,0:T(8,128)(2,1)} %get-tuple-element.57), calls=%async_computation.3 | async-start | bytes 6291456 | tf_op jit(solution)/shard_map/cond/branch_1_fun/all_to_all | solution.py:373
  46.9 65.8 %collective-permute-start.7 = (bf16[2,256,640]{2,1,0:T(8,128)(2,1)S(1)}, bf16[2,256,640]{2,1,0:T(8,128)(2,1)S(1)}, u32[]{:S(2)}, u32[]{:S(2)}) collective-permute-start(bf16[2,256,640]{2,1,0:T(8,128)(2,1)S(1)} %pad_maximum_fusion.5), channel_id=1, source_target_pairs={{0,4},{1,5},{2,6},{3,7},{4,0},{5,1},{6,2},{7,3},{8,12},{9,13},{10,... | collective-permute-start | bytes 1966088 | tf_op jit(solution)/shard_map/cond/branch_1_fun/ppermute | solution.py:280
  113.9 33.9 %copy-start.4 = (bf16[4,3,2,128,128]{4,3,2,1,0:T(8,128)(2,1)S(1)}, bf16[4,3,2,128,128]{4,3,2,1,0:T(8,128)(2,1)}, u32[]{:S(2)}) copy-start(bf16[4,3,2,128,128]{4,3,2,1,0:T(8,128)(2,1)} %copy-done.3) | copy-start | bytes 2359300 | tf_op jit(solution)/shard_map/cond
  113.9 29.4 %collective-permute-start.8 = (bf16[4,256,640]{2,1,0:T(8,128)(2,1)S(1)}, bf16[4,256,640]{2,1,0:T(8,128)(2,1)S(1)}, u32[]{:S(2)}, u32[]{:S(2)}) collective-permute-start(bf16[4,256,640]{2,1,0:T(8,128)(2,1)S(1)} %pad_maximum_fusion.4), channel_id=1, source_target_pairs={{0,2},{1,3},{2,0},{3,1},{4,6},{5,7},{6,4},{7,5},{8,10},{9,11},{10,... | collective-permute-start | bytes 3932168 | tf_op jit(solution)/shard_map/cond/branch_1_fun/ppermute | solution.py:280
  145.9 54.9 %collective-permute-start.9 = (bf16[8,256,640]{2,1,0:T(8,128)(2,1)}, bf16[8,256,640]{2,1,0:T(8,128)(2,1)}, u32[]{:S(2)}, u32[]{:S(2)}) collective-permute-start(bf16[8,256,640]{2,1,0:T(8,128)(2,1)} %pad_maximum_fusion.3.mine_ref), channel_id=1, source_target_pairs={{0,1},{1,0},{2,3},{3,2},{4,5},{5,4},{6,7},{7,6},{8,9},{9,8},{10,11... | collective-permute-start | bytes 7864328 | tf_op jit(solution)/shard_map/cond/branch_1_fun/ppermute | solution.py:280
  148.8 12.9 %collective-permute-start.6 = (bf16[3,2,2,128,128]{4,3,2,1,0:T(8,128)(2,1)}, bf16[3,2,2,128,128]{4,3,2,1,0:T(8,128)(2,1)S(1)}, u32[]{:S(2)}, u32[]{:S(2)}) collective-permute-start(bf16[3,2,2,128,128]{4,3,2,1,0:T(8,128)(2,1)} %get-tuple-element.103), channel_id=1, source_target_pairs={{4,0},{5,1},{6,2},{7,3},{8,4},{9,5},{10,6},{11,7},{12,8},{13,9},{1... | collective-permute-start | bytes 1179656 | tf_op jit(solution)/shard_map/cond/branch_1_fun/ppermute | solution.py:391
  150.9 12.6 %collective-permute-start.5 = (bf16[3,2,2,128,128]{4,3,2,1,0:T(8,128)(2,1)}, bf16[3,2,2,128,128]{4,3,2,1,0:T(8,128)(2,1)}, u32[]{:S(2)}, u32[]{:S(2)}) collective-permute-start(bf16[3,2,2,128,128]{4,3,2,1,0:T(8,128)(2,1)} %get-tuple-element.104), channel_id=1, source_target_pairs={{0,4},{1,5},{2,6},{3,7},{4,8},{5,9},{6,10},{7,11},{8,12},{9,13},{1... | collective-permute-start | bytes 1179656 | tf_op jit(solution)/shard_map/cond/branch_1_fun/ppermute | solution.py:390
  161.6 1.8 copy-start.13
  169.3 5.2 %copy-start = (bf16[16,3,2,128,128]{4,3,2,1,0:T(8,128)(2,1)}, bf16[16,3,2,128,128]{4,3,2,1,0:T(8,128)(2,1)S(1)}, u32[]{:S(2)}) copy-start(bf16[16,3,2,128,128]{4,3,2,1,0:T(8,128)(2,1)S(1)} %all-to-all-done.3.data_ref) | copy-start | bytes 9437188 | tf_op jit(solution)/shard_map/cond
  169.3 24.0 %all-to-all-start.5 = ((bf16[4,2,128,128]{3,2,1,0:T(8,128)(2,1)}), bf16[4,2,128,128]{3,2,1,0:T(8,128)(2,1)S(1)}, u32[]{:S(2)}, u32[]{:S(2)}) async-start(bf16[4,2,128,128]{3,2,1,0:T(8,128)(2,1)} %narrow.1), calls=%async_computation.5 | async-start | bytes 524288 | tf_op jit(solution)/shard_map/cond/branch_1_fun/all_to_all | solution.py:373
  193.3 7.5 %copy-start.7 = (bf16[128,5120]{1,0:T(8,128)(2,1)S(1)}, bf16[128,5120]{1,0:T(8,128)(2,1)}, u32[]{:S(2)}) copy-start(bf16[128,5120]{1,0:T(8,128)(2,1)} %get-tuple-element.96.query_ref) | copy-start | bytes 3932164 | tf_op jit(solution)/shard_map/cond
  193.3 17.5 %copy-start.12 = (bf16[4,2,128,128]{3,2,1,0:T(8,128)(2,1)}, bf16[4,2,128,128]{3,2,1,0:T(8,128)(2,1)S(1)}, u32[]{:S(2)}) copy-start(bf16[4,2,128,128]{3,2,1,0:T(8,128)(2,1)S(1)} %all-to-all-done.5.refs_3_) | copy-start | bytes 786436 | tf_op jit(solution)/shard_map/cond
  193.3 31.8 %all-to-all-start.4 = ((bf16[16,2,128,128]{3,2,1,0:T(8,128)(2,1)}), bf16[16,2,128,128]{3,2,1,0:T(8,128)(2,1)S(1)}, u32[]{:S(2)}, u32[]{:S(2)}) async-start(bf16[16,2,128,128]{3,2,1,0:T(8,128)(2,1)} %attend.3), calls=%async_computation.4 | async-start | bytes 2097152 | tf_op jit(solution)/shard_map/cond/branch_1_fun/all_to_all | solution.py:373
  225.1 1.0 copy-start.10
where the time goes:
time: 230 us; the launch traced here: 229 us
  waiting for transfers between devices  132 us (57%)
  Pallas kernels  48.9 us (21%)
  starting transfers between devices  32.7 us (14%)
  other arithmetic  9.78 us (4%)
  local copies, waits for them, and re-layouts  4.15 us (2%)
    ppermute x4, waiting for transfers between devices, swap(): lax.ppermute(values, 'seq', [(source, source ^ distance) for source in ra...  109 us
    all_to_all x4, starting transfers between devices, exchange(): lax.all_to_all(values, 'seq', split_axis=0, concat_axis=0, tiled=True, ax...  22.9 us
    pallas_call x1, Pallas kernels, attention(): pl.pallas_call(functools.partial(attend_kernel, scale=scale), out_shape=j...  18.8 us
    all_to_all x4, waiting for transfers between devices, exchange(): lax.all_to_all(values, 'seq', split_axis=0, concat_axis=0, tiled=True, ax...  14.3 us
    pallas_call x1, Pallas kernels, cross_attention(): pl.pallas_call(functools.partial(cross_pairs_kernel, head_dim=head_dim, s...  10 us
    ppermute x1, waiting for transfers between devices, attention(): lax.ppermute(own[:REACH, 1:], 'seq', [(high, low) for low, high in upward])  6.86 us
    pallas_call x1, Pallas kernels, attention(): pl.pallas_call(functools.partial(narrow_kernel, scale=scale, reach=REACH)...  5.87 us
    pallas_call x1, Pallas kernels, attention(): pl.pallas_call(functools.partial(pack_kernel, head_dim=head_dim), out_sha...  5.5 us
  transfers between devices with their start and end apart: 10, of which 6 were waited for; matrix products, arithmetic and copies ran while one was open for 3% of the time, Pallas kernels for 17%

commit v1 on v0

--- a/solution.py
+++ b/solution.py
@@ -11,53 +11,54 @@
 
 SB = 16
 SEATS = 4
-REACH = 3
+REACH = 4
 LOG2_E = 1.4426950408889634
 
 
-def pack_kernel(*refs, head_dim):
-    query_ref, key_ref, value_ref = sources = refs[-5:-2] if len(refs) == 7 else refs[-4:-1]
-    orders, outs = (refs[:2], refs[-2:]) if len(refs) == 7 else (refs[:1], refs[-1:])
-    del query_ref, key_ref, value_ref
-    for order_ref, out_ref in zip(orders, outs):
-        per_run = out_ref.shape[2]
-
-        def fill(slot, carry, order_ref=order_ref, out_ref=out_ref, per_run=per_run):
-            head = jnp.maximum(order_ref[slot], 0)
+def pack_kernel(order_ref, query_ref, key_ref, value_ref, *out_refs, head_dim):
+    sources = (query_ref, key_ref, value_ref)
+    first = 0
+    for out_ref in out_refs:
+        seats, _ = out_ref.shape[:2]
+
+        def fill(seat, carry, out_ref=out_ref, first=first):
+            head = jnp.maximum(order_ref[first + seat], 0)
             columns = pl.ds(pl.multiple_of(head * head_dim, head_dim), head_dim)
             for index, source in enumerate(sources):
-                out_ref[slot // per_run, index, slot % per_run] = source[:, columns]
+                out_ref[seat, index] = source[:, columns]
             return carry
 
-        lax.fori_loop(0, out_ref.shape[0] * per_run, fill, 0)
-
-
-def unpack_kernel(*refs, head_dim):
-    count = len(refs) // 2
+        lax.fori_loop(0, seats, fill, 0)
+        first += seats
+
+
+def unpack_kernel(order_ref, *refs, head_dim):
     out_ref = refs[-1]
-    for order_ref, returned_ref in zip(refs[:count], refs[count:-1]):
-        per_run = returned_ref.shape[1]
-
-        def fill(slot, carry, order_ref=order_ref, returned_ref=returned_ref, per_run=per_run):
-            head = order_ref[slot]
+    first = 0
+    for returned_ref in refs[:-1]:
+        seats = returned_ref.shape[0]
+
+        def fill(seat, carry, returned_ref=returned_ref, first=first):
+            head = order_ref[first + seat]
 
             @pl.when(head >= 0)
             def _():
                 columns = pl.ds(pl.multiple_of(head * head_dim, head_dim), head_dim)
-                out_ref[:, columns] = returned_ref[slot // per_run, slot % per_run]
+                out_ref[:, columns] = returned_ref[seat]
 
             return carry
 
-        lax.fori_loop(0, returned_ref.shape[0] * per_run, fill, 0)
+        lax.fori_loop(0, seats, fill, 0)
+        first += seats
 
 
 def attend_tile(tile, width, band, data_ref, out_ref, score_ref, scale):
-    stripe_len, _, _, rows, head_dim = data_ref.shape
+    stripe_len, _, rows, head_dim = data_ref.shape
     start = jnp.clip(2 * tile - band, 0, stripe_len - width)
-    query = data_ref[pl.ds(2 * tile, 2), 0, 0].reshape(2 * rows, head_dim)
+    query = data_ref[pl.ds(2 * tile, 2), 0].reshape(2 * rows, head_dim)
     peak = None
     for chunk in range(0, width, 2):
-        keys = data_ref[pl.ds(start + chunk, 2), 1, 0].reshape(2 * rows, head_dim)
+        keys = data_ref[pl.ds(start + chunk, 2), 1].reshape(2 * rows, head_dim)
         scores = lax.dot_general(
             query, keys, (((1,), (1,)), ((), ())), preferred_element_type=jnp.float32
         )
@@ -80,7 +81,7 @@
         weights = jnp.exp2(
             (score_ref[:, chunk * rows : (chunk + 2) * rows] - peak) * (scale * LOG2_E)
         )
-        values = data_ref[pl.ds(start + chunk, 2), 2, 0].reshape(2 * rows, head_dim)
+        values = data_ref[pl.ds(start + chunk, 2), 2].reshape(2 * rows, head_dim)
         partial = weights[:, :rows] + weights[:, rows:]
         product = jnp.dot(
             weights.astype(jnp.bfloat16), values, preferred_element_type=jnp.float32
@@ -88,14 +89,14 @@
         total = partial if total is None else total + partial
         running = product if running is None else running + product
     total = jnp.sum(total, axis=1, keepdims=True)
-    out_ref[pl.ds(2 * tile, 2), 0] = (
+    out_ref[pl.ds(2 * tile, 2)] = (
         (running / total).astype(jnp.bfloat16).reshape(2, rows, head_dim)
     )
 
 
 def attend_kernel(band_ref, data_ref, out_ref, score_ref, *, scale):
     stripe_len = data_ref.shape[0]
-    band = band_ref[pl.program_id(0)]
+    band = band_ref[0]
 
     def step(tile, carry):
         low = jnp.maximum(2 * tile - band, 0)
@@ -142,46 +143,55 @@
     lax.fori_loop(0, query_ref.shape[1] // head_dim // group, step, 0)
 
 
-def narrow_kernel(band_ref, place_ref, own_ref, low_ref, high_ref, out_ref, *, scale, reach):
-    seats, _, per_run, _, _ = own_ref.shape
-    first = place_ref[0]
-
-    def block_of(part, place, run):
-        if place < reach:
-            return low_ref[place, part, run]
-        if place < reach + seats:
-            return own_ref[place - reach, part + 1, run]
-        return high_ref[place - reach - seats, part, run]
+def narrow_kernel(place_ref, *refs, scale):
+    own_refs, (low_ref, high_ref) = refs[:SEATS], refs[SEATS : SEATS + 2]
+    out_refs, (query_ref, key_ref, value_ref) = refs[SEATS + 2 : -3], refs[-3:]
+    per_run, _, _, _ = own_refs[0].shape
+    seat, first = place_ref[0], place_ref[1]
 
     def step(run, carry):
-        band = band_ref[run]
-        for seat in range(seats):
-            query = own_ref[seat, 0, run]
+        band = place_ref[2 + run]
+        for turn in range(SEATS):
+            there = seat ^ turn
+            query_ref[there] = own_refs[turn][run, 0]
+            key_ref[SEATS + there] = own_refs[turn][run, 1]
+            value_ref[SEATS + there] = own_refs[turn][run, 2]
+            key_ref[there] = low_ref[turn, run, 0]
+            value_ref[there] = low_ref[turn, run, 1]
+            key_ref[2 * SEATS + there] = high_ref[turn, run, 0]
+            value_ref[2 * SEATS + there] = high_ref[turn, run, 1]
+
+        def attend(turn):
+            there = seat ^ turn
+            query = query_ref[there]
             tiles = []
-            for place in range(seat, seat + 2 * reach + 1):
+            for gap in range(-REACH, REACH + 1):
                 scores = lax.dot_general(
                     query,
-                    block_of(0, place, run),
+                    key_ref[SEATS + there + gap],
                     (((1,), (1,)), ((), ())),
                     preferred_element_type=jnp.float32,
                 )
-                if place != seat + reach:
-                    block = first + place - reach
-                    outside = (abs(place - seat - reach) > band) | (block < 0) | (block >= SB)
+                if gap:
+                    block = first + there + gap
+                    outside = (abs(gap) > band) | (block < 0) | (block >= SB)
                     scores = scores + jnp.where(outside, -jnp.inf, 0.0).astype(jnp.float32)
                 tiles.append(scores)
             peak = jnp.max(functools.reduce(jnp.maximum, tiles), axis=1, keepdims=True)
             total, running = 0.0, 0.0
-            for place, scores in enumerate(tiles, seat):
+            for gap, scores in enumerate(tiles, -REACH):
                 weights = jnp.exp2((scores - peak) * (scale * LOG2_E))
                 total = total + weights
                 running = running + jnp.dot(
                     weights.astype(jnp.bfloat16),
-                    block_of(1, place, run),
+                    value_ref[SEATS + there + gap],
                     preferred_element_type=jnp.float32,
                 )
             total = jnp.sum(total, axis=1, keepdims=True)
-            out_ref[seat, run] = (running / total).astype(jnp.bfloat16)
+            out_refs[turn][run] = (running / total).astype(jnp.bfloat16)
+
+        for turn in range(SEATS):
+            attend(turn)
         return carry
 
     lax.fori_loop(0, per_run, step, 0)
@@ -324,19 +334,16 @@
     )(place, cross_query, text, other)
 
 
-def deal(rank, band_width, first, seats, per_run):
-    slot_ids = jnp.arange(seats * per_run, dtype=jnp.int32)
-    run, seat = slot_ids % per_run, slot_ids // per_run
-    wanted = first + run * seats + jnp.where(run % 2 == 0, seat, seats - 1 - seat)
-    hits = wanted[:, None] == rank[None, :]
-    head_ids = jnp.arange(rank.shape[0], dtype=jnp.int32)
-    order = jnp.sum(jnp.where(hits, head_ids[None, :] + 1, 0), axis=1) - 1
-    bands = jnp.sum(jnp.where(hits, band_width[None, :] + 1, 0), axis=1) - 1
-    return order, bands
-
-
-def index_groups(devices, size):
-    return [list(range(first, first + size)) for first in range(0, devices, size)]
+def exchange(values):
+    devices = lax.axis_size("seq")
+    return lax.all_to_all(
+        values,
+        "seq",
+        split_axis=0,
+        concat_axis=0,
+        tiled=True,
+        axis_index_groups=[list(range(first, first + SB)) for first in range(0, devices, SB)],
+    )
 
 
 def attention(rank, per_run, narrow_run, arrays):
@@ -351,96 +358,90 @@
     scale = 1.0 / math.sqrt(head_dim)
     vmem = pl.BlockSpec(memory_space=pltpu.VMEM)
     smem = pl.BlockSpec(memory_space=pltpu.SMEM)
+    seat = device % SEATS
+
+    def block_array(*lead):
+        return jax.ShapeDtypeStruct(lead + (tok_rows, head_dim), jnp.bfloat16)
 
     text = None
     if doubles(key_weight, head_dim):
         text = project(context, key_weight, value_weight)
         came = swap(text, devices // 2)
-    deals = [deal(rank, band_width, 0, SB, per_run)]
-    shapes = [(SB, 3, per_run, tok_rows, head_dim)]
+        text = jnp.concatenate([text, came], axis=0)
+
+    slot_ids = jnp.arange(SB * per_run, dtype=jnp.int32)
+    run, place = slot_ids // SB, slot_ids % SB
+    wanted = run * SB + jnp.where(run % 2 == 0, place, SB - 1 - place)
+    mine = jnp.where(jnp.arange(per_run) % 2 == 0, device % SB, SB - 1 - device % SB)
+    mine = mine + jnp.arange(per_run, dtype=jnp.int32) * SB
     if narrow_run:
-        deals.append(deal(rank, band_width, SB * per_run, SEATS, narrow_run))
-        shapes.append((SEATS, 3, narrow_run, tok_rows, head_dim))
+        slot_ids = jnp.arange(SEATS * narrow_run, dtype=jnp.int32)
+        run, place = slot_ids % narrow_run, (slot_ids // narrow_run) ^ seat
+        near = SB * per_run + run * SEATS + jnp.where(run % 2 == 0, place, SEATS - 1 - place)
+        wanted = jnp.concatenate([wanted, near])
+        mine = jnp.concatenate([mine, near[:narrow_run]])
+    head_ids = jnp.arange(head_count, dtype=jnp.int32)
+    order = jnp.sum(jnp.where(wanted[:, None] == rank[None, :], head_ids + 1, 0), axis=1) - 1
+    bands = jnp.sum(jnp.where(mine[:, None] == rank[None, :], band_width + 1, 0), axis=1) - 1
+
     packed = pl.pallas_call(
         functools.partial(pack_kernel, head_dim=head_dim),
-        out_shape=[jax.ShapeDtypeStruct(shape, jnp.bfloat16) for shape in shapes],
-        in_specs=[smem] * len(deals) + [vmem] * 3,
-        out_specs=[vmem] * len(deals),
+        out_shape=[block_array(SB, 3)] * per_run
+        + [block_array(narrow_run, 3)] * (SEATS if narrow_run else 0),
+        in_specs=[smem] + [vmem] * 3,
+        out_specs=[vmem] * (per_run + (SEATS if narrow_run else 0)),
         name="pack",
-    )(*[order for order, _ in deals], self_query, self_key, self_value)
-
-    def exchange(values, size):
-        return lax.all_to_all(
-            values,
-            "seq",
-            split_axis=0,
-            concat_axis=0,
-            tiled=True,
-            axis_index_groups=index_groups(devices, size),
-        )
-
-    outgoing = packed[0]
+    )(order, self_query, self_key, self_value)
+
+    returned = []
+    for index in range(per_run):
+        arrived = exchange(packed[index])
+        result = pl.pallas_call(
+            functools.partial(attend_kernel, scale=scale),
+            out_shape=block_array(SB),
+            in_specs=[smem, vmem],
+            out_specs=vmem,
+            scratch_shapes=[pltpu.VMEM((2 * tok_rows, SB * tok_rows), jnp.float32)],
+            name="attend",
+        )(bands[index : index + 1], arrived)
+        returned.append(exchange(result))
     if narrow_run:
-        own = exchange(packed[1], SEATS)
+        own = [packed[per_run]]
+        for turn in range(1, SEATS):
+            own.append(swap(packed[per_run + turn], turn))
+        pairs = jnp.stack([part[:, 1:] for part in own])
         upward = [
             (source, source + SEATS)
             for source in range(devices - SEATS)
             if source // SB == (source + SEATS) // SB
         ]
-        low = lax.ppermute(own[SEATS - REACH :, 1:], "seq", upward)
-        high = lax.ppermute(own[:REACH, 1:], "seq", [(high, low) for low, high in upward])
-        if text is not None:
-            outgoing, came, own = lax.optimization_barrier((outgoing, came, own))
-        else:
-            outgoing, own = lax.optimization_barrier((outgoing, own))
-    elif text is not None:
-        outgoing, came = lax.optimization_barrier((outgoing, came))
-    arrived = exchange(outgoing, SB)
-    if text is not None:
-        text = jnp.concatenate([text, came], axis=0)
+        low = lax.ppermute(pairs, "seq", upward)
+        high = lax.ppermute(pairs, "seq", [(high, low) for low, high in upward])
+        places = jnp.stack([seat, device % SB - seat]).astype(jnp.int32)
+        near = pl.pallas_call(
+            functools.partial(narrow_kernel, scale=scale),
+            out_shape=[block_array(narrow_run)] * SEATS,
+            in_specs=[smem] + [vmem] * (SEATS + 2),
+            out_specs=[vmem] * SEATS,
+            scratch_shapes=[
+                pltpu.VMEM((count * SEATS, tok_rows, head_dim), jnp.bfloat16)
+                for count in (1, 3, 3)
+            ],
+            name="narrow",
+        )(jnp.concatenate([places, bands[per_run:]]), *own, low, high)
+        returned.append(near[0])
+        for turn in range(1, SEATS):
+            returned.append(swap(near[turn], turn))
     cross_out = cross_attention(
         cross_query, context, key_weight, value_weight, head_dim, scale, text
     )
-    own_bands = lax.dynamic_slice_in_dim(deals[0][1], (device % SB) * per_run, per_run)
-    results = pl.pallas_call(
-        functools.partial(attend_kernel, scale=scale),
-        out_shape=jax.ShapeDtypeStruct((SB, per_run, tok_rows, head_dim), jnp.bfloat16),
-        grid_spec=pltpu.PrefetchScalarGridSpec(
-            num_scalar_prefetch=1,
-            grid=(per_run,),
-            in_specs=[
-                pl.BlockSpec(
-                    (SB, 3, 1, tok_rows, head_dim), lambda run, bands: (0, 0, run, 0, 0)
-                )
-            ],
-            out_specs=pl.BlockSpec(
-                (SB, 1, tok_rows, head_dim), lambda run, bands: (0, run, 0, 0)
-            ),
-            scratch_shapes=[pltpu.VMEM((2 * tok_rows, SB * tok_rows), jnp.float32)],
-        ),
-        name="attend",
-    )(own_bands, arrived)
-    returned = [exchange(results, SB)]
-    if narrow_run:
-        narrow_bands = lax.dynamic_slice_in_dim(
-            deals[1][1], (device % SEATS) * narrow_run, narrow_run
-        )
-        first = jnp.reshape(device % SB // SEATS * SEATS, (1,)).astype(jnp.int32)
-        narrow = pl.pallas_call(
-            functools.partial(narrow_kernel, scale=scale, reach=REACH),
-            out_shape=jax.ShapeDtypeStruct((SEATS, narrow_run, tok_rows, head_dim), jnp.bfloat16),
-            in_specs=[smem, smem, vmem, vmem, vmem],
-            out_specs=vmem,
-            name="narrow",
-        )(narrow_bands, first, own, low, high)
-        returned.append(exchange(narrow, SEATS))
     self_out = pl.pallas_call(
         functools.partial(unpack_kernel, head_dim=head_dim),
         out_shape=jax.ShapeDtypeStruct((tok_rows, width), jnp.bfloat16),
-        in_specs=[smem] * len(deals) + [vmem] * len(deals),
+        in_specs=[smem] + [vmem] * len(returned),
         out_specs=vmem,
         name="unpack",
-    )(*[order for order, _ in deals], *returned)
+    )(order, *returned)
     return (self_out, cross_out)
 
 

time: 230 us -> 233 us (1.013)
  waiting for transfers between devices: 132 us -> 111 us
  starting transfers between devices: 32.7 us -> 52.8 us
  Pallas kernels: 48.9 us -> 52.4 us
    ppermute x4 -> x10, waiting for transfers between devices: 109 us -> 94.8 us  [swap(): lax.ppermute(values, 'seq', [(source, source ^ distance) for source in ra...]
    ppermute x4 -> x10, starting transfers between devices: 4.55 us -> 19 us  [swap(): lax.ppermute(values, 'seq', [(source, source ^ distance) for source in ra...]
    all_to_all x4, waiting for transfers between devices: 14.3 us -> 0.01 us  [exchange(): lax.all_to_all(values, 'seq', split_axis=0, concat_axis=0, tiled=True, ax...]
    ppermute x2, waiting for transfers between devices: 8.69 us -> 15.9 us  [the longest x1 15.9 us: attention(): high = lax.ppermute(pairs, 'seq', [(high, low) for low, high in upward])]
    all_to_all x4, starting transfers between devices: 22.9 us -> 28.4 us  [exchange(): lax.all_to_all(values, 'seq', split_axis=0, concat_axis=0, tiled=True, ax...]
    pallas_call x2 -> x3, Pallas kernels: 24.6 us -> 28.2 us  [the longest x2 21.6 us: attention(): pl.pallas_call(functools.partial(attend_kernel, scale=scale), out_shape=b...]
    another operation x0 -> x4, local copies, waits for them, and re-layouts: none -> 2.95 us  [attention(): pairs = jnp.stack([part[:, 1:] for part in own])]
  transfers between devices with their start and end apart: 10 -> 16, of which waited for: 6 -> 7; matrix products, arithmetic and copies ran while one was open for 3% -> 4% of each run, Pallas kernels for 17% -> 16%
where the time goes in v1:
time: 233 us; the launch traced here: 232 us
  waiting for transfers between devices  111 us (48%)
  starting transfers between devices  52.8 us (23%)
  Pallas kernels  52.4 us (22%)
  other arithmetic  9.16 us (4%)
  local copies, waits for them, and re-layouts  5 us (2%)
    ppermute x10, waiting for transfers between devices, swap(): lax.ppermute(values, 'seq', [(source, source ^ distance) for source in ra...  94.8 us
    all_to_all x4, starting transfers between devices, exchange(): lax.all_to_all(values, 'seq', split_axis=0, concat_axis=0, tiled=True, ax...  28.4 us
    pallas_call x2, Pallas kernels, attention(): pl.pallas_call(functools.partial(attend_kernel, scale=scale), out_shape=b...  21.6 us
    ppermute x10, starting transfers between devices, swap(): lax.ppermute(values, 'seq', [(source, source ^ distance) for source in ra...  19 us
    ppermute x1, waiting for transfers between devices, attention(): high = lax.ppermute(pairs, 'seq', [(high, low) for low, high in upward])  15.9 us
    pallas_call x1, Pallas kernels, cross_attention(): pl.pallas_call(functools.partial(cross_pairs_kernel, head_dim=head_dim, s...  10.4 us
    pallas_call x1, Pallas kernels, attention(): pl.pallas_call(functools.partial(narrow_kernel, scale=scale), out_shape=[...  6.61 us
    pallas_call x1, Pallas kernels, project(): pl.pallas_call(project_kernel, out_shape=jax.ShapeDtypeStruct((1, text_le...  5.42 us
  transfers between devices with their start and end apart: 16, of which 7 were waited for; matrix products, arithmetic and copies ran while one was open for 4% of the time, Pallas kernels for 16%

profile of v1, /device:TPU:13, one launch (start us, length us, event | category | flops | bytes accessed | tf_op | source)
XLA Modules:
  0.0 231.6 jit_solution(16778376307900007356)
XLA Ops:
  3.4 228.2 %conditional.1 = (bf16[128,5120]{1,0:T(8,128)(2,1)}, bf16[128,5120]{1,0:T(8,128)(2,1)}) conditional(s32[]{:T(128)} %convert_element_type.10, (s32[40,40]{1,0:T(8,128)S(1)}, s32[40]{0:T(128)}, bf16[128,5120]{1,0:T(8,128)(2,1)}, bf16[128,5120]{1,0:T(8,128)(2,1)}, bf16[128,5120]{1,0:T(8,128)(2,1)}, /*index=5*/bf16[4096,320]{0,1:T(8,128)(2,1)}, ...), branch_computations={%region_2.5_spmd, %region_5.8_spmd} | conditional | flops 6365161 | bytes 81537792 | solution.py:462
  4.5 5.3 %pack.3 = (bf16[16,3,128,128]{3,2,1,0:T(8,128)(2,1)}, bf16[16,3,128,128]{3,2,1,0:T(8,128)(2,1)}, bf16[2,3,128,128]{3,2,1,0:T(8,128)(2,1)}, bf16[2,3,128,128]{3,2...) custom-call(s32[40]{0:T(128)} %broadcast_add_fusion.4.order_ref, ...), custom_call_target="tpu_custom_call" | custom-call | tf_op jit(solution)/shard_map/cond/branch_1_fun/pack/pallas_call | solution.py:387
  9.8 6.8 %all-to-all-start.6 = ((bf16[16,3,128,128]{3,2,1,0:T(8,128)(2,1)}), bf16[16,3,128,128]{3,2,1,0:T(8,128)(2,1)}, u32[]{:S(2)}, u32[]{:S(2)}) async-start(bf16[16,3,128,128]{3,2,1,0:T(8,128)(2,1)} %get-tuple-element.53), calls=%async_computation.6 | async-start | bytes 3145728 | tf_op jit(solution)/shard_map/cond/branch_1_fun/all_to_all | solution.py:339
  16.6 5.4 %project.3 = bf16[1,256,640]{2,1,0:T(8,128)(2,1)} custom-call(bf16[256,4096]{1,0:T(8,128)(2,1)} %get-tuple-element.100.context_ref, bf16[320,4096]{1,0:T(8,128)(2,1)S(1)} %bitcast.20, bf16[320,4096]{1,0:T(8,128)(2,1)} %bitcast.22), custom_call_target="tpu_custom_call" | custom-call | tf_op jit(solution)/shard_map/cond/branch_1_fun/project/pallas_call | solution.py:224
  22.0 2.1 collective-permute-start.12
  24.1 40.5 %collective-permute-done.12 = bf16[1,256,640]{2,1,0:T(8,128)(2,1)S(1)} collective-permute-done((bf16[1,256,640]{2,1,0:T(8,128)(2,1)}, bf16[1,256,640]{2,1,0:T(8,128)(2,1)S(1)}, u32[]{:S(2)}, u32[]{:S(2)}) %collective-permute-start.12) | collective-permute-done | bytes 327712 | tf_op jit(solution)/shard_map/cond/branch_1_fun/ppermute | solution.py:290
  65.7 3.2 %collective-permute-start.13 = (bf16[2,256,640]{2,1,0:T(8,128)(2,1)S(1)}, bf16[2,256,640]{2,1,0:T(8,128)(2,1)S(1)}, u32[]{:S(2)}, u32[]{:S(2)}) collective-permute-start(bf16[2,256,640]{2,1,0:T(8,128)(2,1)S(1)} %pad_maximum_fusion.5), channel_id=1, source_target_pairs={{0,4},{1,5},{2,6},{3,7},{4,0},{5,1},{6,2},{7,3},{8,12},{9,13},{10,... | collective-permute-start | bytes 1966088 | tf_op jit(solution)/shard_map/cond/branch_1_fun/ppermute | solution.py:290
  68.8 5.2 %all-to-all-start.8 = ((bf16[16,3,128,128]{3,2,1,0:T(8,128)(2,1)}), bf16[16,3,128,128]{3,2,1,0:T(8,128)(2,1)}, u32[]{:S(2)}, u32[]{:S(2)}) async-start(bf16[16,3,128,128]{3,2,1,0:T(8,128)(2,1)} %get-tuple-element.54), calls=%async_computation.8 | async-start | bytes 3145728 | tf_op jit(solution)/shard_map/cond/branch_1_fun/all_to_all | solution.py:339
  74.1 14.2 %collective-permute-done.13 = bf16[2,256,640]{2,1,0:T(8,128)(2,1)S(1)} collective-permute-done((bf16[2,256,640]{2,1,0:T(8,128)(2,1)S(1)}, bf16[2,256,640]{2,1,0:T(8,128)(2,1)S(1)}, u32[]{:S(2)}, u32[]{:S(2)}) %collective-permute-start.13) | collective-permute-done | bytes 655392 | tf_op jit(solution)/shard_map/cond/branch_1_fun/ppermute | solution.py:290
  88.5 2.4 %collective-permute-start.14 = (bf16[4,256,640]{2,1,0:T(8,128)(2,1)S(1)}, bf16[4,256,640]{2,1,0:T(8,128)(2,1)}, u32[]{:S(2)}, u32[]{:S(2)}) collective-permute-start(bf16[4,256,640]{2,1,0:T(8,128)(2,1)S(1)} %pad_maximum_fusion.4), channel_id=1, source_target_pairs={{0,2},{1,3},{2,0},{3,1},{4,6},{5,7},{6,4},{7,5},{8,10},{9,11},{10,... | collective-permute-start | bytes 3932168 | tf_op jit(solution)/shard_map/cond/branch_1_fun/ppermute | solution.py:290
  90.9 31.0 %collective-permute-done.14 = bf16[4,256,640]{2,1,0:T(8,128)(2,1)} collective-permute-done((bf16[4,256,640]{2,1,0:T(8,128)(2,1)S(1)}, bf16[4,256,640]{2,1,0:T(8,128)(2,1)}, u32[]{:S(2)}, u32[]{:S(2)}) %collective-permute-start.14) | collective-permute-done | bytes 1310752 | tf_op jit(solution)/shard_map/cond/branch_1_fun/ppermute | solution.py:290
  123.6 6.6 %collective-permute-start.15 = (bf16[8,256,640]{2,1,0:T(8,128)(2,1)S(1)}, bf16[8,256,640]{2,1,0:T(8,128)(2,1)}, u32[]{:S(2)}, u32[]{:S(2)}) collective-permute-start(bf16[8,256,640]{2,1,0:T(8,128)(2,1)S(1)} %pad_maximum_fusion.3.mine_ref), channel_id=1, source_target_pairs={{0,1},{1,0},{2,3},{3,2},{4,5},{5,4},{6,7},{7,6},{8,9},{9,8},{10,11... | collective-permute-start | bytes 7864328 | tf_op jit(solution)/shard_map/cond/branch_1_fun/ppermute | solution.py:290
  131.0 11.7 %attend.8 = bf16[16,128,128]{2,1,0:T(8,128)(2,1)} custom-call(s32[1]{0:T(128)} %get-tuple-element.107.band_ref, bf16[16,3,128,128]{3,2,1,0:T(8,128)(2,1)} %all-to-all-done.6.data_ref), custom_call_target="tpu_custom_call" | custom-call | tf_op jit(solution)/shard_map/cond/branch_1_fun/attend/pallas_call | solution.py:399
  142.7 7.0 %all-to-all-start.7 = ((bf16[16,128,128]{2,1,0:T(8,128)(2,1)}), bf16[16,128,128]{2,1,0:T(8,128)(2,1)S(1)}, u32[]{:S(2)}, u32[]{:S(2)}) async-start(bf16[16,128,128]{2,1,0:T(8,128)(2,1)} %attend.8), calls=%async_computation.7 | async-start | bytes 1048576 | tf_op jit(solution)/shard_map/cond/branch_1_fun/all_to_all | solution.py:339
  153.2 5.9 %collective-permute-done.5.refs_2_ = bf16[2,3,128,128]{3,2,1,0:T(8,128)(2,1)S(1)} collective-permute-done((bf16[2,3,128,128]{3,2,1,0:T(8,128)(2,1)}, bf16[2,3,128,128]{3,2,1,0:T(8,128)(2,1)S(1)}, u32[]{:S(2)}, u32[]{:S(2)}) %collective-permute-start.5) | collective-permute-done | bytes 196640 | tf_op jit(solution)/shard_map/cond/branch_1_fun/ppermute | solution.py:290
  160.5 9.9 %attend.9 = bf16[16,128,128]{2,1,0:T(8,128)(2,1)} custom-call(s32[1]{0:T(128)} %get-tuple-element.106.band_ref, bf16[16,3,128,128]{3,2,1,0:T(8,128)(2,1)} %all-to-all-done.8.data_ref), custom_call_target="tpu_custom_call" | custom-call | tf_op jit(solution)/shard_map/cond/branch_1_fun/attend/pallas_call | solution.py:399
  170.5 9.4 %all-to-all-start.9 = ((bf16[16,128,128]{2,1,0:T(8,128)(2,1)}), bf16[16,128,128]{2,1,0:T(8,128)(2,1)}, u32[]{:S(2)}, u32[]{:S(2)}) async-start(bf16[16,128,128]{2,1,0:T(8,128)(2,1)} %attend.9), calls=%async_computation.9 | async-start | bytes 1048576 | tf_op jit(solution)/shard_map/cond/branch_1_fun/all_to_all | solution.py:339
  180.9 1.8 pad_maximum_fusion.6
  182.7 2.2 collective-permute-start.8
  184.9 3.1 %collective-permute-start.7 = (bf16[4,2,2,128,128]{4,3,2,1,0:T(8,128)(2,1)}, bf16[4,2,2,128,128]{4,3,2,1,0:T(8,128)(2,1)}, u32[]{:S(2)}, u32[]{:S(2)}) collective-permute-start(bf16[4,2,2,128,128]{4,3,2,1,0:T(8,128)(2,1)} %pad_maximum_fusion.6), channel_id=1, source_target_pairs={{0,4},{1,5},{2,6},{3,7},{4,8},{5,9},{6,10},{7,11},{8,12},{9,13},{1... | collective-permute-start | bytes 1572872 | tf_op jit(solution)/shard_map/cond/branch_1_fun/ppermute | solution.py:418
  188.7 15.9 %collective-permute-done.8.refs_5_ = bf16[4,2,2,128,128]{4,3,2,1,0:T(8,128)(2,1)} collective-permute-done((bf16[4,2,2,128,128]{4,3,2,1,0:T(8,128)(2,1)}, bf16[4,2,2,128,128]{4,3,2,1,0:T(8,128)(2,1)}, u32[]{:S(2)}, u32[]{:S(2)}) %collective-permute-start.8) | collective-permute-done | bytes 524320 | tf_op jit(solution)/shard_map/cond/branch_1_fun/ppermute | solution.py:419
  204.6 6.6 %narrow.1 = (bf16[2,128,128]{2,1,0:T(8,128)(2,1)}, bf16[2,128,128]{2,1,0:T(8,128)(2,1)}, bf16[2,128,128]{2,1,0:T(8,128)(2,1)}, bf16[2,128,128]{2,1,0:T(8,128)(2,1)}) custom-call(s32[4]{0:T(128)} %pad_add_fusion.3.place_ref, bf16[2,3,128,128]{3,2,1,0:T(8,128)(2,1)} %get-tuple-element.55.refs_0_, bf16[2,3,128,128]{3,2,1,0:T(8,128)(2,1)} %copy-done.12, ...), custom_call_target="tpu_custom_call" | custom-call | tf_op jit(solution)/shard_map/cond/branch_1_fun/narrow/pallas_call | solution.py:421
  218.2 3.0 %unpack.3 = bf16[128,5120]{1,0:T(8,128)(2,1)} custom-call(s32[40]{0:T(128)} %broadcast_add_fusion.4.order_ref, bf16[16,128,128]{2,1,0:T(8,128)(2,1)} %copy-done.8, bf16[16,128,128]{2,1,0:T(8,128)(2,1)} %all-to-all-done.9.refs_1_, bf16[2,128,128]{2,1,0:T(8,128)(2,1)} %get-tuple-element.59.refs_2_, bf16[2,128,128]{2,1,0:T(8,128)(2,1)} %copy-done.15, ...), custom_call_target="tpu_custom_call" | custom-call | tf_op jit(solution)/shard_map/cond/branch_1_fun/unpack/pallas_call | solution.py:438
  221.2 10.4 %cross.3 = bf16[128,5120]{1,0:T(8,128)(2,1)} custom-call(s32[2]{0:T(128)} %pad_add_fusion.4.place_ref, bf16[128,5120]{1,0:T(8,128)(2,1)} %get-tuple-element.102.query_ref, bf16[8,256,640]{2,1,0:T(8,128)(2,1)} %copy-done, bf16[8,256,640]{2,1,0:T(8,128)(2,1)} %collective-permute-done.15.other_ref), custom_call_target="tpu_custom_call" | custom-call | tf_op jit(solution)/shard_map/cond/branch_1_fun/cross/pallas_call | solution.py:327
  (67 shorter events, 20.3 us)
Async XLA Ops:
  9.8 6.8 %copy-start.3 = (bf16[4096,320]{0,1:T(8,128)(2,1)S(1)}, bf16[4096,320]{0,1:T(8,128)(2,1)}, u32[]{:S(2)}) copy-start(bf16[4096,320]{0,1:T(8,128)(2,1)} %get-tuple-element.96) | copy-start | bytes 7864324 | tf_op jit(solution)/shard_map/cond
  9.8 59.0 %all-to-all-start.6 = ((bf16[16,3,128,128]{3,2,1,0:T(8,128)(2,1)}), bf16[16,3,128,128]{3,2,1,0:T(8,128)(2,1)}, u32[]{:S(2)}, u32[]{:S(2)}) async-start(bf16[16,3,128,128]{3,2,1,0:T(8,128)(2,1)} %get-tuple-element.53), calls=%async_computation.6 | async-start | bytes 3145728 | tf_op jit(solution)/shard_map/cond/branch_1_fun/all_to_all | solution.py:339
  22.0 42.6 %collective-permute-start.12 = (bf16[1,256,640]{2,1,0:T(8,128)(2,1)}, bf16[1,256,640]{2,1,0:T(8,128)(2,1)S(1)}, u32[]{:S(2)}, u32[]{:S(2)}) collective-permute-start(bf16[1,256,640]{2,1,0:T(8,128)(2,1)} %project.3), channel_id=1, source_target_pairs={{0,8},{1,9},{2,10},{3,11},{4,12},{5,13},{6,14},{7,15},{8,0},{9,1},... | collective-permute-start | bytes 983048 | tf_op jit(solution)/shard_map/cond/branch_1_fun/ppermute | solution.py:290
  65.7 22.6 %collective-permute-start.13 = (bf16[2,256,640]{2,1,0:T(8,128)(2,1)S(1)}, bf16[2,256,640]{2,1,0:T(8,128)(2,1)S(1)}, u32[]{:S(2)}, u32[]{:S(2)}) collective-permute-start(bf16[2,256,640]{2,1,0:T(8,128)(2,1)S(1)} %pad_maximum_fusion.5), channel_id=1, source_target_pairs={{0,4},{1,5},{2,6},{3,7},{4,0},{5,1},{6,2},{7,3},{8,12},{9,13},{10,... | collective-permute-start | bytes 1966088 | tf_op jit(solution)/shard_map/cond/branch_1_fun/ppermute | solution.py:290
  68.8 19.4 %copy-start.5 = (bf16[1,256,640]{2,1,0:T(8,128)(2,1)S(1)}, bf16[1,256,640]{2,1,0:T(8,128)(2,1)}, u32[]{:S(2)}) copy-start(bf16[1,256,640]{2,1,0:T(8,128)(2,1)} %project.3) | copy-start | bytes 983044 | tf_op jit(solution)/shard_map/cond
  68.8 73.9 %all-to-all-start.8 = ((bf16[16,3,128,128]{3,2,1,0:T(8,128)(2,1)}), bf16[16,3,128,128]{3,2,1,0:T(8,128)(2,1)}, u32[]{:S(2)}, u32[]{:S(2)}) async-start(bf16[16,3,128,128]{3,2,1,0:T(8,128)(2,1)} %get-tuple-element.54), calls=%async_computation.8 | async-start | bytes 3145728 | tf_op jit(solution)/shard_map/cond/branch_1_fun/all_to_all | solution.py:339
  88.5 33.5 %collective-permute-start.14 = (bf16[4,256,640]{2,1,0:T(8,128)(2,1)S(1)}, bf16[4,256,640]{2,1,0:T(8,128)(2,1)}, u32[]{:S(2)}, u32[]{:S(2)}) collective-permute-start(bf16[4,256,640]{2,1,0:T(8,128)(2,1)S(1)} %pad_maximum_fusion.4), channel_id=1, source_target_pairs={{0,2},{1,3},{2,0},{3,1},{4,6},{5,7},{6,4},{7,5},{8,10},{9,11},{10,... | collective-permute-start | bytes 3932168 | tf_op jit(solution)/shard_map/cond/branch_1_fun/ppermute | solution.py:290
  90.9 39.3 %copy-start.19 = (s32[40]{0:T(128)S(1)}, s32[40]{0:T(128)}, u32[]{:S(2)}) copy-start(s32[40]{0:T(128)} %get-tuple-element.49) | copy-start | bytes 484 | tf_op jit(solution)/shard_map/cond
  123.6 19.1 %copy-start = (bf16[8,256,640]{2,1,0:T(8,128)(2,1)}, bf16[8,256,640]{2,1,0:T(8,128)(2,1)S(1)}, u32[]{:S(2)}) copy-start(bf16[8,256,640]{2,1,0:T(8,128)(2,1)S(1)} %pad_maximum_fusion.3.mine_ref) | copy-start | bytes 7864324 | tf_op jit(solution)/shard_map/cond
  123.6 97.6 %collective-permute-start.15 = (bf16[8,256,640]{2,1,0:T(8,128)(2,1)S(1)}, bf16[8,256,640]{2,1,0:T(8,128)(2,1)}, u32[]{:S(2)}, u32[]{:S(2)}) collective-permute-start(bf16[8,256,640]{2,1,0:T(8,128)(2,1)S(1)} %pad_maximum_fusion.3.mine_ref), channel_id=1, source_target_pairs={{0,1},{1,0},{2,3},{3,2},{4,5},{5,4},{6,7},{7,6},{8,9},{9,8},{10,11... | collective-permute-start | bytes 7864328 | tf_op jit(solution)/shard_map/cond/branch_1_fun/ppermute | solution.py:290
  131.0 20.8 %copy-start.11 = (bf16[2,3,128,128]{3,2,1,0:T(8,128)(2,1)S(1)}, bf16[2,3,128,128]{3,2,1,0:T(8,128)(2,1)}, u32[]{:S(2)}) copy-start(bf16[2,3,128,128]{3,2,1,0:T(8,128)(2,1)} %get-tuple-element.55.refs_0_) | copy-start | bytes 589828 | tf_op jit(solution)/shard_map/cond
  142.7 27.7 %all-to-all-start.7 = ((bf16[16,128,128]{2,1,0:T(8,128)(2,1)}), bf16[16,128,128]{2,1,0:T(8,128)(2,1)S(1)}, u32[]{:S(2)}, u32[]{:S(2)}) async-start(bf16[16,128,128]{2,1,0:T(8,128)(2,1)} %attend.8), calls=%async_computation.7 | async-start | bytes 1048576 | tf_op jit(solution)/shard_map/cond/branch_1_fun/all_to_all | solution.py:339
  149.7 2.8 %collective-permute-start.4 = (bf16[2,3,128,128]{3,2,1,0:T(8,128)(2,1)}, bf16[2,3,128,128]{3,2,1,0:T(8,128)(2,1)S(1)}, u32[]{:S(2)}, u32[]{:S(2)}) collective-permute-start(bf16[2,3,128,128]{3,2,1,0:T(8,128)(2,1)} %get-tuple-element.56), channel_id=1, source_target_pairs={{0,1},{1,0},{2,3},{3,2},{4,5},{5,4},{6,7},{7,6},{8,9},{9,8},{10,11... | collective-permute-start | bytes 589832 | tf_op jit(solution)/shard_map/cond/branch_1_fun/ppermute | solution.py:290
  150.1 9.0 %collective-permute-start.5 = (bf16[2,3,128,128]{3,2,1,0:T(8,128)(2,1)}, bf16[2,3,128,128]{3,2,1,0:T(8,128)(2,1)S(1)}, u32[]{:S(2)}, u32[]{:S(2)}) collective-permute-start(bf16[2,3,128,128]{3,2,1,0:T(8,128)(2,1)} %get-tuple-element.57), channel_id=1, source_target_pairs={{0,2},{1,3},{2,0},{3,1},{4,6},{5,7},{6,4},{7,5},{8,10},{9,11},{10,... | collective-permute-start | bytes 589832 | tf_op jit(solution)/shard_map/cond/branch_1_fun/ppermute | solution.py:290
  150.4 29.5 %collective-permute-start.6 = (bf16[2,3,128,128]{3,2,1,0:T(8,128)(2,1)}, bf16[2,3,128,128]{3,2,1,0:T(8,128)(2,1)}, u32[]{:S(2)}, u32[]{:S(2)}) collective-permute-start(bf16[2,3,128,128]{3,2,1,0:T(8,128)(2,1)} %get-tuple-element.58), channel_id=1, source_target_pairs={{0,3},{1,2},{2,1},{3,0},{4,7},{5,6},{6,5},{7,4},{8,11},{9,10},{10,... | collective-permute-start | bytes 589832 | tf_op jit(solution)/shard_map/cond/branch_1_fun/ppermute | solution.py:290
  152.5 17.9 %copy-start.12 = (bf16[2,3,128,128]{3,2,1,0:T(8,128)(2,1)}, bf16[2,3,128,128]{3,2,1,0:T(8,128)(2,1)S(1)}, u32[]{:S(2)}) copy-start(bf16[2,3,128,128]{3,2,1,0:T(8,128)(2,1)S(1)} %collective-permute-done.4.refs_1_) | copy-start | bytes 589828 | tf_op jit(solution)/shard_map/cond
  160.5 20.3 %copy-start.14 = (bf16[1,2,2,128,128]{4,3,2,1,0:T(8,128)(2,1)S(1)}, bf16[1,2,2,128,128]{4,3,2,1,0:T(8,128)(2,1)}, u32[]{:S(2)}) copy-start(bf16[1,2,2,128,128]{4,3,2,1,0:T(8,128)(2,1)} %slice_bitcast_fusion.3) | copy-start | bytes 393220 | tf_op jit(solution)/shard_map/cond
  170.5 40.7 %copy-start.8 = (bf16[16,128,128]{2,1,0:T(8,128)(2,1)}, bf16[16,128,128]{2,1,0:T(8,128)(2,1)S(1)}, u32[]{:S(2)}) copy-start(bf16[16,128,128]{2,1,0:T(8,128)(2,1)S(1)} %all-to-all-done.7.refs_0_) | copy-start | bytes 1572868 | tf_op jit(solution)/shard_map/cond
  170.5 47.1 %all-to-all-start.9 = ((bf16[16,128,128]{2,1,0:T(8,128)(2,1)}), bf16[16,128,128]{2,1,0:T(8,128)(2,1)}, u32[]{:S(2)}, u32[]{:S(2)}) async-start(bf16[16,128,128]{2,1,0:T(8,128)(2,1)} %attend.9), calls=%async_computation.9 | async-start | bytes 1048576 | tf_op jit(solution)/shard_map/cond/branch_1_fun/all_to_all | solution.py:339
  182.7 21.9 %collective-permute-start.8 = (bf16[4,2,2,128,128]{4,3,2,1,0:T(8,128)(2,1)}, bf16[4,2,2,128,128]{4,3,2,1,0:T(8,128)(2,1)}, u32[]{:S(2)}, u32[]{:S(2)}) collective-permute-start(bf16[4,2,2,128,128]{4,3,2,1,0:T(8,128)(2,1)} %pad_maximum_fusion.6), channel_id=1, source_target_pairs={{4,0},{5,1},{6,2},{7,3},{8,4},{9,5},{10,6},{11,7},{12,8},{13,9},{1... | collective-permute-start | bytes 1572872 | tf_op jit(solution)/shard_map/cond/branch_1_fun/ppermute | solution.py:419
  184.9 19.7 %collective-permute-start.7 = (bf16[4,2,2,128,128]{4,3,2,1,0:T(8,128)(2,1)}, bf16[4,2,2,128,128]{4,3,2,1,0:T(8,128)(2,1)}, u32[]{:S(2)}, u32[]{:S(2)}) collective-permute-start(bf16[4,2,2,128,128]{4,3,2,1,0:T(8,128)(2,1)} %pad_maximum_fusion.6), channel_id=1, source_target_pairs={{0,4},{1,5},{2,6},{3,7},{4,8},{5,9},{6,10},{7,11},{8,12},{9,13},{1... | collective-permute-start | bytes 1572872 | tf_op jit(solution)/shard_map/cond/branch_1_fun/ppermute | solution.py:418
  211.2 3.3 %collective-permute-start.9 = (bf16[2,128,128]{2,1,0:T(8,128)(2,1)}, bf16[2,128,128]{2,1,0:T(8,128)(2,1)S(1)}, u32[]{:S(2)}, u32[]{:S(2)}) collective-permute-start(bf16[2,128,128]{2,1,0:T(8,128)(2,1)} %get-tuple-element.60), channel_id=1, source_target_pairs={{0,1},{1,0},{2,3},{3,2},{4,5},{5,4},{6,7},{7,6},{8,9},{9,8},{10,11... | collective-permute-start | bytes 196616 | tf_op jit(solution)/shard_map/cond/branch_1_fun/ppermute | solution.py:290
  212.1 3.8 %collective-permute-start.10 = (bf16[2,128,128]{2,1,0:T(8,128)(2,1)}, bf16[2,128,128]{2,1,0:T(8,128)(2,1)S(1)}, u32[]{:S(2)}, u32[]{:S(2)}) collective-permute-start(bf16[2,128,128]{2,1,0:T(8,128)(2,1)} %get-tuple-element.61), channel_id=1, source_target_pairs={{0,2},{1,3},{2,0},{3,1},{4,6},{5,7},{6,4},{7,5},{8,10},{9,11},{10,... | collective-permute-start | bytes 196616 | tf_op jit(solution)/shard_map/cond/branch_1_fun/ppermute | solution.py:290
  212.4 5.1 %collective-permute-start.11 = (bf16[2,128,128]{2,1,0:T(8,128)(2,1)}, bf16[2,128,128]{2,1,0:T(8,128)(2,1)S(1)}, u32[]{:S(2)}, u32[]{:S(2)}) collective-permute-start(bf16[2,128,128]{2,1,0:T(8,128)(2,1)} %get-tuple-element.62), channel_id=1, source_target_pairs={{0,3},{1,2},{2,1},{3,0},{4,7},{5,6},{6,5},{7,4},{8,11},{9,10},{10,... | collective-permute-start | bytes 196616 | tf_op jit(solution)/shard_map/cond/branch_1_fun/ppermute | solution.py:290
  (5 other events, 8.8 us)

commit v2 on v1

--- a/solution.py
+++ b/solution.py
@@ -236,29 +236,68 @@
     )(context, key_weight.T, value_weight.T)
 
 
+def split_kernel(place_ref, query_ref, out_ref):
+    count, _, pair_width = out_ref.shape
+
+    def fill(entry, carry):
+        pair = 2 * entry + 1 - place_ref[1]
+        columns = pl.ds(pl.multiple_of(pair * pair_width, pair_width), pair_width)
+        out_ref[entry] = query_ref[:, columns]
+        return carry
+
+    lax.fori_loop(0, count, fill, 0)
+
+
+def merge_kernel(place_ref, own_ref, came_ref, out_ref):
+    count, _, pair_width = own_ref.shape
+
+    def fill(entry, carry):
+        for offset, part_ref in ((0, own_ref), (1, came_ref)):
+            pair = 2 * entry + (place_ref[1] ^ offset)
+            columns = pl.ds(pl.multiple_of(pair * pair_width, pair_width), pair_width)
+            out_ref[:, columns] = part_ref[entry]
+        return carry
+
+    lax.fori_loop(0, count, fill, 0)
+
+
 def cross_pairs_kernel(
-    place_ref, query_ref, mine_ref, other_ref, out_ref, key_ref, value_ref, *, head_dim, scale
+    place_ref,
+    query_ref,
+    guest_ref,
+    mine_ref,
+    other_ref,
+    own_ref,
+    sent_ref,
+    key_ref,
+    value_ref,
+    *,
+    head_dim,
+    scale,
 ):
     entries, _, pair_width = mine_ref.shape
+    rows = query_ref.shape[0]
     columns = pair_width // 2
     bits = entries.bit_length() - 1
 
     def attend(even_ref, odd_ref):
         def step(entry, carry):
-            pair = place_ref[0]
+            plane = place_ref[0]
             for bit in range(bits):
-                pair = pair ^ (((entry >> bit) & 1) << (bits - 1 - bit))
+                plane = plane ^ (((entry >> bit) & 1) << (bits - 1 - bit))
             key_ref[:, :columns] = even_ref[entry, :, :columns]
             key_ref[:, columns:] = odd_ref[entry, :, :columns]
             value_ref[:, :columns] = even_ref[entry, :, columns:]
             value_ref[:, columns:] = odd_ref[entry, :, columns:]
+            first = (2 * plane + place_ref[1]) * pair_width
             for offset in range(pair_width // head_dim):
                 source = pl.ds(offset * head_dim, head_dim)
-                target = pl.ds(
-                    pl.multiple_of(pair * pair_width + offset * head_dim, head_dim), head_dim
+                target = pl.ds(pl.multiple_of(first + offset * head_dim, head_dim), head_dim)
+                query = jnp.concatenate(
+                    [query_ref[:, target], guest_ref[plane, :, source]], axis=0
                 )
                 scores = lax.dot_general(
-                    query_ref[:, target],
+                    query,
                     key_ref[:, source],
                     (((1,), (1,)), ((), ())),
                     preferred_element_type=jnp.float32,
@@ -271,16 +310,18 @@
                     value_ref[:, source],
                     preferred_element_type=jnp.float32,
                 )
-                out_ref[:, target] = (running / total).astype(jnp.bfloat16)
+                result = (running / total).astype(jnp.bfloat16)
+                own_ref[plane, :, source] = result[:rows]
+                sent_ref[plane, :, source] = result[rows:]
             return carry
 
         lax.fori_loop(0, entries, step, 0)
 
-    @pl.when(place_ref[1] == 0)
+    @pl.when(place_ref[2] == 0)
     def _():
         attend(mine_ref, other_ref)
 
-    @pl.when(place_ref[1] == 1)
+    @pl.when(place_ref[2] == 1)
     def _():
         attend(other_ref, mine_ref)
 
@@ -292,7 +333,7 @@
 
 def doubles(key_weight, head_dim):
     devices = lax.axis_size("seq")
-    return (2 * key_weight.shape[1]) % head_dim == 0 and devices & (devices - 1) == 0
+    return (2 * key_weight.shape[1]) % head_dim == 0 and devices % 4 == 0 and devices & (devices - 1) == 0
 
 
 def cross_attention(cross_query, context, key_weight, value_weight, head_dim, scale, text):
@@ -316,22 +357,39 @@
             lax.all_gather(text_key.astype(jnp.bfloat16), "seq", axis=1, tiled=True),
             lax.all_gather(text_value.astype(jnp.bfloat16), "seq", axis=1, tiled=True),
         )
+    place = jnp.stack([device // 4, device // 2 % 2, device % 2]).astype(jnp.int32)
+    pair_shape = text.shape[1:]
+    part_shape = jax.ShapeDtypeStruct((devices // 4, tok_rows, pair_shape[1]), jnp.bfloat16)
+    leaving = pl.pallas_call(
+        split_kernel,
+        out_shape=part_shape,
+        in_specs=[smem, vmem],
+        out_specs=vmem,
+        name="split",
+    )(place, cross_query)
+    guests = swap(leaving, 2)
     distance = devices // 4
-    while distance > 1:
+    while distance > 2:
         came = swap(text, distance)
         text = jnp.concatenate([text, came], axis=0)
         distance //= 2
     other = swap(text, 1)
-    place = jnp.stack([device // 2, device % 2]).astype(jnp.int32)
-    pair = pltpu.VMEM(text.shape[1:], jnp.bfloat16)
+    own, sent = pl.pallas_call(
+        functools.partial(cross_pairs_kernel, head_dim=head_dim, scale=scale),
+        out_shape=[part_shape] * 2,
+        in_specs=[smem] + [vmem] * 4,
+        out_specs=[vmem] * 2,
+        scratch_shapes=[pltpu.VMEM(pair_shape, jnp.bfloat16)] * 2,
+        name="cross",
+    )(place, cross_query, guests, text, other)
+    back = swap(sent, 2)
     return pl.pallas_call(
-        functools.partial(cross_pairs_kernel, head_dim=head_dim, scale=scale),
+        merge_kernel,
         out_shape=out_shape,
-        in_specs=[smem, vmem, vmem, vmem],
+        in_specs=[smem, vmem, vmem],
         out_specs=vmem,
-        scratch_shapes=[pair, pair],
-        name="cross",
-    )(place, cross_query, text, other)
+        name="merge",
+    )(place, own, back)
 
 
 def exchange(values):
@@ -346,10 +404,35 @@
     )
 
 
-def attention(rank, per_run, narrow_run, arrays):
-    (self_query, self_key, self_value, cross_query, context, key_weight, value_weight, band_width) = (
-        arrays
-    )
+def pack(order, sources, shapes, head_dim):
+    vmem = pl.BlockSpec(memory_space=pltpu.VMEM)
+    return pl.pallas_call(
+        functools.partial(pack_kernel, head_dim=head_dim),
+        out_shape=shapes,
+        in_specs=[pl.BlockSpec(memory_space=pltpu.SMEM)] + [vmem] * 3,
+        out_specs=[vmem] * len(shapes),
+        name="pack",
+    )(order, *sources)
+
+
+def run_slot(outgoing, band, scale):
+    stripe_len, _, tok_rows, head_dim = outgoing.shape
+    vmem = pl.BlockSpec(memory_space=pltpu.VMEM)
+    arrived = exchange(outgoing)
+    result = pl.pallas_call(
+        functools.partial(attend_kernel, scale=scale),
+        out_shape=jax.ShapeDtypeStruct((stripe_len, tok_rows, head_dim), jnp.bfloat16),
+        in_specs=[pl.BlockSpec(memory_space=pltpu.SMEM), vmem],
+        out_specs=vmem,
+        scratch_shapes=[pltpu.VMEM((2 * tok_rows, stripe_len * tok_rows), jnp.float32)],
+        name="attend",
+    )(band, arrived)
+    return exchange(result)
+
+
+def layer(
+    self_query, self_key, self_value, cross_query, context, key_weight, value_weight, band_width
+):
     devices = lax.axis_size("seq")
     device = lax.axis_index("seq")
     tok_rows, width = self_query.shape
@@ -358,7 +441,8 @@
     scale = 1.0 / math.sqrt(head_dim)
     vmem = pl.BlockSpec(memory_space=pltpu.VMEM)
     smem = pl.BlockSpec(memory_space=pltpu.SMEM)
-    seat = device % SEATS
+    seat, turn_seat = device % SEATS, device % SB
+    sources = (self_query, self_key, self_value)
 
     def block_array(*lead):
         return jax.ShapeDtypeStruct(lead + (tok_rows, head_dim), jnp.bfloat16)
@@ -369,102 +453,91 @@
         came = swap(text, devices // 2)
         text = jnp.concatenate([text, came], axis=0)
 
-    slot_ids = jnp.arange(SB * per_run, dtype=jnp.int32)
-    run, place = slot_ids // SB, slot_ids % SB
-    wanted = run * SB + jnp.where(run % 2 == 0, place, SB - 1 - place)
-    mine = jnp.where(jnp.arange(per_run) % 2 == 0, device % SB, SB - 1 - device % SB)
-    mine = mine + jnp.arange(per_run, dtype=jnp.int32) * SB
-    if narrow_run:
-        slot_ids = jnp.arange(SEATS * narrow_run, dtype=jnp.int32)
-        run, place = slot_ids % narrow_run, (slot_ids // narrow_run) ^ seat
-        near = SB * per_run + run * SEATS + jnp.where(run % 2 == 0, place, SEATS - 1 - place)
-        wanted = jnp.concatenate([wanted, near])
-        mine = jnp.concatenate([mine, near[:narrow_run]])
-    head_ids = jnp.arange(head_count, dtype=jnp.int32)
-    order = jnp.sum(jnp.where(wanted[:, None] == rank[None, :], head_ids + 1, 0), axis=1) - 1
-    bands = jnp.sum(jnp.where(mine[:, None] == rank[None, :], band_width + 1, 0), axis=1) - 1
-
-    packed = pl.pallas_call(
-        functools.partial(pack_kernel, head_dim=head_dim),
-        out_shape=[block_array(SB, 3)] * per_run
-        + [block_array(narrow_run, 3)] * (SEATS if narrow_run else 0),
-        in_specs=[smem] + [vmem] * 3,
-        out_specs=[vmem] * (per_run + (SEATS if narrow_run else 0)),
-        name="pack",
-    )(order, self_query, self_key, self_value)
-
-    returned = []
-    for index in range(per_run):
-        arrived = exchange(packed[index])
-        result = pl.pallas_call(
-            functools.partial(attend_kernel, scale=scale),
-            out_shape=block_array(SB),
-            in_specs=[smem, vmem],
-            out_specs=vmem,
-            scratch_shapes=[pltpu.VMEM((2 * tok_rows, SB * tok_rows), jnp.float32)],
-            name="attend",
-        )(bands[index : index + 1], arrived)
-        returned.append(exchange(result))
-    if narrow_run:
-        own = [packed[per_run]]
-        for turn in range(1, SEATS):
-            own.append(swap(packed[per_run + turn], turn))
-        pairs = jnp.stack([part[:, 1:] for part in own])
-        upward = [
-            (source, source + SEATS)
-            for source in range(devices - SEATS)
-            if source // SB == (source + SEATS) // SB
-        ]
-        low = lax.ppermute(pairs, "seq", upward)
-        high = lax.ppermute(pairs, "seq", [(high, low) for low, high in upward])
-        places = jnp.stack([seat, device % SB - seat]).astype(jnp.int32)
-        near = pl.pallas_call(
-            functools.partial(narrow_kernel, scale=scale),
-            out_shape=[block_array(narrow_run)] * SEATS,
-            in_specs=[smem] + [vmem] * (SEATS + 2),
-            out_specs=[vmem] * SEATS,
-            scratch_shapes=[
-                pltpu.VMEM((count * SEATS, tok_rows, head_dim), jnp.bfloat16)
-                for count in (1, 3, 3)
-            ],
-            name="narrow",
-        )(jnp.concatenate([places, bands[per_run:]]), *own, low, high)
-        returned.append(near[0])
-        for turn in range(1, SEATS):
-            returned.append(swap(near[turn], turn))
-    cross_out = cross_attention(
-        cross_query, context, key_weight, value_weight, head_dim, scale, text
-    )
-    self_out = pl.pallas_call(
-        functools.partial(unpack_kernel, head_dim=head_dim),
-        out_shape=jax.ShapeDtypeStruct((tok_rows, width), jnp.bfloat16),
-        in_specs=[smem] + [vmem] * len(returned),
-        out_specs=vmem,
-        name="unpack",
-    )(order, *returned)
-    return (self_out, cross_out)
-
-
-def layer(*arrays):
-    band_width = arrays[-1]
-    head_count = band_width.shape[0]
+    whole_run = head_count // SB
+    rest = head_count - whole_run * SB
+    narrow_run = (rest + SEATS - 1) // SEATS
     head_ids = jnp.arange(head_count, dtype=jnp.int32)
     ahead = (band_width[None, :] > band_width[:, None]) | (
         (band_width[None, :] == band_width[:, None]) & (head_ids[None, :] < head_ids[:, None])
     )
     rank = jnp.sum(ahead.astype(jnp.int32), axis=1)
-    whole_run = head_count // SB
-    narrow_count = head_count - whole_run * SB
-    narrow_run = (narrow_count + SEATS - 1) // SEATS
-    if not narrow_count or not whole_run:
-        return attention(rank, (head_count + SB - 1) // SB, 0, arrays)
-    close = jnp.sum((band_width <= REACH).astype(jnp.int32)) >= narrow_count
-    return lax.cond(
-        close,
-        functools.partial(attention, rank, whole_run, narrow_run),
-        functools.partial(attention, rank, whole_run + 1, 0),
-        arrays,
-    )
+    close = jnp.sum((band_width <= REACH).astype(jnp.int32)) >= rest
+    slot_ids = jnp.arange(SB * (whole_run + 1), dtype=jnp.int32)
+    run, place = slot_ids // SB, slot_ids % SB
+    wanted = run * SB + jnp.where(run % 2 == 0, place, SB - 1 - place)
+    runs = jnp.arange(whole_run + 1, dtype=jnp.int32)
+    mine = runs * SB + jnp.where(runs % 2 == 0, turn_seat, SB - 1 - turn_seat)
+    slot_ids = jnp.arange(SEATS * narrow_run, dtype=jnp.int32)
+    run, place = slot_ids % narrow_run, (slot_ids // narrow_run) ^ seat
+    near = SB * whole_run + run * SEATS + jnp.where(run % 2 == 0, place, SEATS - 1 - place)
+    wanted = jnp.concatenate([wanted, near])
+    mine = jnp.concatenate([mine, near[:narrow_run]])
+    order = jnp.sum(jnp.where(wanted[:, None] == rank[None, :], head_ids + 1, 0), axis=1) - 1
+    bands = jnp.sum(jnp.where(mine[:, None] == rank[None, :], band_width + 1, 0), axis=1) - 1
+    wide_slots, last_slots = SB * whole_run, SB * (whole_run + 1)
+
+    shapes = [block_array(SB, 3)] * whole_run + [block_array(narrow_run, 3)] * SEATS
+    packed = pack(
+        jnp.concatenate([order[:wide_slots], order[last_slots:]]), sources, shapes, head_dim
+    )
+    returned = [
+        run_slot(packed[index], bands[index : index + 1], scale)
+        for index in range(whole_run)
+    ]
+    own = [packed[whole_run]]
+    for turn in range(1, SEATS):
+        own.append(swap(packed[whole_run + turn], turn))
+    pairs = jnp.stack([part[:, 1:] for part in own])
+    upward = [
+        (source, source + SEATS)
+        for source in range(devices - SEATS)
+        if source // SB == (source + SEATS) // SB
+    ]
+    low = lax.ppermute(pairs, "seq", upward)
+    high = lax.ppermute(pairs, "seq", [(high, low) for low, high in upward])
+    places = jnp.stack([seat, turn_seat - seat]).astype(jnp.int32)
+    near_out = pl.pallas_call(
+        functools.partial(narrow_kernel, scale=scale),
+        out_shape=[block_array(narrow_run)] * SEATS,
+        in_specs=[smem] + [vmem] * (SEATS + 2),
+        out_specs=[vmem] * SEATS,
+        scratch_shapes=[
+            pltpu.VMEM((count * SEATS, tok_rows, head_dim), jnp.bfloat16)
+            for count in (1, 3, 3)
+        ],
+        name="narrow",
+    )(jnp.concatenate([places, bands[whole_run + 1 :]]), *own, low, high)
+    nears = [near_out[0]]
+    for turn in range(1, SEATS):
+        nears.append(swap(near_out[turn], turn))
+    cross_out = cross_attention(
+        cross_query, context, key_weight, value_weight, head_dim, scale, text
+    )
+
+    def unpack(order, parts):
+        return pl.pallas_call(
+            functools.partial(unpack_kernel, head_dim=head_dim),
+            out_shape=jax.ShapeDtypeStruct((tok_rows, width), jnp.bfloat16),
+            in_specs=[smem] + [vmem] * len(parts),
+            out_specs=vmem,
+            name="unpack",
+        )(order, *parts)
+
+    wide_order, rest_order = order[:wide_slots], order[wide_slots:last_slots]
+    near_order = order[last_slots:]
+
+    def short(operands):
+        parts, nears, _ = operands
+        return unpack(jnp.concatenate([wide_order, near_order]), [*parts, *nears])
+
+    def full(operands):
+        parts, _, sources = operands
+        (outgoing,) = pack(rest_order, sources, [block_array(SB, 3)], head_dim)
+        last = run_slot(outgoing, bands[whole_run : whole_run + 1], scale)
+        return unpack(jnp.concatenate([wide_order, rest_order]), [*parts, last])
+
+    self_out = lax.cond(close, short, full, (returned, nears, sources))
+    return (self_out, cross_out)
 
 
 def solution(mesh):

time: 233 us -> 207 us (0.89)
  waiting for transfers between devices: 111 us -> 61.3 us
  blocking collectives: 0 us -> 42.7 us
  starting transfers between devices: 52.8 us -> 33.7 us
    ppermute x10 -> x11, waiting for transfers between devices: 94.8 us -> 50 us  [swap(): lax.ppermute(values, 'seq', [(source, source ^ distance) for source in ra...]
    all_to_all x0 -> x1, blocking collectives: none -> 42.7 us  [exchange(): lax.all_to_all(values, 'seq', split_axis=0, concat_axis=0, tiled=True, ax...]
    all_to_all x4 -> x3, starting transfers between devices: 28.4 us -> 16.3 us  [exchange(): lax.all_to_all(values, 'seq', split_axis=0, concat_axis=0, tiled=True, ax...]
    ppermute x10 -> x11, starting transfers between devices: 19 us -> 11.9 us  [swap(): lax.ppermute(values, 'seq', [(source, source ^ distance) for source in ra...]
    ppermute x2, waiting for transfers between devices: 15.9 us -> 11.4 us  [the longest x1 8.55 us: layer(): low = lax.ppermute(pairs, 'seq', upward)]
    unnamed x0 -> x30, local copies, waits for them, and re-layouts: none -> 3.59 us
    pallas_call x5 -> x7, Pallas kernels: 36.5 us -> 40 us  [the longest x2 21.5 us: run_slot(): pl.pallas_call(functools.partial(attend_kernel, scale=scale), out_shape=j...]
    pallas_call x1, Pallas kernels: 10.4 us -> 7.42 us  [cross_attention(): pl.pallas_call(functools.partial(cross_pairs_kernel, head_dim=head_dim, s...]
  transfers between devices with their start and end apart: 16 -> 16, of which waited for: 7 -> 4; matrix products, arithmetic and copies ran while one was open for 4% -> 3% of each run, Pallas kernels for 16% -> 23%
where the time goes in v2:
time: 207 us; the launch traced here: 204 us
  waiting for transfers between devices  61.3 us (30%)
  Pallas kernels  53.2 us (26%)
  blocking collectives  42.7 us (21%)
  starting transfers between devices  33.7 us (16%)
  other arithmetic  7.15 us (3%)
  local copies, waits for them, and re-layouts  4.43 us (2%)
    ppermute x11, waiting for transfers between devices, swap(): lax.ppermute(values, 'seq', [(source, source ^ distance) for source in ra...  50 us
    all_to_all x1, blocking collectives, exchange(): lax.all_to_all(values, 'seq', split_axis=0, concat_axis=0, tiled=True, ax...  42.7 us
    pallas_call x2, Pallas kernels, run_slot(): pl.pallas_call(functools.partial(attend_kernel, scale=scale), out_shape=j...  21.5 us
    all_to_all x3, starting transfers between devices, exchange(): lax.all_to_all(values, 'seq', split_axis=0, concat_axis=0, tiled=True, ax...  16.3 us
    ppermute x11, starting transfers between devices, swap(): lax.ppermute(values, 'seq', [(source, source ^ distance) for source in ra...  11.9 us
    ppermute x1, waiting for transfers between devices, layer(): low = lax.ppermute(pairs, 'seq', upward)  8.55 us
    pallas_call x1, Pallas kernels, cross_attention(): pl.pallas_call(functools.partial(cross_pairs_kernel, head_dim=head_dim, s...  7.42 us
    pallas_call x1, Pallas kernels, layer(): pl.pallas_call(functools.partial(narrow_kernel, scale=scale), out_shape=[...  6.59 us
  transfers between devices with their start and end apart: 16, of which 4 were waited for; matrix products, arithmetic and copies ran while one was open for 3% of the time, Pallas kernels for 23%

profile of v2, /device:TPU:13, one launch (start us, length us, event | category | flops | bytes accessed | tf_op | source)
XLA Modules:
  0.0 204.1 jit_solution(16713967477585470062)
XLA Ops:
  2.4 5.3 %pack.3 = (bf16[16,3,128,128]{3,2,1,0:T(8,128)(2,1)}, bf16[16,3,128,128]{3,2,1,0:T(8,128)(2,1)}, bf16[2,3,128,128]{3,2,1,0:T(8,128)(2,1)}, bf16[2,3,128,128]{3,2...) custom-call(s32[40]{0:T(128)} %pad_add_fusion.4.order_ref, ...), custom_call_target="tpu_custom_call" | custom-call | tf_op jit(solution)/shard_map/pack/pallas_call | solution.py:409
  7.7 42.7 %all_to_all.28.data_ref = bf16[16,3,128,128]{3,2,1,0:T(8,128)(2,1)} all-to-all(bf16[16,3,128,128]{3,2,1,0:T(8,128)(2,1)} %get-tuple-element.66), channel_id=1, replica_groups={{0,1,2,3,4,5,6,7,8,9,10,11,12,13,14,15},{16,17,18,19,20,21,22,23,24,25,..., dimensions={0} | all-to-all | bytes 3145728 | tf_op jit(solution)/shard_map/all_to_all | solution.py:397
  50.4 4.9 %all-to-all-start.4 = ((bf16[16,3,128,128]{3,2,1,0:T(8,128)(2,1)}), bf16[16,3,128,128]{3,2,1,0:T(8,128)(2,1)S(1)}, u32[]{:S(2)}, u32[]{:S(2)}) async-start(bf16[16,3,128,128]{3,2,1,0:T(8,128)(2,1)} %get-tuple-element.67), calls=%async_computation.4 | async-start | bytes 3145728 | tf_op jit(solution)/shard_map/all_to_all | solution.py:397
  55.4 5.8 %project.1 = bf16[1,256,640]{2,1,0:T(8,128)(2,1)} custom-call(bf16[256,4096]{1,0:T(8,128)(2,1)} %context_ref.1, bf16[320,4096]{1,0:T(8,128)(2,1)} %bitcast.17, bf16[320,4096]{1,0:T(8,128)(2,1)} %bitcast.18), custom_call_target="tpu_custom_call" | custom-call | tf_op jit(solution)/shard_map/project/pallas_call | solution.py:224
  61.2 2.1 %collective-permute-start.9 = (bf16[1,256,640]{2,1,0:T(8,128)(2,1)}, bf16[1,256,640]{2,1,0:T(8,128)(2,1)S(1)}, u32[]{:S(2)}, u32[]{:S(2)}) collective-permute-start(bf16[1,256,640]{2,1,0:T(8,128)(2,1)} %project.1), channel_id=1, source_target_pairs={{0,8},{1,9},{2,10},{3,11},{4,12},{5,13},{6,14},{7,15},{8,0},{9,1},... | collective-permute-start | bytes 983048 | tf_op jit(solution)/shard_map/ppermute | solution.py:331
  63.3 40.1 %collective-permute-done.9 = bf16[1,256,640]{2,1,0:T(8,128)(2,1)S(1)} collective-permute-done((bf16[1,256,640]{2,1,0:T(8,128)(2,1)}, bf16[1,256,640]{2,1,0:T(8,128)(2,1)S(1)}, u32[]{:S(2)}, u32[]{:S(2)}) %collective-permute-start.9) | collective-permute-done | bytes 327712 | tf_op jit(solution)/shard_map/ppermute | solution.py:331
  104.6 3.2 %collective-permute-start.10 = (bf16[2,256,640]{2,1,0:T(8,128)(2,1)S(1)}, bf16[2,256,640]{2,1,0:T(8,128)(2,1)}, u32[]{:S(2)}, u32[]{:S(2)}) collective-permute-start(bf16[2,256,640]{2,1,0:T(8,128)(2,1)S(1)} %pad_maximum_fusion.1), channel_id=1, source_target_pairs={{0,4},{1,5},{2,6},{3,7},{4,0},{5,1},{6,2},{7,3},{8,12},{9,13},{10,... | collective-permute-start | bytes 1966088 | tf_op jit(solution)/shard_map/ppermute | solution.py:331
  109.3 11.6 %attend.4 = bf16[16,128,128]{2,1,0:T(8,128)(2,1)} custom-call(s32[1]{0:T(128)} %get-tuple-element.79.band_ref, bf16[16,3,128,128]{3,2,1,0:T(8,128)(2,1)} %all_to_all.28.data_ref), custom_call_target="tpu_custom_call" | custom-call | tf_op jit(solution)/shard_map/attend/pallas_call | solution.py:422
  120.9 5.1 %all-to-all-start.3 = ((bf16[16,128,128]{2,1,0:T(8,128)(2,1)}), bf16[16,128,128]{2,1,0:T(8,128)(2,1)S(1)}, u32[]{:S(2)}, u32[]{:S(2)}) async-start(bf16[16,128,128]{2,1,0:T(8,128)(2,1)} %attend.4), calls=%async_computation.3 | async-start | bytes 1048576 | tf_op jit(solution)/shard_map/all_to_all | solution.py:397
  128.3 1.7 collective-permute-start.2
  130.7 2.2 %split.1 = bf16[4,128,640]{2,1,0:T(8,128)(2,1)} custom-call(s32[3]{0:T(128)} %pad_add_fusion.6.place_ref, bf16[128,5120]{1,0:T(8,128)(2,1)} %query_ref.5), custom_call_target="tpu_custom_call" | custom-call | tf_op jit(solution)/shard_map/split/pallas_call | solution.py:363
  133.2 9.9 %collective-permute-done.2.refs_3_ = bf16[2,3,128,128]{3,2,1,0:T(8,128)(2,1)S(1)} collective-permute-done((bf16[2,3,128,128]{3,2,1,0:T(8,128)(2,1)}, bf16[2,3,128,128]{3,2,1,0:T(8,128)(2,1)S(1)}, u32[]{:S(2)}, u32[]{:S(2)}) %collective-permute-start.2) | collective-permute-done | bytes 196640 | tf_op jit(solution)/shard_map/ppermute | solution.py:331
  143.1 9.9 %attend.5 = bf16[16,128,128]{2,1,0:T(8,128)(2,1)} custom-call(s32[1]{0:T(128)} %get-tuple-element.78.band_ref, bf16[16,3,128,128]{3,2,1,0:T(8,128)(2,1)} %copy-done), custom_call_target="tpu_custom_call" | custom-call | tf_op jit(solution)/shard_map/attend/pallas_call | solution.py:422
  153.0 6.3 %all-to-all-start.5 = ((bf16[16,128,128]{2,1,0:T(8,128)(2,1)}), bf16[16,128,128]{2,1,0:T(8,128)(2,1)}, u32[]{:S(2)}, u32[]{:S(2)}) async-start(bf16[16,128,128]{2,1,0:T(8,128)(2,1)} %attend.5), calls=%async_computation.5 | async-start | bytes 1048576 | tf_op jit(solution)/shard_map/all_to_all | solution.py:397
  160.3 7.4 %cross.1 = (bf16[4,128,640]{2,1,0:T(8,128)(2,1)}, bf16[4,128,640]{2,1,0:T(8,128)(2,1)}) custom-call(s32[3]{0:T(128)} %pad_add_fusion.6.place_ref, bf16[128,5120]{1,0:T(8,128)(2,1)} %query_ref.5, bf16[4,128,640]{2,1,0:T(8,128)(2,1)} %copy-done.8, bf16[4,256,640]{2,1,0:T(8,128)(2,1)} %copy-done.2, bf16[4,256,640]{2,1,0:T(8,128)(2,1)} %collective-permute-done.11.other_ref), custom_call_target="tpu_custom_call" | custom-call | tf_op jit(solution)/shard_map/cross/pallas_call | solution.py:377
  168.1 3.1 %collective-permute-start.3 = (bf16[4,2,2,128,128]{4,3,2,1,0:T(8,128)(2,1)S(1)}, bf16[4,2,2,128,128]{4,3,2,1,0:T(8,128)(2,1)S(1)}, u32[]{:S(2)}, u32[]{:S(2)}) collective-permute-start(bf16[4,2,2,128,128]{4,3,2,1,0:T(8,128)(2,1)S(1)} %pad_maximum_fusion.2), channel_id=1, source_target_pairs={{0,4},{1,5},{2,6},{3,7},{4,8},{5,9},{6,10},{7,11},{8,12},{9,13},{1... | collective-permute-start | bytes 1572872 | tf_op jit(solution)/shard_map/ppermute | solution.py:496
  171.2 2.4 %collective-permute-start.4 = (bf16[4,2,2,128,128]{4,3,2,1,0:T(8,128)(2,1)S(1)}, bf16[4,2,2,128,128]{4,3,2,1,0:T(8,128)(2,1)S(1)}, u32[]{:S(2)}, u32[]{:S(2)}) collective-permute-start(bf16[4,2,2,128,128]{4,3,2,1,0:T(8,128)(2,1)S(1)} %pad_maximum_fusion.2), channel_id=1, source_target_pairs={{4,0},{5,1},{6,2},{7,3},{8,4},{9,5},{10,6},{11,7},{12,8},{13,9},{1... | collective-permute-start | bytes 1572872 | tf_op jit(solution)/shard_map/ppermute | solution.py:497
  174.3 8.5 %collective-permute-done.3.refs_4_ = bf16[4,2,2,128,128]{4,3,2,1,0:T(8,128)(2,1)S(1)} collective-permute-done((bf16[4,2,2,128,128]{4,3,2,1,0:T(8,128)(2,1)S(1)}, bf16[4,2,2,128,128]{4,3,2,1,0:T(8,128)(2,1)S(1)}, u32[]{:S(2)}, u32[]{:S(2)}) %collective-permute-start.3) | collective-permute-done | bytes 524320 | tf_op jit(solution)/shard_map/ppermute | solution.py:496
  182.8 2.8 %collective-permute-done.4.refs_5_ = bf16[4,2,2,128,128]{4,3,2,1,0:T(8,128)(2,1)S(1)} collective-permute-done((bf16[4,2,2,128,128]{4,3,2,1,0:T(8,128)(2,1)S(1)}, bf16[4,2,2,128,128]{4,3,2,1,0:T(8,128)(2,1)S(1)}, u32[]{:S(2)}, u32[]{:S(2)}) %collective-permute-start.4) | collective-permute-done | bytes 524320 | tf_op jit(solution)/shard_map/ppermute | solution.py:497
  186.4 6.6 %narrow.1 = (bf16[2,128,128]{2,1,0:T(8,128)(2,1)S(1)}, bf16[2,128,128]{2,1,0:T(8,128)(2,1)}, bf16[2,128,128]{2,1,0:T(8,128)(2,1)}, bf16[2,128,128]{2,1,0:T(8,128)(2,1)}) custom-call(s32[4]{0:T(128)} %pad_add_fusion.5.place_ref, bf16[2,3,128,128]{3,2,1,0:T(8,128)(2,1)} %get-tuple-element.68.refs_0_, bf16[2,3,128,128]{3,2,1,0:T(8,128)(2,1)} %copy-done.11, ...), custom_call_target="tpu_custom_call" | custom-call | tf_op jit(solution)/shard_map/narrow/pallas_call | solution.py:499
  193.0 1.8 collective-permute-start.5
  198.0 2.6 %merge.1 = bf16[128,5120]{1,0:T(8,128)(2,1)} custom-call(s32[3]{0:T(128)} %pad_add_fusion.6.place_ref, bf16[4,128,640]{2,1,0:T(8,128)(2,1)} %get-tuple-element.76.own_ref, bf16[4,128,640]{2,1,0:T(8,128)(2,1)} %copy-done.9), custom_call_target="tpu_custom_call" | custom-call | tf_op jit(solution)/shard_map/merge/pallas_call | solution.py:386
  200.7 2.4 %conditional.1 = (bf16[128,5120]{1,0:T(8,128)(2,1)S(1)}) conditional(s32[]{:T(128)} %convert_element_type.10, (s32[56]{0:T(128)S(1)}, s32[32]{0:T(128)S(1)}, s32[5]{0:T(128)S(1)}, bf16[128,5120]{1,0:T(8,128)(2,1)S(1)}, bf16[128,5120]{1,0:T(8,128)(2,1)S(1)}, /*index=5*/bf16[128,5120]{1,0:T(8,128)(2,1)}, bf16[16,128,128]{2,1,0:T(8,128)(2,1)S(1)}, ...), branch_computations={%region_4.5_spmd, %region_5.6_spmd} | conditional | flops 48 | bytes 14680996 | solution.py:539
  201.3 1.7 unpack.3
  (75 shorter events, 14.7 us)
Async XLA Ops:
  50.4 70.5 %all-to-all-start.4 = ((bf16[16,3,128,128]{3,2,1,0:T(8,128)(2,1)}), bf16[16,3,128,128]{3,2,1,0:T(8,128)(2,1)S(1)}, u32[]{:S(2)}, u32[]{:S(2)}) async-start(bf16[16,3,128,128]{3,2,1,0:T(8,128)(2,1)} %get-tuple-element.67), calls=%async_computation.4 | async-start | bytes 3145728 | tf_op jit(solution)/shard_map/all_to_all | solution.py:397
  61.2 46.6 %copy-start.17 = (s32[40]{0:T(128)S(1)}, s32[40]{0:T(128)}, u32[]{:S(2)}) copy-start(s32[40]{0:T(128)} %param.17) | copy-start | bytes 484
  61.2 42.2 %collective-permute-start.9 = (bf16[1,256,640]{2,1,0:T(8,128)(2,1)}, bf16[1,256,640]{2,1,0:T(8,128)(2,1)S(1)}, u32[]{:S(2)}, u32[]{:S(2)}) collective-permute-start(bf16[1,256,640]{2,1,0:T(8,128)(2,1)} %project.1), channel_id=1, source_target_pairs={{0,8},{1,9},{2,10},{3,11},{4,12},{5,13},{6,14},{7,15},{8,0},{9,1},... | collective-permute-start | bytes 983048 | tf_op jit(solution)/shard_map/ppermute | solution.py:331
  103.4 17.5 %copy-start.6 = (bf16[1,256,640]{2,1,0:T(8,128)(2,1)}, bf16[1,256,640]{2,1,0:T(8,128)(2,1)S(1)}, u32[]{:S(2)}) copy-start(bf16[1,256,640]{2,1,0:T(8,128)(2,1)S(1)} %collective-permute-done.9) | copy-start | bytes 983044
  104.6 21.4 %collective-permute-start.10 = (bf16[2,256,640]{2,1,0:T(8,128)(2,1)S(1)}, bf16[2,256,640]{2,1,0:T(8,128)(2,1)}, u32[]{:S(2)}, u32[]{:S(2)}) collective-permute-start(bf16[2,256,640]{2,1,0:T(8,128)(2,1)S(1)} %pad_maximum_fusion.1), channel_id=1, source_target_pairs={{0,4},{1,5},{2,6},{3,7},{4,0},{5,1},{6,2},{7,3},{8,12},{9,13},{10,... | collective-permute-start | bytes 1966088 | tf_op jit(solution)/shard_map/ppermute | solution.py:331
  120.9 6.5 %copy-start = (bf16[16,3,128,128]{3,2,1,0:T(8,128)(2,1)}, bf16[16,3,128,128]{3,2,1,0:T(8,128)(2,1)S(1)}, u32[]{:S(2)}) copy-start(bf16[16,3,128,128]{3,2,1,0:T(8,128)(2,1)S(1)} %all-to-all-done.4.data_ref) | copy-start | bytes 4718596
  120.9 32.1 %all-to-all-start.3 = ((bf16[16,128,128]{2,1,0:T(8,128)(2,1)}), bf16[16,128,128]{2,1,0:T(8,128)(2,1)S(1)}, u32[]{:S(2)}, u32[]{:S(2)}) async-start(bf16[16,128,128]{2,1,0:T(8,128)(2,1)} %attend.4), calls=%async_computation.3 | async-start | bytes 1048576 | tf_op jit(solution)/shard_map/all_to_all | solution.py:397
  127.4 25.6 %copy-start.2 = (bf16[4,256,640]{2,1,0:T(8,128)(2,1)}, bf16[4,256,640]{2,1,0:T(8,128)(2,1)S(1)}, u32[]{:S(2)}) copy-start(bf16[4,256,640]{2,1,0:T(8,128)(2,1)S(1)} %pad_maximum_fusion.mine_ref) | copy-start | bytes 3932164
  127.4 32.0 %collective-permute-start.11 = (bf16[4,256,640]{2,1,0:T(8,128)(2,1)S(1)}, bf16[4,256,640]{2,1,0:T(8,128)(2,1)}, u32[]{:S(2)}, u32[]{:S(2)}) collective-permute-start(bf16[4,256,640]{2,1,0:T(8,128)(2,1)S(1)} %pad_maximum_fusion.mine_ref), channel_id=1, source_target_pairs={{0,1},{1,0},{2,3},{3,2},{4,5},{5,4},{6,7},{7,6},{8,9},{9,8},{10,11... | collective-permute-start | bytes 3932168 | tf_op jit(solution)/shard_map/ppermute | solution.py:331
  127.9 5.3 %copy-start.10 = (bf16[2,3,128,128]{3,2,1,0:T(8,128)(2,1)S(1)}, bf16[2,3,128,128]{3,2,1,0:T(8,128)(2,1)}, u32[]{:S(2)}) copy-start(bf16[2,3,128,128]{3,2,1,0:T(8,128)(2,1)} %get-tuple-element.68.refs_0_) | copy-start | bytes 589828
  127.9 31.5 %collective-permute-start = (bf16[2,3,128,128]{3,2,1,0:T(8,128)(2,1)}, bf16[2,3,128,128]{3,2,1,0:T(8,128)(2,1)S(1)}, u32[]{:S(2)}, u32[]{:S(2)}) collective-permute-start(bf16[2,3,128,128]{3,2,1,0:T(8,128)(2,1)} %get-tuple-element.69), channel_id=1, source_target_pairs={{0,1},{1,0},{2,3},{3,2},{4,5},{5,4},{6,7},{7,6},{8,9},{9,8},{10,11... | collective-permute-start | bytes 589832 | tf_op jit(solution)/shard_map/ppermute | solution.py:331
  128.0 31.3 %collective-permute-start.1 = (bf16[2,3,128,128]{3,2,1,0:T(8,128)(2,1)}, bf16[2,3,128,128]{3,2,1,0:T(8,128)(2,1)S(1)}, u32[]{:S(2)}, u32[]{:S(2)}) collective-permute-start(bf16[2,3,128,128]{3,2,1,0:T(8,128)(2,1)} %get-tuple-element.70), channel_id=1, source_target_pairs={{0,2},{1,3},{2,0},{3,1},{4,6},{5,7},{6,4},{7,5},{8,10},{9,11},{10,... | collective-permute-start | bytes 589832 | tf_op jit(solution)/shard_map/ppermute | solution.py:331
  128.3 14.8 %collective-permute-start.2 = (bf16[2,3,128,128]{3,2,1,0:T(8,128)(2,1)}, bf16[2,3,128,128]{3,2,1,0:T(8,128)(2,1)S(1)}, u32[]{:S(2)}, u32[]{:S(2)}) collective-permute-start(bf16[2,3,128,128]{3,2,1,0:T(8,128)(2,1)} %get-tuple-element.71), channel_id=1, source_target_pairs={{0,3},{1,2},{2,1},{3,0},{4,7},{5,6},{6,5},{7,4},{8,11},{9,10},{10,... | collective-permute-start | bytes 589832 | tf_op jit(solution)/shard_map/ppermute | solution.py:331
  132.9 26.5 %collective-permute-start.8 = (bf16[4,128,640]{2,1,0:T(8,128)(2,1)}, bf16[4,128,640]{2,1,0:T(8,128)(2,1)S(1)}, u32[]{:S(2)}, u32[]{:S(2)}) collective-permute-start(bf16[4,128,640]{2,1,0:T(8,128)(2,1)} %split.1), channel_id=1, source_target_pairs={{0,2},{1,3},{2,0},{3,1},{4,6},{5,7},{6,4},{7,5},{8,10},{9,11},{10,... | collective-permute-start | bytes 1966088 | tf_op jit(solution)/shard_map/ppermute | solution.py:331
  143.1 9.9 %copy-start.13 = (bf16[2,3,128,128]{3,2,1,0:T(8,128)(2,1)}, bf16[2,3,128,128]{3,2,1,0:T(8,128)(2,1)S(1)}, u32[]{:S(2)}) copy-start(bf16[2,3,128,128]{3,2,1,0:T(8,128)(2,1)S(1)} %collective-permute-done.2.refs_3_) | copy-start | bytes 589828
  153.0 47.6 %all-to-all-start.5 = ((bf16[16,128,128]{2,1,0:T(8,128)(2,1)}), bf16[16,128,128]{2,1,0:T(8,128)(2,1)}, u32[]{:S(2)}, u32[]{:S(2)}) async-start(bf16[16,128,128]{2,1,0:T(8,128)(2,1)} %attend.5), calls=%async_computation.5 | async-start | bytes 1048576 | tf_op jit(solution)/shard_map/all_to_all | solution.py:397
  159.3 8.4 %copy-start.12 = (bf16[2,3,128,128]{3,2,1,0:T(8,128)(2,1)}, bf16[2,3,128,128]{3,2,1,0:T(8,128)(2,1)S(1)}, u32[]{:S(2)}) copy-start(bf16[2,3,128,128]{3,2,1,0:T(8,128)(2,1)S(1)} %collective-permute-done.1.refs_2_) | copy-start | bytes 589828
  159.4 8.3 %copy-start.11 = (bf16[2,3,128,128]{3,2,1,0:T(8,128)(2,1)}, bf16[2,3,128,128]{3,2,1,0:T(8,128)(2,1)S(1)}, u32[]{:S(2)}) copy-start(bf16[2,3,128,128]{3,2,1,0:T(8,128)(2,1)S(1)} %collective-permute-done.refs_1_) | copy-start | bytes 589828
  167.7 29.5 %collective-permute-start.12 = (bf16[4,128,640]{2,1,0:T(8,128)(2,1)}, bf16[4,128,640]{2,1,0:T(8,128)(2,1)S(1)}, u32[]{:S(2)}, u32[]{:S(2)}) collective-permute-start(bf16[4,128,640]{2,1,0:T(8,128)(2,1)} %get-tuple-element.77), channel_id=1, source_target_pairs={{0,2},{1,3},{2,0},{3,1},{4,6},{5,7},{6,4},{7,5},{8,10},{9,11},{10,... | collective-permute-start | bytes 1966088 | tf_op jit(solution)/shard_map/ppermute | solution.py:331
  168.1 14.7 %collective-permute-start.3 = (bf16[4,2,2,128,128]{4,3,2,1,0:T(8,128)(2,1)S(1)}, bf16[4,2,2,128,128]{4,3,2,1,0:T(8,128)(2,1)S(1)}, u32[]{:S(2)}, u32[]{:S(2)}) collective-permute-start(bf16[4,2,2,128,128]{4,3,2,1,0:T(8,128)(2,1)S(1)} %pad_maximum_fusion.2), channel_id=1, source_target_pairs={{0,4},{1,5},{2,6},{3,7},{4,8},{5,9},{6,10},{7,11},{8,12},{9,13},{1... | collective-permute-start | bytes 1572872 | tf_op jit(solution)/shard_map/ppermute | solution.py:496
  171.2 14.4 %collective-permute-start.4 = (bf16[4,2,2,128,128]{4,3,2,1,0:T(8,128)(2,1)S(1)}, bf16[4,2,2,128,128]{4,3,2,1,0:T(8,128)(2,1)S(1)}, u32[]{:S(2)}, u32[]{:S(2)}) collective-permute-start(bf16[4,2,2,128,128]{4,3,2,1,0:T(8,128)(2,1)S(1)} %pad_maximum_fusion.2), channel_id=1, source_target_pairs={{4,0},{5,1},{6,2},{7,3},{8,4},{9,5},{10,6},{11,7},{12,8},{13,9},{1... | collective-permute-start | bytes 1572872 | tf_op jit(solution)/shard_map/ppermute | solution.py:497
  193.0 7.6 %collective-permute-start.5 = (bf16[2,128,128]{2,1,0:T(8,128)(2,1)}, bf16[2,128,128]{2,1,0:T(8,128)(2,1)S(1)}, u32[]{:S(2)}, u32[]{:S(2)}) collective-permute-start(bf16[2,128,128]{2,1,0:T(8,128)(2,1)} %get-tuple-element.73), channel_id=1, source_target_pairs={{0,1},{1,0},{2,3},{3,2},{4,5},{5,4},{6,7},{7,6},{8,9},{9,8},{10,11... | collective-permute-start | bytes 196616 | tf_op jit(solution)/shard_map/ppermute | solution.py:331
  194.8 5.8 %collective-permute-start.6 = (bf16[2,128,128]{2,1,0:T(8,128)(2,1)}, bf16[2,128,128]{2,1,0:T(8,128)(2,1)S(1)}, u32[]{:S(2)}, u32[]{:S(2)}) collective-permute-start(bf16[2,128,128]{2,1,0:T(8,128)(2,1)} %get-tuple-element.74), channel_id=1, source_target_pairs={{0,2},{1,3},{2,0},{3,1},{4,6},{5,7},{6,4},{7,5},{8,10},{9,11},{10,... | collective-permute-start | bytes 196616 | tf_op jit(solution)/shard_map/ppermute | solution.py:331
  196.0 4.6 %collective-permute-start.7 = (bf16[2,128,128]{2,1,0:T(8,128)(2,1)}, bf16[2,128,128]{2,1,0:T(8,128)(2,1)S(1)}, u32[]{:S(2)}, u32[]{:S(2)}) collective-permute-start(bf16[2,128,128]{2,1,0:T(8,128)(2,1)} %get-tuple-element.75), channel_id=1, source_target_pairs={{0,3},{1,2},{2,1},{3,0},{4,7},{5,6},{6,5},{7,4},{8,11},{9,10},{10,... | collective-permute-start | bytes 196616 | tf_op jit(solution)/shard_map/ppermute | solution.py:331
  (7 other events, 11.7 us)

commit v3 on v2

--- a/solution.py
+++ b/solution.py
@@ -12,6 +12,7 @@
 SB = 16
 SEATS = 4
 REACH = 4
+ROOM = pltpu.CompilerParams(vmem_limit_bytes=24 << 20)
 LOG2_E = 1.4426950408889634
 
 
@@ -33,23 +34,27 @@
 
 
 def unpack_kernel(order_ref, *refs, head_dim):
-    out_ref = refs[-1]
+    out_ref, done = refs[-2:]
     first = 0
-    for returned_ref in refs[:-1]:
-        seats = returned_ref.shape[0]
-
-        def fill(seat, carry, returned_ref=returned_ref, first=first):
-            head = order_ref[first + seat]
-
-            @pl.when(head >= 0)
-            def _():
-                columns = pl.ds(pl.multiple_of(head * head_dim, head_dim), head_dim)
-                out_ref[:, columns] = returned_ref[seat]
-
-            return carry
-
-        lax.fori_loop(0, seats, fill, 0)
-        first += seats
+    for returned_ref in refs[:-2]:
+        seats, runs = returned_ref.shape[:2]
+        for run in range(runs):
+
+            def fill(seat, carry, returned_ref=returned_ref, first=first, run=run):
+                head = order_ref[first + seat]
+
+                @pl.when(head >= 0)
+                def _():
+                    columns = pl.ds(pl.multiple_of(head * head_dim, head_dim), head_dim)
+                    pltpu.make_async_copy(
+                        returned_ref.at[seat, run], out_ref.at[:, columns], done
+                    ).start()
+
+                return carry
+
+            lax.fori_loop(0, seats, fill, 0)
+            first += seats
+    pltpu.make_async_copy(out_ref, out_ref, done).wait()
 
 
 def attend_tile(tile, width, band, data_ref, out_ref, score_ref, scale):
@@ -89,12 +94,16 @@
         total = partial if total is None else total + partial
         running = product if running is None else running + product
     total = jnp.sum(total, axis=1, keepdims=True)
-    out_ref[pl.ds(2 * tile, 2)] = (
+    out_ref[pl.ds(2 * tile, 2), 0] = (
         (running / total).astype(jnp.bfloat16).reshape(2, rows, head_dim)
     )
 
 
-def attend_kernel(band_ref, data_ref, out_ref, score_ref, *, scale):
+def attend_kernel(band_ref, source_ref, *refs, scale):
+    out_ref, score_ref, data_ref, done = refs[-4:]
+    load = pltpu.make_async_copy(source_ref, data_ref, done)
+    load.start()
+    load.wait()
     stripe_len = data_ref.shape[0]
     band = band_ref[0]
 
@@ -143,6 +152,11 @@
     lax.fori_loop(0, query_ref.shape[1] // head_dim // group, step, 0)
 
 
+def pairs_kernel(*refs):
+    for turn, own_ref in enumerate(refs[:-1]):
+        refs[-1][turn] = own_ref[:, 1:]
+
+
 def narrow_kernel(place_ref, *refs, scale):
     own_refs, (low_ref, high_ref) = refs[:SEATS], refs[SEATS : SEATS + 2]
     out_refs, (query_ref, key_ref, value_ref) = refs[SEATS + 2 : -3], refs[-3:]
@@ -216,7 +230,7 @@
         out_ref[0] = total_ref[...].astype(jnp.bfloat16)
 
 
-def project(context, key_weight, value_weight, steps=4):
+def project(context, key_weight, value_weight, steps=2):
     text_len, depth = context.shape
     columns = key_weight.shape[1]
     part = depth // steps
@@ -352,6 +366,7 @@
             in_specs=[vmem, vmem, vmem],
             out_specs=vmem,
             name="cross",
+            compiler_params=ROOM,
         )(
             cross_query,
             lax.all_gather(text_key.astype(jnp.bfloat16), "seq", axis=1, tiled=True),
@@ -366,6 +381,7 @@
         in_specs=[smem, vmem],
         out_specs=vmem,
         name="split",
+        compiler_params=ROOM,
     )(place, cross_query)
     guests = swap(leaving, 2)
     distance = devices // 4
@@ -381,6 +397,7 @@
         out_specs=[vmem] * 2,
         scratch_shapes=[pltpu.VMEM(pair_shape, jnp.bfloat16)] * 2,
         name="cross",
+        compiler_params=ROOM,
     )(place, cross_query, guests, text, other)
     back = swap(sent, 2)
     return pl.pallas_call(
@@ -389,6 +406,7 @@
         in_specs=[smem, vmem, vmem],
         out_specs=vmem,
         name="merge",
+        compiler_params=ROOM,
     )(place, own, back)
 
 
@@ -415,18 +433,35 @@
     )(order, *sources)
 
 
-def run_slot(outgoing, band, scale):
-    stripe_len, _, tok_rows, head_dim = outgoing.shape
-    vmem = pl.BlockSpec(memory_space=pltpu.VMEM)
-    arrived = exchange(outgoing)
-    result = pl.pallas_call(
-        functools.partial(attend_kernel, scale=scale),
-        out_shape=jax.ShapeDtypeStruct((stripe_len, tok_rows, head_dim), jnp.bfloat16),
-        in_specs=[pl.BlockSpec(memory_space=pltpu.SMEM), vmem],
-        out_specs=vmem,
-        scratch_shapes=[pltpu.VMEM((2 * tok_rows, stripe_len * tok_rows), jnp.float32)],
-        name="attend",
-    )(band, arrived)
+def run_slots(outgoing, bands, scale):
+    stripe_len, _, tok_rows, head_dim = outgoing[0].shape
+    result = None
+    for index, values in enumerate(outgoing):
+        arrived = exchange(values)
+        result = pl.pallas_call(
+            functools.partial(attend_kernel, scale=scale),
+            out_shape=jax.ShapeDtypeStruct(
+                (stripe_len, len(outgoing), tok_rows, head_dim), jnp.bfloat16
+            ),
+            grid=(1,),
+            in_specs=[
+                pl.BlockSpec(memory_space=pltpu.SMEM),
+                pl.BlockSpec(memory_space=pl.ANY),
+            ]
+            + ([] if result is None else [pl.BlockSpec(memory_space=pl.ANY)]),
+            out_specs=pl.BlockSpec(
+                (stripe_len, 1, tok_rows, head_dim),
+                lambda step, index=index: (0, index, 0, 0),
+            ),
+            scratch_shapes=[
+                pltpu.VMEM((2 * tok_rows, stripe_len * tok_rows), jnp.float32),
+                pltpu.VMEM(values.shape, jnp.bfloat16),
+                pltpu.SemaphoreType.DMA,
+            ],
+            input_output_aliases={} if result is None else {2: 0},
+            compiler_params=ROOM,
+            name="attend",
+        )(bands[index : index + 1], arrived, *([] if result is None else [result]))
     return exchange(result)
 
 
@@ -480,14 +515,17 @@
     packed = pack(
         jnp.concatenate([order[:wide_slots], order[last_slots:]]), sources, shapes, head_dim
     )
-    returned = [
-        run_slot(packed[index], bands[index : index + 1], scale)
-        for index in range(whole_run)
-    ]
+    returned = run_slots(packed[:whole_run], bands[:whole_run], scale)
     own = [packed[whole_run]]
     for turn in range(1, SEATS):
         own.append(swap(packed[whole_run + turn], turn))
-    pairs = jnp.stack([part[:, 1:] for part in own])
+    pairs = pl.pallas_call(
+        pairs_kernel,
+        out_shape=block_array(SEATS, narrow_run, 2),
+        in_specs=[vmem] * SEATS,
+        out_specs=vmem,
+        name="pairs",
+    )(*own)
     upward = [
         (source, source + SEATS)
         for source in range(devices - SEATS)
@@ -506,6 +544,7 @@
             for count in (1, 3, 3)
         ],
         name="narrow",
+        compiler_params=ROOM,
     )(jnp.concatenate([places, bands[whole_run + 1 :]]), *own, low, high)
     nears = [near_out[0]]
     for turn in range(1, SEATS):
@@ -514,29 +553,29 @@
         cross_query, context, key_weight, value_weight, head_dim, scale, text
     )
 
-    def unpack(order, parts):
-        return pl.pallas_call(
-            functools.partial(unpack_kernel, head_dim=head_dim),
-            out_shape=jax.ShapeDtypeStruct((tok_rows, width), jnp.bfloat16),
-            in_specs=[smem] + [vmem] * len(parts),
-            out_specs=vmem,
-            name="unpack",
-        )(order, *parts)
-
-    wide_order, rest_order = order[:wide_slots], order[wide_slots:last_slots]
-    near_order = order[last_slots:]
-
-    def short(operands):
-        parts, nears, _ = operands
-        return unpack(jnp.concatenate([wide_order, near_order]), [*parts, *nears])
-
-    def full(operands):
-        parts, _, sources = operands
-        (outgoing,) = pack(rest_order, sources, [block_array(SB, 3)], head_dim)
-        last = run_slot(outgoing, bands[whole_run : whole_run + 1], scale)
-        return unpack(jnp.concatenate([wide_order, rest_order]), [*parts, last])
-
-    self_out = lax.cond(close, short, full, (returned, nears, sources))
+    def full(sources):
+        (outgoing,) = pack(
+            order[wide_slots:last_slots], sources, [block_array(SB, 3)], head_dim
+        )
+        return run_slots([outgoing], bands[whole_run : whole_run + 1], scale)
+
+    def short(sources):
+        return jnp.zeros((SB, 1, tok_rows, head_dim), jnp.bfloat16)
+
+    last = lax.cond(close, short, full, sources)
+    slot_ids = jnp.arange(order.shape[0], dtype=jnp.int32)
+    from_last = (slot_ids >= wide_slots) & (slot_ids < last_slots)
+    unused = jnp.where(close, from_last, slot_ids >= last_slots)
+    parts = [returned, last] + [part[:, None] for part in nears]
+    self_out = pl.pallas_call(
+        functools.partial(unpack_kernel, head_dim=head_dim),
+        out_shape=jax.ShapeDtypeStruct((tok_rows, width), jnp.bfloat16),
+        in_specs=[smem] + [vmem] * len(parts),
+        out_specs=pl.BlockSpec(memory_space=pl.ANY),
+        scratch_shapes=[pltpu.SemaphoreType.DMA],
+        name="unpack",
+        compiler_params=ROOM,
+    )(jnp.where(unused, -1, order), *parts)
     return (self_out, cross_out)
 
 

time: 207 us -> 229 us (1.11)
  waiting for transfers between devices: 61.3 us -> 90.5 us
  Pallas kernels: 53.2 us -> 48.1 us
    ppermute x11, waiting for transfers between devices: 50 us -> 79.4 us  [swap(): lax.ppermute(values, 'seq', [(source, source ^ distance) for source in ra...]
    all_to_all x3 -> x2, starting transfers between devices: 16.3 us -> 11 us  [exchange(): lax.all_to_all(values, 'seq', split_axis=0, concat_axis=0, tiled=True, ax...]
    ppermute x11, starting transfers between devices: 11.9 us -> 15.4 us  [swap(): lax.ppermute(values, 'seq', [(source, source ^ distance) for source in ra...]
    unnamed x30 -> x34, local copies, waits for them, and re-layouts: 3.59 us -> 5.26 us
    pallas_call x3 -> x4, Pallas kernels: 23.3 us -> 22.9 us  [the longest x2 19.2 us: run_slots(): pl.pallas_call(functools.partial(attend_kernel, scale=scale), out_shape=j...]
  transfers between devices with their start and end apart: 16 -> 15, of which waited for: 4 -> 6; matrix products, arithmetic and copies ran while one was open for 3% -> 1% of each run, Pallas kernels for 23% -> 18%
where the time goes in v3:
time: 229 us; the launch traced here: 226 us
  waiting for transfers between devices  90.5 us (40%)
  Pallas kernels  48.1 us (21%)
  blocking collectives  42.6 us (19%)
  starting transfers between devices  31.6 us (14%)
  local copies, waits for them, and re-layouts  6.16 us (3%)
  other arithmetic  5.68 us (2%)
    ppermute x11, waiting for transfers between devices, swap(): lax.ppermute(values, 'seq', [(source, source ^ distance) for source in ra...  79.4 us
    all_to_all x1, blocking collectives, exchange(): lax.all_to_all(values, 'seq', split_axis=0, concat_axis=0, tiled=True, ax...  42.6 us
    pallas_call x2, Pallas kernels, run_slots(): pl.pallas_call(functools.partial(attend_kernel, scale=scale), out_shape=j...  19.2 us
    ppermute x11, starting transfers between devices, swap(): lax.ppermute(values, 'seq', [(source, source ^ distance) for source in ra...  15.4 us
    all_to_all x2, starting transfers between devices, exchange(): lax.all_to_all(values, 'seq', split_axis=0, concat_axis=0, tiled=True, ax...  11 us
    ppermute x1, waiting for transfers between devices, layer(): low = lax.ppermute(pairs, 'seq', upward)  8.29 us
    pallas_call x1, Pallas kernels, cross_attention(): pl.pallas_call(functools.partial(cross_pairs_kernel, head_dim=head_dim, s...  6.8 us
    pallas_call x1, Pallas kernels, pack(): pl.pallas_call(functools.partial(pack_kernel, head_dim=head_dim), out_sha...  5.44 us
  transfers between devices with their start and end apart: 15, of which 6 were waited for; matrix products, arithmetic and copies ran while one was open for 1% of the time, Pallas kernels for 18%

profile of v3, /device:TPU:13, one launch (start us, length us, event | category | flops | bytes accessed | tf_op | source)
XLA Modules:
  0.0 226.3 jit_solution(4041497403056221336)
XLA Ops:
  1.6 1.3 broadcast_add_fusion.1
  4.7 5.4 %pack.3 = (bf16[16,3,128,128]{3,2,1,0:T(8,128)(2,1)}, bf16[16,3,128,128]{3,2,1,0:T(8,128)(2,1)}, bf16[2,3,128,128]{3,2,1,0:T(8,128)(2,1)}, bf16[2,3,128,128]{3,2...) custom-call(s32[40]{0:T(128)} %pad_add_fusion.2.order_ref, ...), custom_call_target="tpu_custom_call" | custom-call | tf_op jit(solution)/shard_map/pack/pallas_call | solution.py:427
  11.1 42.6 %all_to_all.24.source_ref = bf16[16,3,128,128]{3,2,1,0:T(8,128)(2,1)S(1)} all-to-all(bf16[16,3,128,128]{3,2,1,0:T(8,128)(2,1)} %get-tuple-element.33), channel_id=1, replica_groups={{0,1,2,3,4,5,6,7,8,9,10,11,12,13,14,15},{16,17,18,19,20,21,22,23,24,25,..., dimensions={0} | all-to-all | bytes 3145728 | tf_op jit(solution)/shard_map/all_to_all | solution.py:415
  53.6 4.9 %all-to-all-start.2 = ((bf16[16,3,128,128]{3,2,1,0:T(8,128)(2,1)}), bf16[16,3,128,128]{3,2,1,0:T(8,128)(2,1)S(1)}, u32[]{:S(2)}, u32[]{:S(2)}) async-start(bf16[16,3,128,128]{3,2,1,0:T(8,128)(2,1)} %get-tuple-element.32), calls=%async_computation.2 | async-start | bytes 3145728 | tf_op jit(solution)/shard_map/all_to_all | solution.py:415
  58.6 5.0 %project.1 = bf16[1,256,640]{2,1,0:T(8,128)(2,1)} custom-call(bf16[256,4096]{1,0:T(8,128)(2,1)} %context_ref.1, bf16[320,4096]{1,0:T(8,128)(2,1)} %bitcast.17, bf16[320,4096]{1,0:T(8,128)(2,1)} %bitcast.18), custom_call_target="tpu_custom_call" | custom-call | tf_op jit(solution)/shard_map/project/pallas_call | solution.py:238
  63.5 2.1 collective-permute-start.9
  65.6 41.0 %collective-permute-done.9 = bf16[1,256,640]{2,1,0:T(8,128)(2,1)S(1)} collective-permute-done((bf16[1,256,640]{2,1,0:T(8,128)(2,1)}, bf16[1,256,640]{2,1,0:T(8,128)(2,1)S(1)}, u32[]{:S(2)}, u32[]{:S(2)}) %collective-permute-start.9) | collective-permute-done | bytes 327712 | tf_op jit(solution)/shard_map/ppermute | solution.py:345
  107.7 3.2 %collective-permute-start.10 = (bf16[2,256,640]{2,1,0:T(8,128)(2,1)S(1)}, bf16[2,256,640]{2,1,0:T(8,128)(2,1)S(1)}, u32[]{:S(2)}, u32[]{:S(2)}) collective-permute-start(bf16[2,256,640]{2,1,0:T(8,128)(2,1)S(1)} %pad_maximum_fusion.1), channel_id=1, source_target_pairs={{0,4},{1,5},{2,6},{3,7},{4,0},{5,1},{6,2},{7,3},{8,12},{9,13},{10,... | collective-permute-start | bytes 1966088 | tf_op jit(solution)/shard_map/ppermute | solution.py:345
  110.8 14.1 %collective-permute-done.10 = bf16[2,256,640]{2,1,0:T(8,128)(2,1)S(1)} collective-permute-done((bf16[2,256,640]{2,1,0:T(8,128)(2,1)S(1)}, bf16[2,256,640]{2,1,0:T(8,128)(2,1)S(1)}, u32[]{:S(2)}, u32[]{:S(2)}) %collective-permute-start.10) | collective-permute-done | bytes 655392 | tf_op jit(solution)/shard_map/ppermute | solution.py:345
  126.2 1.5 collective-permute-start.11
  128.4 10.4 %attend.4.refs_0_ = bf16[16,2,128,128]{3,2,1,0:T(8,128)(2,1)} custom-call(s32[1]{0:T(128)} %get-tuple-element.44.band_ref, bf16[16,3,128,128]{3,2,1,0:T(8,128)(2,1)S(1)} %all_to_all.24.source_ref), custom_call_target="tpu_custom_call" | custom-call | tf_op jit(solution)/shard_map/attend/pallas_call | solution.py:441
  138.8 8.8 %attend.5 = bf16[16,2,128,128]{3,2,1,0:T(8,128)(2,1)} custom-call(s32[1]{0:T(128)} %get-tuple-element.45.band_ref, bf16[16,3,128,128]{3,2,1,0:T(8,128)(2,1)S(1)} %all-to-all-done.2.source_ref, bf16[16,2,128,128]{3,2,1,0:T(8,128)(2,1)} %attend.4.refs_0_), custom_call_target="tpu_custom_call", output_to_operand_aliasing={{}: (2, {})} | custom-call | tf_op jit(solution)/shard_map/attend/pallas_call | solution.py:441
  147.6 6.0 %all-to-all-start.4 = ((bf16[16,2,128,128]{3,2,1,0:T(8,128)(2,1)}), bf16[16,2,128,128]{3,2,1,0:T(8,128)(2,1)S(1)}, u32[]{:S(2)}, u32[]{:S(2)}) async-start(bf16[16,2,128,128]{3,2,1,0:T(8,128)(2,1)} %attend.5), calls=%async_computation.4 | async-start | bytes 2097152 | tf_op jit(solution)/shard_map/all_to_all | solution.py:415
  157.0 23.0 %collective-permute-done.8.guest_ref = bf16[4,128,640]{2,1,0:T(8,128)(2,1)S(1)} collective-permute-done((bf16[4,128,640]{2,1,0:T(8,128)(2,1)S(1)}, bf16[4,128,640]{2,1,0:T(8,128)(2,1)S(1)}, u32[]{:S(2)}, u32[]{:S(2)}) %collective-permute-start.8) | collective-permute-done | bytes 655392 | tf_op jit(solution)/shard_map/ppermute | solution.py:345
  180.0 6.8 %cross.1 = (bf16[4,128,640]{2,1,0:T(8,128)(2,1)S(1)}, bf16[4,128,640]{2,1,0:T(8,128)(2,1)}) custom-call(s32[3]{0:T(128)S(1)} %pad_add_fusion.4.place_ref, bf16[128,5120]{1,0:T(8,128)(2,1)S(1)} %copy-done, bf16[4,128,640]{2,1,0:T(8,128)(2,1)S(1)} %collective-permute-done.8.guest_ref, bf16[4,256,640]{2,1,0:T(8,128)(2,1)} %pad_maximum_fusion.mine_ref, ...), custom_call_target="tpu_custom_call" | custom-call | tf_op jit(solution)/shard_map/cross/pallas_call | solution.py:393
  189.7 2.1 pairs.1
  191.8 3.1 %collective-permute-start.3 = (bf16[4,2,2,128,128]{4,3,2,1,0:T(8,128)(2,1)}, bf16[4,2,2,128,128]{4,3,2,1,0:T(8,128)(2,1)S(1)}, u32[]{:S(2)}, u32[]{:S(2)}) collective-permute-start(bf16[4,2,2,128,128]{4,3,2,1,0:T(8,128)(2,1)} %pairs.1), channel_id=1, source_target_pairs={{0,4},{1,5},{2,6},{3,7},{4,8},{5,9},{6,10},{7,11},{8,12},{9,13},{1... | collective-permute-start | bytes 1572872 | tf_op jit(solution)/shard_map/ppermute | solution.py:534
  194.9 2.2 collective-permute-start.4
  197.3 8.3 %collective-permute-done.3.refs_4_ = bf16[4,2,2,128,128]{4,3,2,1,0:T(8,128)(2,1)S(1)} collective-permute-done((bf16[4,2,2,128,128]{4,3,2,1,0:T(8,128)(2,1)}, bf16[4,2,2,128,128]{4,3,2,1,0:T(8,128)(2,1)S(1)}, u32[]{:S(2)}, u32[]{:S(2)}) %collective-permute-start.3) | collective-permute-done | bytes 524320 | tf_op jit(solution)/shard_map/ppermute | solution.py:534
  205.6 2.8 %collective-permute-done.4.refs_5_ = bf16[4,2,2,128,128]{4,3,2,1,0:T(8,128)(2,1)S(1)} collective-permute-done((bf16[4,2,2,128,128]{4,3,2,1,0:T(8,128)(2,1)}, bf16[4,2,2,128,128]{4,3,2,1,0:T(8,128)(2,1)S(1)}, u32[]{:S(2)}, u32[]{:S(2)}) %collective-permute-start.4) | collective-permute-done | bytes 524320 | tf_op jit(solution)/shard_map/ppermute | solution.py:535
  211.2 5.0 %narrow.1 = (bf16[2,128,128]{2,1,0:T(8,128)(2,1)S(1)}, bf16[2,128,128]{2,1,0:T(8,128)(2,1)S(1)}, bf16[2,128,128]{2,1,0:T(8,128)(2,1)S(1)}, bf16[2,128,128]{2,1,0:T(8,128)(2,1)S(1)}) custom-call(s32[4]{0:T(128)S(1)} %pad_add_fusion.3.place_ref, bf16[2,3,128,128]{3,2,1,0:T(8,128)(2,1)S(1)} %copy-done.1, bf16[2,3,128,128]{3,2,1,0:T(8,128)(2,1)S(1)} %copy-done.3, ...), custom_call_target="tpu_custom_call" | custom-call | tf_op jit(solution)/shard_map/narrow/pallas_call | solution.py:537
  216.2 3.0 %collective-permute-start.5 = (bf16[2,128,128]{2,1,0:T(8,128)(2,1)S(1)}, bf16[2,128,128]{2,1,0:T(8,128)(2,1)S(1)}, u32[]{:S(2)}, u32[]{:S(2)}) collective-permute-start(bf16[2,128,128]{2,1,0:T(8,128)(2,1)S(1)} %get-tuple-element.39), channel_id=1, source_target_pairs={{0,1},{1,0},{2,3},{3,2},{4,5},{5,4},{6,7},{7,6},{8,9},{9,8},{10,11... | collective-permute-start | bytes 196616 | tf_op jit(solution)/shard_map/ppermute | solution.py:345
  221.0 2.3 %merge.1 = bf16[128,5120]{1,0:T(8,128)(2,1)} custom-call(s32[3]{0:T(128)S(1)} %pad_add_fusion.4.place_ref, bf16[4,128,640]{2,1,0:T(8,128)(2,1)S(1)} %copy-done.9, bf16[4,128,640]{2,1,0:T(8,128)(2,1)} %collective-permute-done.12.came_ref), custom_call_target="tpu_custom_call" | custom-call | tf_op jit(solution)/shard_map/merge/pallas_call | solution.py:403
  224.5 1.6 unpack.1
  (73 shorter events, 18.1 us)
Async XLA Ops:
  4.7 5.5 %copy-start.10 = (bf16[128,5120]{1,0:T(8,128)(2,1)S(1)}, bf16[128,5120]{1,0:T(8,128)(2,1)}, u32[]{:S(2)}) copy-start(bf16[128,5120]{1,0:T(8,128)(2,1)} %query_ref.3) | copy-start | bytes 3932164
  4.7 5.5 %copy-start.11 = (bf16[128,5120]{1,0:T(8,128)(2,1)S(1)}, bf16[128,5120]{1,0:T(8,128)(2,1)}, u32[]{:S(2)}) copy-start(bf16[128,5120]{1,0:T(8,128)(2,1)} %key_ref.1) | copy-start | bytes 3932164
  53.6 85.2 %all-to-all-start.2 = ((bf16[16,3,128,128]{3,2,1,0:T(8,128)(2,1)}), bf16[16,3,128,128]{3,2,1,0:T(8,128)(2,1)S(1)}, u32[]{:S(2)}, u32[]{:S(2)}) async-start(bf16[16,3,128,128]{3,2,1,0:T(8,128)(2,1)} %get-tuple-element.32), calls=%async_computation.2 | async-start | bytes 3145728 | tf_op jit(solution)/shard_map/all_to_all | solution.py:415
  63.5 61.4 %copy-start.12 = (bf16[1,256,640]{2,1,0:T(8,128)(2,1)S(1)}, bf16[1,256,640]{2,1,0:T(8,128)(2,1)}, u32[]{:S(2)}) copy-start(bf16[1,256,640]{2,1,0:T(8,128)(2,1)} %project.1) | copy-start | bytes 983044
  63.5 43.1 %collective-permute-start.9 = (bf16[1,256,640]{2,1,0:T(8,128)(2,1)}, bf16[1,256,640]{2,1,0:T(8,128)(2,1)S(1)}, u32[]{:S(2)}, u32[]{:S(2)}) collective-permute-start(bf16[1,256,640]{2,1,0:T(8,128)(2,1)} %project.1), channel_id=1, source_target_pairs={{0,8},{1,9},{2,10},{3,11},{4,12},{5,13},{6,14},{7,15},{8,0},{9,1},... | collective-permute-start | bytes 983048 | tf_op jit(solution)/shard_map/ppermute | solution.py:345
  107.7 17.3 %collective-permute-start.10 = (bf16[2,256,640]{2,1,0:T(8,128)(2,1)S(1)}, bf16[2,256,640]{2,1,0:T(8,128)(2,1)S(1)}, u32[]{:S(2)}, u32[]{:S(2)}) collective-permute-start(bf16[2,256,640]{2,1,0:T(8,128)(2,1)S(1)} %pad_maximum_fusion.1), channel_id=1, source_target_pairs={{0,4},{1,5},{2,6},{3,7},{4,0},{5,1},{6,2},{7,3},{8,12},{9,13},{10,... | collective-permute-start | bytes 1966088 | tf_op jit(solution)/shard_map/ppermute | solution.py:345
  126.2 53.9 %collective-permute-start.11 = (bf16[4,256,640]{2,1,0:T(8,128)(2,1)}, bf16[4,256,640]{2,1,0:T(8,128)(2,1)}, u32[]{:S(2)}, u32[]{:S(2)}) collective-permute-start(bf16[4,256,640]{2,1,0:T(8,128)(2,1)} %pad_maximum_fusion.mine_ref), channel_id=1, source_target_pairs={{0,1},{1,0},{2,3},{3,2},{4,5},{5,4},{6,7},{7,6},{8,9},{9,8},{10,11... | collective-permute-start | bytes 3932168 | tf_op jit(solution)/shard_map/ppermute | solution.py:345
  147.6 6.2 %copy-start = (bf16[128,5120]{1,0:T(8,128)(2,1)S(1)}, bf16[128,5120]{1,0:T(8,128)(2,1)}, u32[]{:S(2)}) copy-start(bf16[128,5120]{1,0:T(8,128)(2,1)} %query_ref.5) | copy-start | bytes 3932164
  147.6 76.9 %all-to-all-start.4 = ((bf16[16,2,128,128]{3,2,1,0:T(8,128)(2,1)}), bf16[16,2,128,128]{3,2,1,0:T(8,128)(2,1)S(1)}, u32[]{:S(2)}, u32[]{:S(2)}) async-start(bf16[16,2,128,128]{3,2,1,0:T(8,128)(2,1)} %attend.5), calls=%async_computation.4 | async-start | bytes 2097152 | tf_op jit(solution)/shard_map/all_to_all | solution.py:415
  153.6 1.8 copy-start.16
  153.6 3.0 %copy-start.15 = (bf16[2,3,128,128]{3,2,1,0:T(8,128)(2,1)S(1)}, bf16[2,3,128,128]{3,2,1,0:T(8,128)(2,1)}, u32[]{:S(2)}) copy-start(bf16[2,3,128,128]{3,2,1,0:T(8,128)(2,1)} %get-tuple-element.37) | copy-start | bytes 589828
  154.4 25.7 %collective-permute-start.8 = (bf16[4,128,640]{2,1,0:T(8,128)(2,1)S(1)}, bf16[4,128,640]{2,1,0:T(8,128)(2,1)S(1)}, u32[]{:S(2)}, u32[]{:S(2)}) collective-permute-start(bf16[4,128,640]{2,1,0:T(8,128)(2,1)S(1)} %split.1), channel_id=1, source_target_pairs={{0,2},{1,3},{2,0},{3,1},{4,6},{5,7},{6,4},{7,5},{8,10},{9,11},{10,... | collective-permute-start | bytes 1966088 | tf_op jit(solution)/shard_map/ppermute | solution.py:345
  154.7 34.1 %collective-permute-start = (bf16[2,3,128,128]{3,2,1,0:T(8,128)(2,1)}, bf16[2,3,128,128]{3,2,1,0:T(8,128)(2,1)S(1)}, u32[]{:S(2)}, u32[]{:S(2)}) collective-permute-start(bf16[2,3,128,128]{3,2,1,0:T(8,128)(2,1)} %get-tuple-element.35), channel_id=1, source_target_pairs={{0,1},{1,0},{2,3},{3,2},{4,5},{5,4},{6,7},{7,6},{8,9},{9,8},{10,11... | collective-permute-start | bytes 589832 | tf_op jit(solution)/shard_map/ppermute | solution.py:345
  155.4 33.5 %collective-permute-start.1 = (bf16[2,3,128,128]{3,2,1,0:T(8,128)(2,1)S(1)}, bf16[2,3,128,128]{3,2,1,0:T(8,128)(2,1)S(1)}, u32[]{:S(2)}, u32[]{:S(2)}) collective-permute-start(bf16[2,3,128,128]{3,2,1,0:T(8,128)(2,1)S(1)} %copy-done.16), channel_id=1, source_target_pairs={{0,2},{1,3},{2,0},{3,1},{4,6},{5,7},{6,4},{7,5},{8,10},{9,11},{10,... | collective-permute-start | bytes 589832 | tf_op jit(solution)/shard_map/ppermute | solution.py:345
  156.6 32.3 %collective-permute-start.2 = (bf16[2,3,128,128]{3,2,1,0:T(8,128)(2,1)S(1)}, bf16[2,3,128,128]{3,2,1,0:T(8,128)(2,1)S(1)}, u32[]{:S(2)}, u32[]{:S(2)}) collective-permute-start(bf16[2,3,128,128]{3,2,1,0:T(8,128)(2,1)S(1)} %copy-done.15), channel_id=1, source_target_pairs={{0,3},{1,2},{2,1},{3,0},{4,7},{5,6},{6,5},{7,4},{8,11},{9,10},{10,... | collective-permute-start | bytes 589832 | tf_op jit(solution)/shard_map/ppermute | solution.py:345
  187.7 20.7 %copy-start.1 = (bf16[2,3,128,128]{3,2,1,0:T(8,128)(2,1)S(1)}, bf16[2,3,128,128]{3,2,1,0:T(8,128)(2,1)}, u32[]{:S(2)}) copy-start(bf16[2,3,128,128]{3,2,1,0:T(8,128)(2,1)} %get-tuple-element.34.refs_0_) | copy-start | bytes 589828
  187.7 33.3 %collective-permute-start.12 = (bf16[4,128,640]{2,1,0:T(8,128)(2,1)}, bf16[4,128,640]{2,1,0:T(8,128)(2,1)}, u32[]{:S(2)}, u32[]{:S(2)}) collective-permute-start(bf16[4,128,640]{2,1,0:T(8,128)(2,1)} %get-tuple-element.43), channel_id=1, source_target_pairs={{0,2},{1,3},{2,0},{3,1},{4,6},{5,7},{6,4},{7,5},{8,10},{9,11},{10,... | collective-permute-start | bytes 1966088 | tf_op jit(solution)/shard_map/ppermute | solution.py:345
  189.7 31.3 %copy-start.9 = (bf16[4,128,640]{2,1,0:T(8,128)(2,1)S(1)}, bf16[4,128,640]{2,1,0:T(8,128)(2,1)}, u32[]{:S(2)}) copy-start(bf16[4,128,640]{2,1,0:T(8,128)(2,1)} %copy-done.8) | copy-start | bytes 1966084
  191.8 13.8 %collective-permute-start.3 = (bf16[4,2,2,128,128]{4,3,2,1,0:T(8,128)(2,1)}, bf16[4,2,2,128,128]{4,3,2,1,0:T(8,128)(2,1)S(1)}, u32[]{:S(2)}, u32[]{:S(2)}) collective-permute-start(bf16[4,2,2,128,128]{4,3,2,1,0:T(8,128)(2,1)} %pairs.1), channel_id=1, source_target_pairs={{0,4},{1,5},{2,6},{3,7},{4,8},{5,9},{6,10},{7,11},{8,12},{9,13},{1... | collective-permute-start | bytes 1572872 | tf_op jit(solution)/shard_map/ppermute | solution.py:534
  194.9 13.5 %collective-permute-start.4 = (bf16[4,2,2,128,128]{4,3,2,1,0:T(8,128)(2,1)}, bf16[4,2,2,128,128]{4,3,2,1,0:T(8,128)(2,1)S(1)}, u32[]{:S(2)}, u32[]{:S(2)}) collective-permute-start(bf16[4,2,2,128,128]{4,3,2,1,0:T(8,128)(2,1)} %pairs.1), channel_id=1, source_target_pairs={{4,0},{5,1},{6,2},{7,3},{8,4},{9,5},{10,6},{11,7},{12,8},{13,9},{1... | collective-permute-start | bytes 1572872 | tf_op jit(solution)/shard_map/ppermute | solution.py:535
  216.2 7.1 %collective-permute-start.5 = (bf16[2,128,128]{2,1,0:T(8,128)(2,1)S(1)}, bf16[2,128,128]{2,1,0:T(8,128)(2,1)S(1)}, u32[]{:S(2)}, u32[]{:S(2)}) collective-permute-start(bf16[2,128,128]{2,1,0:T(8,128)(2,1)S(1)} %get-tuple-element.39), channel_id=1, source_target_pairs={{0,1},{1,0},{2,3},{3,2},{4,5},{5,4},{6,7},{7,6},{8,9},{9,8},{10,11... | collective-permute-start | bytes 196616 | tf_op jit(solution)/shard_map/ppermute | solution.py:345
  219.2 4.1 %collective-permute-start.6 = (bf16[2,128,128]{2,1,0:T(8,128)(2,1)S(1)}, bf16[2,128,128]{2,1,0:T(8,128)(2,1)S(1)}, u32[]{:S(2)}, u32[]{:S(2)}) collective-permute-start(bf16[2,128,128]{2,1,0:T(8,128)(2,1)S(1)} %get-tuple-element.40), channel_id=1, source_target_pairs={{0,2},{1,3},{2,0},{3,1},{4,6},{5,7},{6,4},{7,5},{8,10},{9,11},{10,... | collective-permute-start | bytes 196616 | tf_op jit(solution)/shard_map/ppermute | solution.py:345
  220.2 4.4 %collective-permute-start.7 = (bf16[2,128,128]{2,1,0:T(8,128)(2,1)S(1)}, bf16[2,128,128]{2,1,0:T(8,128)(2,1)S(1)}, u32[]{:S(2)}, u32[]{:S(2)}) collective-permute-start(bf16[2,128,128]{2,1,0:T(8,128)(2,1)S(1)} %get-tuple-element.41), channel_id=1, source_target_pairs={{0,3},{1,2},{2,1},{3,0},{4,7},{5,6},{6,5},{7,4},{8,11},{9,10},{10,... | collective-permute-start | bytes 196616 | tf_op jit(solution)/shard_map/ppermute | solution.py:345
  221.0 3.6 %copy-start.14 = (bf16[16,1,128,128]{3,2,1,0:T(8,128)(2,1)S(1)}, bf16[16,1,128,128]{3,2,1,0:T(8,128)(2,1)}, u32[]{:S(2)}) copy-start(bf16[16,1,128,128]{3,2,1,0:T(8,128)(2,1)} %copy-done.13) | copy-start | bytes 1572868
  (8 other events, 6.6 us)

commit v4 on v3

--- a/solution.py
+++ b/solution.py
@@ -57,74 +57,104 @@
     pltpu.make_async_copy(out_ref, out_ref, done).wait()
 
 
-def attend_tile(tile, width, band, data_ref, out_ref, score_ref, scale):
+def score_step(tile, chunk, width, band, data_ref, score_ref, peak):
     stripe_len, _, rows, head_dim = data_ref.shape
     start = jnp.clip(2 * tile - band, 0, stripe_len - width)
     query = data_ref[pl.ds(2 * tile, 2), 0].reshape(2 * rows, head_dim)
+    keys = data_ref[pl.ds(start + chunk, 2), 1].reshape(2 * rows, head_dim)
+    scores = lax.dot_general(
+        query, keys, (((1,), (1,)), ((), ())), preferred_element_type=jnp.float32
+    )
+    for part in range(2):
+        key_block = start + chunk + part
+        halves = []
+        for half in range(2):
+            outside = jnp.abs(2 * tile + half - key_block) > band
+            bias = jnp.where(outside, -jnp.inf, 0.0).astype(jnp.float32)
+            halves.append(
+                scores[half * rows : (half + 1) * rows, part * rows : (part + 1) * rows] + bias
+            )
+        masked = jnp.concatenate(halves, axis=0)
+        score_ref[:, (chunk + part) * rows : (chunk + part + 1) * rows] = masked
+        peak = masked if peak is None else jnp.maximum(peak, masked)
+    return peak
+
+
+def value_step(tile, chunk, width, band, data_ref, score_ref, peak, totals, scale):
+    stripe_len, _, rows, head_dim = data_ref.shape
+    start = jnp.clip(2 * tile - band, 0, stripe_len - width)
+    weights = jnp.exp2(
+        (score_ref[:, chunk * rows : (chunk + 2) * rows] - peak) * (scale * LOG2_E)
+    )
+    values = data_ref[pl.ds(start + chunk, 2), 2].reshape(2 * rows, head_dim)
+    partial = weights[:, :rows] + weights[:, rows:]
+    product = jnp.dot(weights.astype(jnp.bfloat16), values, preferred_element_type=jnp.float32)
+    if totals is None:
+        return partial, product
+    return totals[0] + partial, totals[1] + product
+
+
+def attend_width(width, band, data_ref, out_ref, score_refs, peak_refs, scale, late):
+    stripe_len, _, rows, head_dim = data_ref.shape
+    tiles = stripe_len // 2
     peak = None
     for chunk in range(0, width, 2):
-        keys = data_ref[pl.ds(start + chunk, 2), 1].reshape(2 * rows, head_dim)
-        scores = lax.dot_general(
-            query, keys, (((1,), (1,)), ((), ())), preferred_element_type=jnp.float32
-        )
-        for part in range(2):
-            key_block = start + chunk + part
-            halves = []
-            for half in range(2):
-                outside = jnp.abs(2 * tile + half - key_block) > band
-                bias = jnp.where(outside, -jnp.inf, 0.0).astype(jnp.float32)
-                halves.append(
-                    scores[half * rows : (half + 1) * rows, part * rows : (part + 1) * rows] + bias
+        peak = score_step(0, chunk, width, band, data_ref, score_refs[0], peak)
+    peak_refs[0][...] = peak
+    late.wait()
+
+    def step(pair, carry):
+        for turn in range(2):
+            tile = 2 * pair + turn
+            following = jnp.minimum(tile + 1, tiles - 1)
+            peak = jnp.max(peak_refs[turn][...], axis=1, keepdims=True)
+            ahead, totals = None, None
+            for chunk in range(0, width, 2):
+                ahead = score_step(
+                    following, chunk, width, band, data_ref, score_refs[1 - turn], ahead
                 )
-            masked = jnp.concatenate(halves, axis=0)
-            score_ref[:, (chunk + part) * rows : (chunk + part + 1) * rows] = masked
-            peak = masked if peak is None else jnp.maximum(peak, masked)
-    peak = jnp.max(peak, axis=1, keepdims=True)
-    total = None
-    running = None
-    for chunk in range(0, width, 2):
-        weights = jnp.exp2(
-            (score_ref[:, chunk * rows : (chunk + 2) * rows] - peak) * (scale * LOG2_E)
-        )
-        values = data_ref[pl.ds(start + chunk, 2), 2].reshape(2 * rows, head_dim)
-        partial = weights[:, :rows] + weights[:, rows:]
-        product = jnp.dot(
-            weights.astype(jnp.bfloat16), values, preferred_element_type=jnp.float32
-        )
-        total = partial if total is None else total + partial
-        running = product if running is None else running + product
-    total = jnp.sum(total, axis=1, keepdims=True)
-    out_ref[pl.ds(2 * tile, 2), 0] = (
-        (running / total).astype(jnp.bfloat16).reshape(2, rows, head_dim)
-    )
+                totals = value_step(
+                    tile, chunk, width, band, data_ref, score_refs[turn], peak, totals, scale
+                )
+            peak_refs[1 - turn][...] = ahead
+            total = jnp.sum(totals[0], axis=1, keepdims=True)
+            out_ref[pl.ds(2 * tile, 2), 0] = (
+                (totals[1] / total).astype(jnp.bfloat16).reshape(2, rows, head_dim)
+            )
+        return carry
+
+    lax.fori_loop(0, tiles // 2, step, 0)
 
 
 def attend_kernel(band_ref, source_ref, *refs, scale):
-    out_ref, score_ref, data_ref, done = refs[-4:]
-    load = pltpu.make_async_copy(source_ref, data_ref, done)
-    load.start()
-    load.wait()
+    out_ref, *buffers, data_ref, done = refs[-7:]
+    early = pltpu.make_async_copy(source_ref.at[:, :2], data_ref.at[:, :2], done.at[0])
+    late = pltpu.make_async_copy(source_ref.at[:, 2:], data_ref.at[:, 2:], done.at[1])
+    early.start()
+    late.start()
+    early.wait()
     stripe_len = data_ref.shape[0]
     band = band_ref[0]
-
-    def step(tile, carry):
-        low = jnp.maximum(2 * tile - band, 0)
-        high = jnp.minimum(2 * tile + 1 + band, stripe_len - 1)
-        quarter = stripe_len // 4
-        level = (high - low) // quarter
-        for index in range(4):
-
-            @pl.when(level == index)
-            def _():
-                attend_tile(
-                    tile, (index + 1) * quarter, band, data_ref, out_ref, score_ref, scale
-                )
-
-        return carry
-
-    @pl.when(band >= 0)
+    quarter = stripe_len // 4
+    level = jnp.minimum(2 * band + 1, stripe_len - 1) // quarter
+    for index in range(4):
+
+        @pl.when((band >= 0) & (level == index))
+        def _():
+            attend_width(
+                (index + 1) * quarter,
+                band,
+                data_ref,
+                out_ref,
+                buffers[:2],
+                buffers[2:],
+                scale,
+                late,
+            )
+
+    @pl.when(band < 0)
     def _():
-        lax.fori_loop(0, stripe_len // 2, step, 0)
+        late.wait()
 
 
 def cross_kernel(query_ref, key_ref, value_ref, out_ref, *, head_dim, scale, group):
@@ -455,14 +485,21 @@
             ),
             scratch_shapes=[
                 pltpu.VMEM((2 * tok_rows, stripe_len * tok_rows), jnp.float32),
+                pltpu.VMEM((2 * tok_rows, stripe_len * tok_rows), jnp.float32),
+                pltpu.VMEM((2 * tok_rows, tok_rows), jnp.float32),
+                pltpu.VMEM((2 * tok_rows, tok_rows), jnp.float32),
                 pltpu.VMEM(values.shape, jnp.bfloat16),
-                pltpu.SemaphoreType.DMA,
+                pltpu.SemaphoreType.DMA((2,)),
             ],
             input_output_aliases={} if result is None else {2: 0},
             compiler_params=ROOM,
             name="attend",
         )(bands[index : index + 1], arrived, *([] if result is None else [result]))
     return exchange(result)
+
+
+def seat_rank(place):
+    return jnp.where(place < SB // 2, 2 * place, 2 * (SB - 1 - place) + 1)
 
 
 def layer(
@@ -499,9 +536,9 @@
     close = jnp.sum((band_width <= REACH).astype(jnp.int32)) >= rest
     slot_ids = jnp.arange(SB * (whole_run + 1), dtype=jnp.int32)
     run, place = slot_ids // SB, slot_ids % SB
-    wanted = run * SB + jnp.where(run % 2 == 0, place, SB - 1 - place)
+    wanted = run * SB + seat_rank(place)
     runs = jnp.arange(whole_run + 1, dtype=jnp.int32)
-    mine = runs * SB + jnp.where(runs % 2 == 0, turn_seat, SB - 1 - turn_seat)
+    mine = runs * SB + seat_rank(turn_seat)
     slot_ids = jnp.arange(SEATS * narrow_run, dtype=jnp.int32)
     run, place = slot_ids % narrow_run, (slot_ids // narrow_run) ^ seat
     near = SB * whole_run + run * SEATS + jnp.where(run % 2 == 0, place, SEATS - 1 - place)

time: 229 us -> 226 us (0.987)
  Pallas kernels: 48.1 us -> 43.3 us
    pallas_call x2, Pallas kernels: 19.2 us -> 14.6 us  [run_slots(): pl.pallas_call(functools.partial(attend_kernel, scale=scale), out_shape=j...]
  transfers between devices with their start and end apart: 15 -> 15, of which waited for: 6 -> 6; matrix products, arithmetic and copies ran while one was open for 1% -> 1% of each run, Pallas kernels for 18% -> 16%
where the time goes in v4:
time: 226 us; the launch traced here: 224 us
  waiting for transfers between devices  90.5 us (40%)
  Pallas kernels  43.3 us (19%)
  blocking collectives  42.6 us (19%)
  starting transfers between devices  33.8 us (15%)
  local copies, waits for them, and re-layouts  6.13 us (3%)
  other arithmetic  5.68 us (3%)
    ppermute x11, waiting for transfers between devices, swap(): lax.ppermute(values, 'seq', [(source, source ^ distance) for source in ra...  79.4 us
    all_to_all x1, blocking collectives, exchange(): lax.all_to_all(values, 'seq', split_axis=0, concat_axis=0, tiled=True, ax...  42.6 us
    ppermute x11, starting transfers between devices, swap(): lax.ppermute(values, 'seq', [(source, source ^ distance) for source in ra...  15.4 us
    pallas_call x2, Pallas kernels, run_slots(): pl.pallas_call(functools.partial(attend_kernel, scale=scale), out_shape=j...  14.6 us
    all_to_all x2, starting transfers between devices, exchange(): lax.all_to_all(values, 'seq', split_axis=0, concat_axis=0, tiled=True, ax...  13.1 us
    ppermute x1, waiting for transfers between devices, layer(): low = lax.ppermute(pairs, 'seq', upward)  8.29 us
    pallas_call x1, Pallas kernels, cross_attention(): pl.pallas_call(functools.partial(cross_pairs_kernel, head_dim=head_dim, s...  6.62 us
    pallas_call x1, Pallas kernels, pack(): pl.pallas_call(functools.partial(pack_kernel, head_dim=head_dim), out_sha...  5.44 us
  transfers between devices with their start and end apart: 15, of which 6 were waited for; matrix products, arithmetic and copies ran while one was open for 1% of the time, Pallas kernels for 16%

profile of v4, /device:TPU:13, one launch (start us, length us, event | category | flops | bytes accessed | tf_op | source)
XLA Modules:
  0.0 223.7 jit_solution(6325163734187739896)
XLA Ops:
  1.6 1.3 broadcast_add_fusion.1
  4.7 5.4 %pack.3 = (bf16[16,3,128,128]{3,2,1,0:T(8,128)(2,1)}, bf16[16,3,128,128]{3,2,1,0:T(8,128)(2,1)}, bf16[2,3,128,128]{3,2,1,0:T(8,128)(2,1)}, bf16[2,3,128,128]{3,2...) custom-call(s32[40]{0:T(128)} %pad_add_fusion.2.order_ref, ...), custom_call_target="tpu_custom_call" | custom-call | tf_op jit(solution)/shard_map/pack/pallas_call | solution.py:457
  11.1 42.6 %all_to_all.24.source_ref = bf16[16,3,128,128]{3,2,1,0:T(8,128)(2,1)S(1)} all-to-all(bf16[16,3,128,128]{3,2,1,0:T(8,128)(2,1)} %get-tuple-element.33), channel_id=1, replica_groups={{0,1,2,3,4,5,6,7,8,9,10,11,12,13,14,15},{16,17,18,19,20,21,22,23,24,25,..., dimensions={0} | all-to-all | bytes 3145728 | tf_op jit(solution)/shard_map/all_to_all | solution.py:445
  53.6 4.9 %all-to-all-start.2 = ((bf16[16,3,128,128]{3,2,1,0:T(8,128)(2,1)}), bf16[16,3,128,128]{3,2,1,0:T(8,128)(2,1)S(1)}, u32[]{:S(2)}, u32[]{:S(2)}) async-start(bf16[16,3,128,128]{3,2,1,0:T(8,128)(2,1)} %get-tuple-element.32), calls=%async_computation.2 | async-start | bytes 3145728 | tf_op jit(solution)/shard_map/all_to_all | solution.py:445
  58.6 5.0 %project.1 = bf16[1,256,640]{2,1,0:T(8,128)(2,1)} custom-call(bf16[256,4096]{1,0:T(8,128)(2,1)} %context_ref.1, bf16[320,4096]{1,0:T(8,128)(2,1)} %bitcast.17, bf16[320,4096]{1,0:T(8,128)(2,1)} %bitcast.18), custom_call_target="tpu_custom_call" | custom-call | tf_op jit(solution)/shard_map/project/pallas_call | solution.py:268
  63.5 2.1 collective-permute-start.9
  65.6 41.0 %collective-permute-done.9 = bf16[1,256,640]{2,1,0:T(8,128)(2,1)S(1)} collective-permute-done((bf16[1,256,640]{2,1,0:T(8,128)(2,1)}, bf16[1,256,640]{2,1,0:T(8,128)(2,1)S(1)}, u32[]{:S(2)}, u32[]{:S(2)}) %collective-permute-start.9) | collective-permute-done | bytes 327712 | tf_op jit(solution)/shard_map/ppermute | solution.py:375
  107.6 3.2 %collective-permute-start.10 = (bf16[2,256,640]{2,1,0:T(8,128)(2,1)S(1)}, bf16[2,256,640]{2,1,0:T(8,128)(2,1)S(1)}, u32[]{:S(2)}, u32[]{:S(2)}) collective-permute-start(bf16[2,256,640]{2,1,0:T(8,128)(2,1)S(1)} %pad_maximum_fusion.1), channel_id=1, source_target_pairs={{0,4},{1,5},{2,6},{3,7},{4,0},{5,1},{6,2},{7,3},{8,12},{9,13},{10,... | collective-permute-start | bytes 1966088 | tf_op jit(solution)/shard_map/ppermute | solution.py:375
  110.8 14.1 %collective-permute-done.10 = bf16[2,256,640]{2,1,0:T(8,128)(2,1)S(1)} collective-permute-done((bf16[2,256,640]{2,1,0:T(8,128)(2,1)S(1)}, bf16[2,256,640]{2,1,0:T(8,128)(2,1)S(1)}, u32[]{:S(2)}, u32[]{:S(2)}) %collective-permute-start.10) | collective-permute-done | bytes 655392 | tf_op jit(solution)/shard_map/ppermute | solution.py:375
  126.2 1.5 collective-permute-start.11
  128.4 8.9 %attend.4.refs_0_ = bf16[16,2,128,128]{3,2,1,0:T(8,128)(2,1)} custom-call(s32[1]{0:T(128)} %get-tuple-element.44.band_ref, bf16[16,3,128,128]{3,2,1,0:T(8,128)(2,1)S(1)} %all_to_all.24.source_ref), custom_call_target="tpu_custom_call" | custom-call | tf_op jit(solution)/shard_map/attend/pallas_call | solution.py:471
  137.3 5.7 %attend.5 = bf16[16,2,128,128]{3,2,1,0:T(8,128)(2,1)} custom-call(s32[1]{0:T(128)} %get-tuple-element.45.band_ref, bf16[16,3,128,128]{3,2,1,0:T(8,128)(2,1)S(1)} %all-to-all-done.2.source_ref, bf16[16,2,128,128]{3,2,1,0:T(8,128)(2,1)} %attend.4.refs_0_), custom_call_target="tpu_custom_call", output_to_operand_aliasing={{}: (2, {})} | custom-call | tf_op jit(solution)/shard_map/attend/pallas_call | solution.py:471
  143.0 8.2 %all-to-all-start.4 = ((bf16[16,2,128,128]{3,2,1,0:T(8,128)(2,1)}), bf16[16,2,128,128]{3,2,1,0:T(8,128)(2,1)S(1)}, u32[]{:S(2)}, u32[]{:S(2)}) async-start(bf16[16,2,128,128]{3,2,1,0:T(8,128)(2,1)} %attend.5), calls=%async_computation.4 | async-start | bytes 2097152 | tf_op jit(solution)/shard_map/all_to_all | solution.py:445
  154.6 23.0 %collective-permute-done.8.guest_ref = bf16[4,128,640]{2,1,0:T(8,128)(2,1)S(1)} collective-permute-done((bf16[4,128,640]{2,1,0:T(8,128)(2,1)S(1)}, bf16[4,128,640]{2,1,0:T(8,128)(2,1)S(1)}, u32[]{:S(2)}, u32[]{:S(2)}) %collective-permute-start.8) | collective-permute-done | bytes 655392 | tf_op jit(solution)/shard_map/ppermute | solution.py:375
  177.6 6.6 %cross.1 = (bf16[4,128,640]{2,1,0:T(8,128)(2,1)S(1)}, bf16[4,128,640]{2,1,0:T(8,128)(2,1)}) custom-call(s32[3]{0:T(128)S(1)} %pad_add_fusion.4.place_ref, bf16[128,5120]{1,0:T(8,128)(2,1)S(1)} %copy-done, bf16[4,128,640]{2,1,0:T(8,128)(2,1)S(1)} %collective-permute-done.8.guest_ref, bf16[4,256,640]{2,1,0:T(8,128)(2,1)} %pad_maximum_fusion.mine_ref, ...), custom_call_target="tpu_custom_call" | custom-call | tf_op jit(solution)/shard_map/cross/pallas_call | solution.py:423
  187.1 2.1 pairs.1
  189.2 3.1 %collective-permute-start.3 = (bf16[4,2,2,128,128]{4,3,2,1,0:T(8,128)(2,1)}, bf16[4,2,2,128,128]{4,3,2,1,0:T(8,128)(2,1)S(1)}, u32[]{:S(2)}, u32[]{:S(2)}) collective-permute-start(bf16[4,2,2,128,128]{4,3,2,1,0:T(8,128)(2,1)} %pairs.1), channel_id=1, source_target_pairs={{0,4},{1,5},{2,6},{3,7},{4,8},{5,9},{6,10},{7,11},{8,12},{9,13},{1... | collective-permute-start | bytes 1572872 | tf_op jit(solution)/shard_map/ppermute | solution.py:571
  192.3 2.2 collective-permute-start.4
  194.7 8.3 %collective-permute-done.3.refs_4_ = bf16[4,2,2,128,128]{4,3,2,1,0:T(8,128)(2,1)S(1)} collective-permute-done((bf16[4,2,2,128,128]{4,3,2,1,0:T(8,128)(2,1)}, bf16[4,2,2,128,128]{4,3,2,1,0:T(8,128)(2,1)S(1)}, u32[]{:S(2)}, u32[]{:S(2)}) %collective-permute-start.3) | collective-permute-done | bytes 524320 | tf_op jit(solution)/shard_map/ppermute | solution.py:571
  203.0 2.8 %collective-permute-done.4.refs_5_ = bf16[4,2,2,128,128]{4,3,2,1,0:T(8,128)(2,1)S(1)} collective-permute-done((bf16[4,2,2,128,128]{4,3,2,1,0:T(8,128)(2,1)}, bf16[4,2,2,128,128]{4,3,2,1,0:T(8,128)(2,1)S(1)}, u32[]{:S(2)}, u32[]{:S(2)}) %collective-permute-start.4) | collective-permute-done | bytes 524320 | tf_op jit(solution)/shard_map/ppermute | solution.py:572
  208.6 5.0 %narrow.1 = (bf16[2,128,128]{2,1,0:T(8,128)(2,1)S(1)}, bf16[2,128,128]{2,1,0:T(8,128)(2,1)S(1)}, bf16[2,128,128]{2,1,0:T(8,128)(2,1)S(1)}, bf16[2,128,128]{2,1,0:T(8,128)(2,1)S(1)}) custom-call(s32[4]{0:T(128)S(1)} %pad_add_fusion.3.place_ref, bf16[2,3,128,128]{3,2,1,0:T(8,128)(2,1)S(1)} %copy-done.1, bf16[2,3,128,128]{3,2,1,0:T(8,128)(2,1)S(1)} %copy-done.3, ...), custom_call_target="tpu_custom_call" | custom-call | tf_op jit(solution)/shard_map/narrow/pallas_call | solution.py:574
  213.6 3.0 %collective-permute-start.5 = (bf16[2,128,128]{2,1,0:T(8,128)(2,1)S(1)}, bf16[2,128,128]{2,1,0:T(8,128)(2,1)S(1)}, u32[]{:S(2)}, u32[]{:S(2)}) collective-permute-start(bf16[2,128,128]{2,1,0:T(8,128)(2,1)S(1)} %get-tuple-element.39), channel_id=1, source_target_pairs={{0,1},{1,0},{2,3},{3,2},{4,5},{5,4},{6,7},{7,6},{8,9},{9,8},{10,11... | collective-permute-start | bytes 196616 | tf_op jit(solution)/shard_map/ppermute | solution.py:375
  218.3 2.3 %merge.1 = bf16[128,5120]{1,0:T(8,128)(2,1)} custom-call(s32[3]{0:T(128)S(1)} %pad_add_fusion.4.place_ref, bf16[4,128,640]{2,1,0:T(8,128)(2,1)S(1)} %copy-done.9, bf16[4,128,640]{2,1,0:T(8,128)(2,1)} %collective-permute-done.12.came_ref), custom_call_target="tpu_custom_call" | custom-call | tf_op jit(solution)/shard_map/merge/pallas_call | solution.py:433
  221.9 1.6 unpack.1
  (73 shorter events, 18.0 us)
Async XLA Ops:
  4.7 5.5 %copy-start.10 = (bf16[128,5120]{1,0:T(8,128)(2,1)S(1)}, bf16[128,5120]{1,0:T(8,128)(2,1)}, u32[]{:S(2)}) copy-start(bf16[128,5120]{1,0:T(8,128)(2,1)} %query_ref.3) | copy-start | bytes 3932164
  4.7 5.5 %copy-start.11 = (bf16[128,5120]{1,0:T(8,128)(2,1)S(1)}, bf16[128,5120]{1,0:T(8,128)(2,1)}, u32[]{:S(2)}) copy-start(bf16[128,5120]{1,0:T(8,128)(2,1)} %key_ref.1) | copy-start | bytes 3932164
  53.6 83.6 %all-to-all-start.2 = ((bf16[16,3,128,128]{3,2,1,0:T(8,128)(2,1)}), bf16[16,3,128,128]{3,2,1,0:T(8,128)(2,1)S(1)}, u32[]{:S(2)}, u32[]{:S(2)}) async-start(bf16[16,3,128,128]{3,2,1,0:T(8,128)(2,1)} %get-tuple-element.32), calls=%async_computation.2 | async-start | bytes 3145728 | tf_op jit(solution)/shard_map/all_to_all | solution.py:445
  63.5 61.4 %copy-start.12 = (bf16[1,256,640]{2,1,0:T(8,128)(2,1)S(1)}, bf16[1,256,640]{2,1,0:T(8,128)(2,1)}, u32[]{:S(2)}) copy-start(bf16[1,256,640]{2,1,0:T(8,128)(2,1)} %project.1) | copy-start | bytes 983044
  63.5 43.1 %collective-permute-start.9 = (bf16[1,256,640]{2,1,0:T(8,128)(2,1)}, bf16[1,256,640]{2,1,0:T(8,128)(2,1)S(1)}, u32[]{:S(2)}, u32[]{:S(2)}) collective-permute-start(bf16[1,256,640]{2,1,0:T(8,128)(2,1)} %project.1), channel_id=1, source_target_pairs={{0,8},{1,9},{2,10},{3,11},{4,12},{5,13},{6,14},{7,15},{8,0},{9,1},... | collective-permute-start | bytes 983048 | tf_op jit(solution)/shard_map/ppermute | solution.py:375
  107.6 17.3 %collective-permute-start.10 = (bf16[2,256,640]{2,1,0:T(8,128)(2,1)S(1)}, bf16[2,256,640]{2,1,0:T(8,128)(2,1)S(1)}, u32[]{:S(2)}, u32[]{:S(2)}) collective-permute-start(bf16[2,256,640]{2,1,0:T(8,128)(2,1)S(1)} %pad_maximum_fusion.1), channel_id=1, source_target_pairs={{0,4},{1,5},{2,6},{3,7},{4,0},{5,1},{6,2},{7,3},{8,12},{9,13},{10,... | collective-permute-start | bytes 1966088 | tf_op jit(solution)/shard_map/ppermute | solution.py:375
  126.2 51.4 %collective-permute-start.11 = (bf16[4,256,640]{2,1,0:T(8,128)(2,1)}, bf16[4,256,640]{2,1,0:T(8,128)(2,1)}, u32[]{:S(2)}, u32[]{:S(2)}) collective-permute-start(bf16[4,256,640]{2,1,0:T(8,128)(2,1)} %pad_maximum_fusion.mine_ref), channel_id=1, source_target_pairs={{0,1},{1,0},{2,3},{3,2},{4,5},{5,4},{6,7},{7,6},{8,9},{9,8},{10,11... | collective-permute-start | bytes 3932168 | tf_op jit(solution)/shard_map/ppermute | solution.py:375
  143.0 8.3 %copy-start = (bf16[128,5120]{1,0:T(8,128)(2,1)S(1)}, bf16[128,5120]{1,0:T(8,128)(2,1)}, u32[]{:S(2)}) copy-start(bf16[128,5120]{1,0:T(8,128)(2,1)} %query_ref.5) | copy-start | bytes 3932164
  143.0 78.9 %all-to-all-start.4 = ((bf16[16,2,128,128]{3,2,1,0:T(8,128)(2,1)}), bf16[16,2,128,128]{3,2,1,0:T(8,128)(2,1)S(1)}, u32[]{:S(2)}, u32[]{:S(2)}) async-start(bf16[16,2,128,128]{3,2,1,0:T(8,128)(2,1)} %attend.5), calls=%async_computation.4 | async-start | bytes 2097152 | tf_op jit(solution)/shard_map/all_to_all | solution.py:445
  151.2 1.8 copy-start.16
  151.2 3.0 %copy-start.15 = (bf16[2,3,128,128]{3,2,1,0:T(8,128)(2,1)S(1)}, bf16[2,3,128,128]{3,2,1,0:T(8,128)(2,1)}, u32[]{:S(2)}) copy-start(bf16[2,3,128,128]{3,2,1,0:T(8,128)(2,1)} %get-tuple-element.37) | copy-start | bytes 589828
  151.9 25.7 %collective-permute-start.8 = (bf16[4,128,640]{2,1,0:T(8,128)(2,1)S(1)}, bf16[4,128,640]{2,1,0:T(8,128)(2,1)S(1)}, u32[]{:S(2)}, u32[]{:S(2)}) collective-permute-start(bf16[4,128,640]{2,1,0:T(8,128)(2,1)S(1)} %split.1), channel_id=1, source_target_pairs={{0,2},{1,3},{2,0},{3,1},{4,6},{5,7},{6,4},{7,5},{8,10},{9,11},{10,... | collective-permute-start | bytes 1966088 | tf_op jit(solution)/shard_map/ppermute | solution.py:375
  152.3 34.0 %collective-permute-start = (bf16[2,3,128,128]{3,2,1,0:T(8,128)(2,1)}, bf16[2,3,128,128]{3,2,1,0:T(8,128)(2,1)S(1)}, u32[]{:S(2)}, u32[]{:S(2)}) collective-permute-start(bf16[2,3,128,128]{3,2,1,0:T(8,128)(2,1)} %get-tuple-element.35), channel_id=1, source_target_pairs={{0,1},{1,0},{2,3},{3,2},{4,5},{5,4},{6,7},{7,6},{8,9},{9,8},{10,11... | collective-permute-start | bytes 589832 | tf_op jit(solution)/shard_map/ppermute | solution.py:375
  153.0 33.3 %collective-permute-start.1 = (bf16[2,3,128,128]{3,2,1,0:T(8,128)(2,1)S(1)}, bf16[2,3,128,128]{3,2,1,0:T(8,128)(2,1)S(1)}, u32[]{:S(2)}, u32[]{:S(2)}) collective-permute-start(bf16[2,3,128,128]{3,2,1,0:T(8,128)(2,1)S(1)} %copy-done.16), channel_id=1, source_target_pairs={{0,2},{1,3},{2,0},{3,1},{4,6},{5,7},{6,4},{7,5},{8,10},{9,11},{10,... | collective-permute-start | bytes 589832 | tf_op jit(solution)/shard_map/ppermute | solution.py:375
  154.1 32.2 %collective-permute-start.2 = (bf16[2,3,128,128]{3,2,1,0:T(8,128)(2,1)S(1)}, bf16[2,3,128,128]{3,2,1,0:T(8,128)(2,1)S(1)}, u32[]{:S(2)}, u32[]{:S(2)}) collective-permute-start(bf16[2,3,128,128]{3,2,1,0:T(8,128)(2,1)S(1)} %copy-done.15), channel_id=1, source_target_pairs={{0,3},{1,2},{2,1},{3,0},{4,7},{5,6},{6,5},{7,4},{8,11},{9,10},{10,... | collective-permute-start | bytes 589832 | tf_op jit(solution)/shard_map/ppermute | solution.py:375
  185.1 20.7 %copy-start.1 = (bf16[2,3,128,128]{3,2,1,0:T(8,128)(2,1)S(1)}, bf16[2,3,128,128]{3,2,1,0:T(8,128)(2,1)}, u32[]{:S(2)}) copy-start(bf16[2,3,128,128]{3,2,1,0:T(8,128)(2,1)} %get-tuple-element.34.refs_0_) | copy-start | bytes 589828
  185.1 33.3 %collective-permute-start.12 = (bf16[4,128,640]{2,1,0:T(8,128)(2,1)}, bf16[4,128,640]{2,1,0:T(8,128)(2,1)}, u32[]{:S(2)}, u32[]{:S(2)}) collective-permute-start(bf16[4,128,640]{2,1,0:T(8,128)(2,1)} %get-tuple-element.43), channel_id=1, source_target_pairs={{0,2},{1,3},{2,0},{3,1},{4,6},{5,7},{6,4},{7,5},{8,10},{9,11},{10,... | collective-permute-start | bytes 1966088 | tf_op jit(solution)/shard_map/ppermute | solution.py:375
  187.1 31.3 %copy-start.9 = (bf16[4,128,640]{2,1,0:T(8,128)(2,1)S(1)}, bf16[4,128,640]{2,1,0:T(8,128)(2,1)}, u32[]{:S(2)}) copy-start(bf16[4,128,640]{2,1,0:T(8,128)(2,1)} %copy-done.8) | copy-start | bytes 1966084
  189.2 13.8 %collective-permute-start.3 = (bf16[4,2,2,128,128]{4,3,2,1,0:T(8,128)(2,1)}, bf16[4,2,2,128,128]{4,3,2,1,0:T(8,128)(2,1)S(1)}, u32[]{:S(2)}, u32[]{:S(2)}) collective-permute-start(bf16[4,2,2,128,128]{4,3,2,1,0:T(8,128)(2,1)} %pairs.1), channel_id=1, source_target_pairs={{0,4},{1,5},{2,6},{3,7},{4,8},{5,9},{6,10},{7,11},{8,12},{9,13},{1... | collective-permute-start | bytes 1572872 | tf_op jit(solution)/shard_map/ppermute | solution.py:571
  192.3 13.5 %collective-permute-start.4 = (bf16[4,2,2,128,128]{4,3,2,1,0:T(8,128)(2,1)}, bf16[4,2,2,128,128]{4,3,2,1,0:T(8,128)(2,1)S(1)}, u32[]{:S(2)}, u32[]{:S(2)}) collective-permute-start(bf16[4,2,2,128,128]{4,3,2,1,0:T(8,128)(2,1)} %pairs.1), channel_id=1, source_target_pairs={{4,0},{5,1},{6,2},{7,3},{8,4},{9,5},{10,6},{11,7},{12,8},{13,9},{1... | collective-permute-start | bytes 1572872 | tf_op jit(solution)/shard_map/ppermute | solution.py:572
  213.6 7.1 %collective-permute-start.5 = (bf16[2,128,128]{2,1,0:T(8,128)(2,1)S(1)}, bf16[2,128,128]{2,1,0:T(8,128)(2,1)S(1)}, u32[]{:S(2)}, u32[]{:S(2)}) collective-permute-start(bf16[2,128,128]{2,1,0:T(8,128)(2,1)S(1)} %get-tuple-element.39), channel_id=1, source_target_pairs={{0,1},{1,0},{2,3},{3,2},{4,5},{5,4},{6,7},{7,6},{8,9},{9,8},{10,11... | collective-permute-start | bytes 196616 | tf_op jit(solution)/shard_map/ppermute | solution.py:375
  216.6 4.1 %collective-permute-start.6 = (bf16[2,128,128]{2,1,0:T(8,128)(2,1)S(1)}, bf16[2,128,128]{2,1,0:T(8,128)(2,1)S(1)}, u32[]{:S(2)}, u32[]{:S(2)}) collective-permute-start(bf16[2,128,128]{2,1,0:T(8,128)(2,1)S(1)} %get-tuple-element.40), channel_id=1, source_target_pairs={{0,2},{1,3},{2,0},{3,1},{4,6},{5,7},{6,4},{7,5},{8,10},{9,11},{10,... | collective-permute-start | bytes 196616 | tf_op jit(solution)/shard_map/ppermute | solution.py:375
  217.7 4.1 %collective-permute-start.7 = (bf16[2,128,128]{2,1,0:T(8,128)(2,1)S(1)}, bf16[2,128,128]{2,1,0:T(8,128)(2,1)S(1)}, u32[]{:S(2)}, u32[]{:S(2)}) collective-permute-start(bf16[2,128,128]{2,1,0:T(8,128)(2,1)S(1)} %get-tuple-element.41), channel_id=1, source_target_pairs={{0,3},{1,2},{2,1},{3,0},{4,7},{5,6},{6,5},{7,4},{8,11},{9,10},{10,... | collective-permute-start | bytes 196616 | tf_op jit(solution)/shard_map/ppermute | solution.py:375
  218.3 3.5 %copy-start.14 = (bf16[16,1,128,128]{3,2,1,0:T(8,128)(2,1)S(1)}, bf16[16,1,128,128]{3,2,1,0:T(8,128)(2,1)}, u32[]{:S(2)}) copy-start(bf16[16,1,128,128]{3,2,1,0:T(8,128)(2,1)} %copy-done.13) | copy-start | bytes 1572868
  (8 other events, 6.6 us)

commit v5 on v4

--- a/solution.py
+++ b/solution.py
@@ -135,14 +135,14 @@
     early.wait()
     stripe_len = data_ref.shape[0]
     band = band_ref[0]
-    quarter = stripe_len // 4
-    level = jnp.minimum(2 * band + 1, stripe_len - 1) // quarter
-    for index in range(4):
-
-        @pl.when((band >= 0) & (level == index))
+    reach = jnp.minimum(2 * band + 2, stripe_len)
+    widths = (stripe_len // 2, stripe_len * 5 // 8, stripe_len * 3 // 4, stripe_len)
+    for below, width in zip((0,) + widths[:-1], widths):
+
+        @pl.when((band >= 0) & (reach > below) & (reach <= width))
         def _():
             attend_width(
-                (index + 1) * quarter,
+                width,
                 band,
                 data_ref,
                 out_ref,
@@ -492,7 +492,7 @@
                 pltpu.SemaphoreType.DMA((2,)),
             ],
             input_output_aliases={} if result is None else {2: 0},
-            compiler_params=ROOM,
+            compiler_params=pltpu.CompilerParams(vmem_limit_bytes=40 << 20),
             name="attend",
         )(bands[index : index + 1], arrived, *([] if result is None else [result]))
     return exchange(result)

time: 226 us -> 226 us (level)
  no operation moved by 1% of the time
where the time goes in v5:
time: 226 us; the launch traced here: 224 us
  waiting for transfers between devices  90.4 us (40%)
  Pallas kernels  43.6 us (19%)
  blocking collectives  42.6 us (19%)
  starting transfers between devices  33.8 us (15%)
  local copies, waits for them, and re-layouts  6.16 us (3%)
  other arithmetic  5.68 us (3%)
    ppermute x11, waiting for transfers between devices, swap(): lax.ppermute(values, 'seq', [(source, source ^ distance) for source in ra...  79.3 us
    all_to_all x1, blocking collectives, exchange(): lax.all_to_all(values, 'seq', split_axis=0, concat_axis=0, tiled=True, ax...  42.6 us
    ppermute x11, starting transfers between devices, swap(): lax.ppermute(values, 'seq', [(source, source ^ distance) for source in ra...  15.4 us
    pallas_call x2, Pallas kernels, run_slots(): pl.pallas_call(functools.partial(attend_kernel, scale=scale), out_shape=j...  14.6 us
    all_to_all x2, starting transfers between devices, exchange(): lax.all_to_all(values, 'seq', split_axis=0, concat_axis=0, tiled=True, ax...  13.1 us
    ppermute x1, waiting for transfers between devices, layer(): low = lax.ppermute(pairs, 'seq', upward)  8.29 us
    pallas_call x1, Pallas kernels, cross_attention(): pl.pallas_call(functools.partial(cross_pairs_kernel, head_dim=head_dim, s...  6.84 us
    pallas_call x1, Pallas kernels, pack(): pl.pallas_call(functools.partial(pack_kernel, head_dim=head_dim), out_sha...  5.44 us
  transfers between devices with their start and end apart: 15, of which 6 were waited for; matrix products, arithmetic and copies ran while one was open for 1% of the time, Pallas kernels for 16%

profile of v5, /device:TPU:13, one launch (start us, length us, event | category | flops | bytes accessed | tf_op | source)
XLA Modules:
  0.0 223.9 jit_solution(7165084675950892845)
XLA Ops:
  1.6 1.3 broadcast_add_fusion.1
  4.7 5.4 %pack.3 = (bf16[16,3,128,128]{3,2,1,0:T(8,128)(2,1)}, bf16[16,3,128,128]{3,2,1,0:T(8,128)(2,1)}, bf16[2,3,128,128]{3,2,1,0:T(8,128)(2,1)}, bf16[2,3,128,128]{3,2...) custom-call(s32[40]{0:T(128)} %pad_add_fusion.2.order_ref, ...), custom_call_target="tpu_custom_call" | custom-call | tf_op jit(solution)/shard_map/pack/pallas_call | solution.py:457
  11.1 42.6 %all_to_all.24.source_ref = bf16[16,3,128,128]{3,2,1,0:T(8,128)(2,1)S(1)} all-to-all(bf16[16,3,128,128]{3,2,1,0:T(8,128)(2,1)} %get-tuple-element.33), channel_id=1, replica_groups={{0,1,2,3,4,5,6,7,8,9,10,11,12,13,14,15},{16,17,18,19,20,21,22,23,24,25,..., dimensions={0} | all-to-all | bytes 3145728 | tf_op jit(solution)/shard_map/all_to_all | solution.py:445
  53.6 4.9 %all-to-all-start.2 = ((bf16[16,3,128,128]{3,2,1,0:T(8,128)(2,1)}), bf16[16,3,128,128]{3,2,1,0:T(8,128)(2,1)S(1)}, u32[]{:S(2)}, u32[]{:S(2)}) async-start(bf16[16,3,128,128]{3,2,1,0:T(8,128)(2,1)} %get-tuple-element.32), calls=%async_computation.2 | async-start | bytes 3145728 | tf_op jit(solution)/shard_map/all_to_all | solution.py:445
  58.6 5.0 %project.1 = bf16[1,256,640]{2,1,0:T(8,128)(2,1)} custom-call(bf16[256,4096]{1,0:T(8,128)(2,1)} %context_ref.1, bf16[320,4096]{1,0:T(8,128)(2,1)} %bitcast.17, bf16[320,4096]{1,0:T(8,128)(2,1)} %bitcast.18), custom_call_target="tpu_custom_call" | custom-call | tf_op jit(solution)/shard_map/project/pallas_call | solution.py:268
  63.5 2.1 collective-permute-start.9
  65.6 41.0 %collective-permute-done.9 = bf16[1,256,640]{2,1,0:T(8,128)(2,1)S(1)} collective-permute-done((bf16[1,256,640]{2,1,0:T(8,128)(2,1)}, bf16[1,256,640]{2,1,0:T(8,128)(2,1)S(1)}, u32[]{:S(2)}, u32[]{:S(2)}) %collective-permute-start.9) | collective-permute-done | bytes 327712 | tf_op jit(solution)/shard_map/ppermute | solution.py:375
  107.6 3.2 %collective-permute-start.10 = (bf16[2,256,640]{2,1,0:T(8,128)(2,1)S(1)}, bf16[2,256,640]{2,1,0:T(8,128)(2,1)S(1)}, u32[]{:S(2)}, u32[]{:S(2)}) collective-permute-start(bf16[2,256,640]{2,1,0:T(8,128)(2,1)S(1)} %pad_maximum_fusion.1), channel_id=1, source_target_pairs={{0,4},{1,5},{2,6},{3,7},{4,0},{5,1},{6,2},{7,3},{8,12},{9,13},{10,... | collective-permute-start | bytes 1966088 | tf_op jit(solution)/shard_map/ppermute | solution.py:375
  110.8 14.1 %collective-permute-done.10 = bf16[2,256,640]{2,1,0:T(8,128)(2,1)S(1)} collective-permute-done((bf16[2,256,640]{2,1,0:T(8,128)(2,1)S(1)}, bf16[2,256,640]{2,1,0:T(8,128)(2,1)S(1)}, u32[]{:S(2)}, u32[]{:S(2)}) %collective-permute-start.10) | collective-permute-done | bytes 655392 | tf_op jit(solution)/shard_map/ppermute | solution.py:375
  126.2 1.5 collective-permute-start.11
  128.4 8.9 %attend.4.refs_0_ = bf16[16,2,128,128]{3,2,1,0:T(8,128)(2,1)} custom-call(s32[1]{0:T(128)} %get-tuple-element.44.band_ref, bf16[16,3,128,128]{3,2,1,0:T(8,128)(2,1)S(1)} %all_to_all.24.source_ref), custom_call_target="tpu_custom_call" | custom-call | tf_op jit(solution)/shard_map/attend/pallas_call | solution.py:471
  137.3 5.7 %attend.5 = bf16[16,2,128,128]{3,2,1,0:T(8,128)(2,1)} custom-call(s32[1]{0:T(128)} %get-tuple-element.45.band_ref, bf16[16,3,128,128]{3,2,1,0:T(8,128)(2,1)S(1)} %all-to-all-done.2.source_ref, bf16[16,2,128,128]{3,2,1,0:T(8,128)(2,1)} %attend.4.refs_0_), custom_call_target="tpu_custom_call", output_to_operand_aliasing={{}: (2, {})} | custom-call | tf_op jit(solution)/shard_map/attend/pallas_call | solution.py:471
  143.0 8.2 %all-to-all-start.4 = ((bf16[16,2,128,128]{3,2,1,0:T(8,128)(2,1)}), bf16[16,2,128,128]{3,2,1,0:T(8,128)(2,1)S(1)}, u32[]{:S(2)}, u32[]{:S(2)}) async-start(bf16[16,2,128,128]{3,2,1,0:T(8,128)(2,1)} %attend.5), calls=%async_computation.4 | async-start | bytes 2097152 | tf_op jit(solution)/shard_map/all_to_all | solution.py:445
  154.6 23.0 %collective-permute-done.8.guest_ref = bf16[4,128,640]{2,1,0:T(8,128)(2,1)S(1)} collective-permute-done((bf16[4,128,640]{2,1,0:T(8,128)(2,1)S(1)}, bf16[4,128,640]{2,1,0:T(8,128)(2,1)S(1)}, u32[]{:S(2)}, u32[]{:S(2)}) %collective-permute-start.8) | collective-permute-done | bytes 655392 | tf_op jit(solution)/shard_map/ppermute | solution.py:375
  177.6 6.8 %cross.1 = (bf16[4,128,640]{2,1,0:T(8,128)(2,1)S(1)}, bf16[4,128,640]{2,1,0:T(8,128)(2,1)}) custom-call(s32[3]{0:T(128)S(1)} %pad_add_fusion.4.place_ref, bf16[128,5120]{1,0:T(8,128)(2,1)S(1)} %copy-done, bf16[4,128,640]{2,1,0:T(8,128)(2,1)S(1)} %collective-permute-done.8.guest_ref, bf16[4,256,640]{2,1,0:T(8,128)(2,1)} %pad_maximum_fusion.mine_ref, ...), custom_call_target="tpu_custom_call" | custom-call | tf_op jit(solution)/shard_map/cross/pallas_call | solution.py:423
  187.3 2.1 pairs.1
  189.4 3.1 %collective-permute-start.3 = (bf16[4,2,2,128,128]{4,3,2,1,0:T(8,128)(2,1)}, bf16[4,2,2,128,128]{4,3,2,1,0:T(8,128)(2,1)S(1)}, u32[]{:S(2)}, u32[]{:S(2)}) collective-permute-start(bf16[4,2,2,128,128]{4,3,2,1,0:T(8,128)(2,1)} %pairs.1), channel_id=1, source_target_pairs={{0,4},{1,5},{2,6},{3,7},{4,8},{5,9},{6,10},{7,11},{8,12},{9,13},{1... | collective-permute-start | bytes 1572872 | tf_op jit(solution)/shard_map/ppermute | solution.py:571
  192.5 2.2 collective-permute-start.4
  194.9 8.3 %collective-permute-done.3.refs_4_ = bf16[4,2,2,128,128]{4,3,2,1,0:T(8,128)(2,1)S(1)} collective-permute-done((bf16[4,2,2,128,128]{4,3,2,1,0:T(8,128)(2,1)}, bf16[4,2,2,128,128]{4,3,2,1,0:T(8,128)(2,1)S(1)}, u32[]{:S(2)}, u32[]{:S(2)}) %collective-permute-start.3) | collective-permute-done | bytes 524320 | tf_op jit(solution)/shard_map/ppermute | solution.py:571
  203.2 2.8 %collective-permute-done.4.refs_5_ = bf16[4,2,2,128,128]{4,3,2,1,0:T(8,128)(2,1)S(1)} collective-permute-done((bf16[4,2,2,128,128]{4,3,2,1,0:T(8,128)(2,1)}, bf16[4,2,2,128,128]{4,3,2,1,0:T(8,128)(2,1)S(1)}, u32[]{:S(2)}, u32[]{:S(2)}) %collective-permute-start.4) | collective-permute-done | bytes 524320 | tf_op jit(solution)/shard_map/ppermute | solution.py:572
  208.8 5.0 %narrow.1 = (bf16[2,128,128]{2,1,0:T(8,128)(2,1)S(1)}, bf16[2,128,128]{2,1,0:T(8,128)(2,1)S(1)}, bf16[2,128,128]{2,1,0:T(8,128)(2,1)S(1)}, bf16[2,128,128]{2,1,0:T(8,128)(2,1)S(1)}) custom-call(s32[4]{0:T(128)S(1)} %pad_add_fusion.3.place_ref, bf16[2,3,128,128]{3,2,1,0:T(8,128)(2,1)S(1)} %copy-done.1, bf16[2,3,128,128]{3,2,1,0:T(8,128)(2,1)S(1)} %copy-done.3, ...), custom_call_target="tpu_custom_call" | custom-call | tf_op jit(solution)/shard_map/narrow/pallas_call | solution.py:574
  213.8 3.0 %collective-permute-start.5 = (bf16[2,128,128]{2,1,0:T(8,128)(2,1)S(1)}, bf16[2,128,128]{2,1,0:T(8,128)(2,1)S(1)}, u32[]{:S(2)}, u32[]{:S(2)}) collective-permute-start(bf16[2,128,128]{2,1,0:T(8,128)(2,1)S(1)} %get-tuple-element.39), channel_id=1, source_target_pairs={{0,1},{1,0},{2,3},{3,2},{4,5},{5,4},{6,7},{7,6},{8,9},{9,8},{10,11... | collective-permute-start | bytes 196616 | tf_op jit(solution)/shard_map/ppermute | solution.py:375
  218.6 2.3 %merge.1 = bf16[128,5120]{1,0:T(8,128)(2,1)} custom-call(s32[3]{0:T(128)S(1)} %pad_add_fusion.4.place_ref, bf16[4,128,640]{2,1,0:T(8,128)(2,1)S(1)} %copy-done.9, bf16[4,128,640]{2,1,0:T(8,128)(2,1)} %collective-permute-done.12.came_ref), custom_call_target="tpu_custom_call" | custom-call | tf_op jit(solution)/shard_map/merge/pallas_call | solution.py:433
  222.1 1.6 unpack.1
  (73 shorter events, 18.0 us)
Async XLA Ops:
  4.7 5.5 %copy-start.10 = (bf16[128,5120]{1,0:T(8,128)(2,1)S(1)}, bf16[128,5120]{1,0:T(8,128)(2,1)}, u32[]{:S(2)}) copy-start(bf16[128,5120]{1,0:T(8,128)(2,1)} %query_ref.3) | copy-start | bytes 3932164
  4.7 5.5 %copy-start.11 = (bf16[128,5120]{1,0:T(8,128)(2,1)S(1)}, bf16[128,5120]{1,0:T(8,128)(2,1)}, u32[]{:S(2)}) copy-start(bf16[128,5120]{1,0:T(8,128)(2,1)} %key_ref.1) | copy-start | bytes 3932164
  53.6 83.6 %all-to-all-start.2 = ((bf16[16,3,128,128]{3,2,1,0:T(8,128)(2,1)}), bf16[16,3,128,128]{3,2,1,0:T(8,128)(2,1)S(1)}, u32[]{:S(2)}, u32[]{:S(2)}) async-start(bf16[16,3,128,128]{3,2,1,0:T(8,128)(2,1)} %get-tuple-element.32), calls=%async_computation.2 | async-start | bytes 3145728 | tf_op jit(solution)/shard_map/all_to_all | solution.py:445
  63.5 61.4 %copy-start.12 = (bf16[1,256,640]{2,1,0:T(8,128)(2,1)S(1)}, bf16[1,256,640]{2,1,0:T(8,128)(2,1)}, u32[]{:S(2)}) copy-start(bf16[1,256,640]{2,1,0:T(8,128)(2,1)} %project.1) | copy-start | bytes 983044
  63.5 43.1 %collective-permute-start.9 = (bf16[1,256,640]{2,1,0:T(8,128)(2,1)}, bf16[1,256,640]{2,1,0:T(8,128)(2,1)S(1)}, u32[]{:S(2)}, u32[]{:S(2)}) collective-permute-start(bf16[1,256,640]{2,1,0:T(8,128)(2,1)} %project.1), channel_id=1, source_target_pairs={{0,8},{1,9},{2,10},{3,11},{4,12},{5,13},{6,14},{7,15},{8,0},{9,1},... | collective-permute-start | bytes 983048 | tf_op jit(solution)/shard_map/ppermute | solution.py:375
  107.6 17.3 %collective-permute-start.10 = (bf16[2,256,640]{2,1,0:T(8,128)(2,1)S(1)}, bf16[2,256,640]{2,1,0:T(8,128)(2,1)S(1)}, u32[]{:S(2)}, u32[]{:S(2)}) collective-permute-start(bf16[2,256,640]{2,1,0:T(8,128)(2,1)S(1)} %pad_maximum_fusion.1), channel_id=1, source_target_pairs={{0,4},{1,5},{2,6},{3,7},{4,0},{5,1},{6,2},{7,3},{8,12},{9,13},{10,... | collective-permute-start | bytes 1966088 | tf_op jit(solution)/shard_map/ppermute | solution.py:375
  126.2 51.4 %collective-permute-start.11 = (bf16[4,256,640]{2,1,0:T(8,128)(2,1)}, bf16[4,256,640]{2,1,0:T(8,128)(2,1)}, u32[]{:S(2)}, u32[]{:S(2)}) collective-permute-start(bf16[4,256,640]{2,1,0:T(8,128)(2,1)} %pad_maximum_fusion.mine_ref), channel_id=1, source_target_pairs={{0,1},{1,0},{2,3},{3,2},{4,5},{5,4},{6,7},{7,6},{8,9},{9,8},{10,11... | collective-permute-start | bytes 3932168 | tf_op jit(solution)/shard_map/ppermute | solution.py:375
  143.0 8.3 %copy-start = (bf16[128,5120]{1,0:T(8,128)(2,1)S(1)}, bf16[128,5120]{1,0:T(8,128)(2,1)}, u32[]{:S(2)}) copy-start(bf16[128,5120]{1,0:T(8,128)(2,1)} %query_ref.5) | copy-start | bytes 3932164
  143.0 79.1 %all-to-all-start.4 = ((bf16[16,2,128,128]{3,2,1,0:T(8,128)(2,1)}), bf16[16,2,128,128]{3,2,1,0:T(8,128)(2,1)S(1)}, u32[]{:S(2)}, u32[]{:S(2)}) async-start(bf16[16,2,128,128]{3,2,1,0:T(8,128)(2,1)} %attend.5), calls=%async_computation.4 | async-start | bytes 2097152 | tf_op jit(solution)/shard_map/all_to_all | solution.py:445
  151.2 1.8 copy-start.16
  151.2 3.0 %copy-start.15 = (bf16[2,3,128,128]{3,2,1,0:T(8,128)(2,1)S(1)}, bf16[2,3,128,128]{3,2,1,0:T(8,128)(2,1)}, u32[]{:S(2)}) copy-start(bf16[2,3,128,128]{3,2,1,0:T(8,128)(2,1)} %get-tuple-element.37) | copy-start | bytes 589828
  151.9 25.7 %collective-permute-start.8 = (bf16[4,128,640]{2,1,0:T(8,128)(2,1)S(1)}, bf16[4,128,640]{2,1,0:T(8,128)(2,1)S(1)}, u32[]{:S(2)}, u32[]{:S(2)}) collective-permute-start(bf16[4,128,640]{2,1,0:T(8,128)(2,1)S(1)} %split.1), channel_id=1, source_target_pairs={{0,2},{1,3},{2,0},{3,1},{4,6},{5,7},{6,4},{7,5},{8,10},{9,11},{10,... | collective-permute-start | bytes 1966088 | tf_op jit(solution)/shard_map/ppermute | solution.py:375
  152.3 34.2 %collective-permute-start = (bf16[2,3,128,128]{3,2,1,0:T(8,128)(2,1)}, bf16[2,3,128,128]{3,2,1,0:T(8,128)(2,1)S(1)}, u32[]{:S(2)}, u32[]{:S(2)}) collective-permute-start(bf16[2,3,128,128]{3,2,1,0:T(8,128)(2,1)} %get-tuple-element.35), channel_id=1, source_target_pairs={{0,1},{1,0},{2,3},{3,2},{4,5},{5,4},{6,7},{7,6},{8,9},{9,8},{10,11... | collective-permute-start | bytes 589832 | tf_op jit(solution)/shard_map/ppermute | solution.py:375
  152.9 33.5 %collective-permute-start.1 = (bf16[2,3,128,128]{3,2,1,0:T(8,128)(2,1)S(1)}, bf16[2,3,128,128]{3,2,1,0:T(8,128)(2,1)S(1)}, u32[]{:S(2)}, u32[]{:S(2)}) collective-permute-start(bf16[2,3,128,128]{3,2,1,0:T(8,128)(2,1)S(1)} %copy-done.16), channel_id=1, source_target_pairs={{0,2},{1,3},{2,0},{3,1},{4,6},{5,7},{6,4},{7,5},{8,10},{9,11},{10,... | collective-permute-start | bytes 589832 | tf_op jit(solution)/shard_map/ppermute | solution.py:375
  154.1 32.3 %collective-permute-start.2 = (bf16[2,3,128,128]{3,2,1,0:T(8,128)(2,1)S(1)}, bf16[2,3,128,128]{3,2,1,0:T(8,128)(2,1)S(1)}, u32[]{:S(2)}, u32[]{:S(2)}) collective-permute-start(bf16[2,3,128,128]{3,2,1,0:T(8,128)(2,1)S(1)} %copy-done.15), channel_id=1, source_target_pairs={{0,3},{1,2},{2,1},{3,0},{4,7},{5,6},{6,5},{7,4},{8,11},{9,10},{10,... | collective-permute-start | bytes 589832 | tf_op jit(solution)/shard_map/ppermute | solution.py:375
  185.3 20.7 %copy-start.1 = (bf16[2,3,128,128]{3,2,1,0:T(8,128)(2,1)S(1)}, bf16[2,3,128,128]{3,2,1,0:T(8,128)(2,1)}, u32[]{:S(2)}) copy-start(bf16[2,3,128,128]{3,2,1,0:T(8,128)(2,1)} %get-tuple-element.34.refs_0_) | copy-start | bytes 589828
  185.3 33.3 %collective-permute-start.12 = (bf16[4,128,640]{2,1,0:T(8,128)(2,1)}, bf16[4,128,640]{2,1,0:T(8,128)(2,1)}, u32[]{:S(2)}, u32[]{:S(2)}) collective-permute-start(bf16[4,128,640]{2,1,0:T(8,128)(2,1)} %get-tuple-element.43), channel_id=1, source_target_pairs={{0,2},{1,3},{2,0},{3,1},{4,6},{5,7},{6,4},{7,5},{8,10},{9,11},{10,... | collective-permute-start | bytes 1966088 | tf_op jit(solution)/shard_map/ppermute | solution.py:375
  187.3 31.3 %copy-start.9 = (bf16[4,128,640]{2,1,0:T(8,128)(2,1)S(1)}, bf16[4,128,640]{2,1,0:T(8,128)(2,1)}, u32[]{:S(2)}) copy-start(bf16[4,128,640]{2,1,0:T(8,128)(2,1)} %copy-done.8) | copy-start | bytes 1966084
  189.4 13.8 %collective-permute-start.3 = (bf16[4,2,2,128,128]{4,3,2,1,0:T(8,128)(2,1)}, bf16[4,2,2,128,128]{4,3,2,1,0:T(8,128)(2,1)S(1)}, u32[]{:S(2)}, u32[]{:S(2)}) collective-permute-start(bf16[4,2,2,128,128]{4,3,2,1,0:T(8,128)(2,1)} %pairs.1), channel_id=1, source_target_pairs={{0,4},{1,5},{2,6},{3,7},{4,8},{5,9},{6,10},{7,11},{8,12},{9,13},{1... | collective-permute-start | bytes 1572872 | tf_op jit(solution)/shard_map/ppermute | solution.py:571
  192.5 13.5 %collective-permute-start.4 = (bf16[4,2,2,128,128]{4,3,2,1,0:T(8,128)(2,1)}, bf16[4,2,2,128,128]{4,3,2,1,0:T(8,128)(2,1)S(1)}, u32[]{:S(2)}, u32[]{:S(2)}) collective-permute-start(bf16[4,2,2,128,128]{4,3,2,1,0:T(8,128)(2,1)} %pairs.1), channel_id=1, source_target_pairs={{4,0},{5,1},{6,2},{7,3},{8,4},{9,5},{10,6},{11,7},{12,8},{13,9},{1... | collective-permute-start | bytes 1572872 | tf_op jit(solution)/shard_map/ppermute | solution.py:572
  213.8 7.1 %collective-permute-start.5 = (bf16[2,128,128]{2,1,0:T(8,128)(2,1)S(1)}, bf16[2,128,128]{2,1,0:T(8,128)(2,1)S(1)}, u32[]{:S(2)}, u32[]{:S(2)}) collective-permute-start(bf16[2,128,128]{2,1,0:T(8,128)(2,1)S(1)} %get-tuple-element.39), channel_id=1, source_target_pairs={{0,1},{1,0},{2,3},{3,2},{4,5},{5,4},{6,7},{7,6},{8,9},{9,8},{10,11... | collective-permute-start | bytes 196616 | tf_op jit(solution)/shard_map/ppermute | solution.py:375
  216.8 4.1 %collective-permute-start.6 = (bf16[2,128,128]{2,1,0:T(8,128)(2,1)S(1)}, bf16[2,128,128]{2,1,0:T(8,128)(2,1)S(1)}, u32[]{:S(2)}, u32[]{:S(2)}) collective-permute-start(bf16[2,128,128]{2,1,0:T(8,128)(2,1)S(1)} %get-tuple-element.40), channel_id=1, source_target_pairs={{0,2},{1,3},{2,0},{3,1},{4,6},{5,7},{6,4},{7,5},{8,10},{9,11},{10,... | collective-permute-start | bytes 196616 | tf_op jit(solution)/shard_map/ppermute | solution.py:375
  217.7 4.4 %collective-permute-start.7 = (bf16[2,128,128]{2,1,0:T(8,128)(2,1)S(1)}, bf16[2,128,128]{2,1,0:T(8,128)(2,1)S(1)}, u32[]{:S(2)}, u32[]{:S(2)}) collective-permute-start(bf16[2,128,128]{2,1,0:T(8,128)(2,1)S(1)} %get-tuple-element.41), channel_id=1, source_target_pairs={{0,3},{1,2},{2,1},{3,0},{4,7},{5,6},{6,5},{7,4},{8,11},{9,10},{10,... | collective-permute-start | bytes 196616 | tf_op jit(solution)/shard_map/ppermute | solution.py:375
  218.6 3.5 %copy-start.14 = (bf16[16,1,128,128]{3,2,1,0:T(8,128)(2,1)S(1)}, bf16[16,1,128,128]{3,2,1,0:T(8,128)(2,1)}, u32[]{:S(2)}) copy-start(bf16[16,1,128,128]{3,2,1,0:T(8,128)(2,1)} %copy-done.13) | copy-start | bytes 1572868
  (8 other events, 6.6 us)
